TPU v7x, 32 devices: a whole 2x2x4 slice. The times are simulated.
32 devices in a mesh: dp: 8 (over y, x, core), ctx: 4 (over z).
Axes of the slice: x: 2, y: 2, z: 4, core: 2. Of those that a mesh axis runs over, the one named last changes fastest.
Arguments:
- inputs: bfloat16 [8, 1024, 1152], P('dp', 'ctx'), may hold values from -6 to 6
- counts: int32 [8], P('dp'), may hold values from 512 to 1024
- params: float32 [1, 15241216], P(None, ('dp', 'ctx')), as said below
- first_moment: float32 [1, 15241216], P(None, ('dp', 'ctx')), may hold values from -60 to 60
- second_moment: float32 [1, 15241216], P(None, ('dp', 'ctx')), may hold values from 10 to 10000
- out_cotangent: float32 [8, 1024, 1152], P('dp', 'ctx'), may hold values from -6 to 6
Outputs:
- output: bfloat16 [8, 1024, 1152], P('dp', 'ctx')
- input_grad: float32 [8, 1024, 1152], P('dp', 'ctx')
- param_grads: float32 [1, 15241216], P(None, ('dp', 'ctx'))
- new_params: float32 [1, 15241216], P(None, ('dp', 'ctx'))
- new_first: float32 [1, 15241216], P(None, ('dp', 'ctx'))
- new_second: float32 [1, 15241216], P(None, ('dp', 'ctx'))
Inputs may be any that keep to these rules, and one draw needn't show every extreme that they name: `counts`: valid patch tokens of each image; slots from this count up to 1024 are padding. `params`: laid out as the first step says, zeros in each row's tail.
All inputs are finite; a program needn't handle non-finite values.
Results may differ from a plain program's by a relative error of at most 0.014.
The roundings to bfloat16 on the way count: a program that leaves them out, or rounds other values in their place, can miss the bound.
Values may be sent and summed in bfloat16 or wider, within the bound.
No kernel may reach another device: no remote copies, remote signals or barrier semaphores. Data moves between devices by JAX's collectives and lax.ppermute only.
A program may use at most 320 MiB of HBM per device.

v0:
```python
import functools
import math

import jax
import jax.numpy as jnp
from jax import lax
from jax.experimental import pallas as pl
from jax.experimental.pallas import tpu as pltpu
from jax.sharding import PartitionSpec as P

D = 1152
H = 16
HD = 72
FF = 4304
LANES = 128
TILE = 16

norm_epsilon = 1e-06
beta_one = 0.9
beta_two = 0.95
adam_epsilon = 1e-08
adam_step = 3
rate_matrix = 0.005
rate_vector = 0.1
weight_decay = 0.1
masked_score = -1e30

BF = jnp.bfloat16
F32 = jnp.float32

QKV_BLOCKS = 3 * D // LANES
D_BLOCKS = D // LANES
ROW_QKV = 0
ROW_OUT = D * QKV_BLOCKS
ROW_UP = ROW_OUT + D * D_BLOCKS
ROW_DOWN = ROW_UP + D * FF // LANES
ROW_VEC = ROW_DOWN + FF * D_BLOCKS
VEC_ROWS = 128
VEC_LENGTHS = [D] * 8 + [FF]

UP_GROUP = LANES // math.gcd(FF, LANES)
UP_STRIDE = UP_GROUP * FF // LANES
UP_BLOCKS = -(-FF // LANES)
UP_TAIL = FF - (UP_BLOCKS - 1) * LANES
STEPS = 9
BLOCK = D // STEPS
DOWN_BLOCK = -(-FF // (STEPS * TILE)) * TILE
VMEM_LIMIT = 60 * 1024 * 1024


class Layout:
    def __init__(self, dp, ctx, shard_length):
        self.dp, self.ctx = dp, ctx
        self.devices = dp * ctx
        self.columns = dp // 2
        self.half = self.columns // 2
        self.rows = shard_length // LANES
        longest = (self.rows + TILE - 1) // TILE
        self.piece = -(-longest // self.columns) * TILE
        self.total = self.rows * self.devices

    def start(self, shard):
        return shard * self.rows // TILE * TILE

    def pieces(self, shard):
        group, within = divmod(shard, 2 * self.ctx)
        found = []
        for column in range(self.columns):
            device = column * 2 * self.ctx + within
            first = self.start(shard) + column * self.piece
            rows = min(self.piece, self.start(shard + 1) - first)
            source = (device * self.half + group % self.half) * self.piece
            if rows > 0:
                found.append((group // self.half, source, first, rows))
        return found

    def covering(self, low, high):
        return [
            shard
            for shard in range(self.devices)
            if self.start(shard) < high and self.start(shard + 1) > low
        ]


def lane_index(rows):
    return lax.broadcasted_iota(jnp.int32, (rows, LANES), 1)


def rows_to_matrix(flat, base, rows, blocks, wide, out):
    wide[pl.ds(0, rows * blocks), :] = flat[pl.ds(base, rows * blocks), :].astype(F32)
    for block in range(blocks):
        part = wide[pl.ds(block, rows, stride=blocks), :]
        out[:, block * LANES : (block + 1) * LANES] = part.astype(BF)


def matrix_to_rows(matrix, rows, blocks, wide, flat, base):
    for block in range(blocks):
        part = matrix[:, block * LANES : (block + 1) * LANES].astype(F32)
        wide[pl.ds(block, rows, stride=blocks), :] = part
    flat[pl.ds(base, rows * blocks), :] = wide[pl.ds(0, rows * blocks), :].astype(BF)


def rows_to_up(flat, base, wide, square, out):
    groups = BLOCK // UP_GROUP
    length = groups * UP_STRIDE
    wide[pl.ds(0, length), :] = flat[pl.ds(base, length), :].astype(F32)
    lanes = lane_index(groups)
    for row in range(UP_GROUP):
        first, shift = divmod(row * FF, LANES)
        held = None
        for block in range(UP_BLOCKS + 1):
            if block == UP_BLOCKS and shift + UP_TAIL <= LANES:
                piece = held
            else:
                piece = wide[pl.ds(first + block, groups, stride=UP_STRIDE), :]
                if shift:
                    piece = pltpu.roll(piece, LANES - shift, 1)
            if block:
                value = jnp.where(lanes < LANES - shift, held, piece) if shift else held
                square[block - 1, pl.ds(row, groups, stride=UP_GROUP), :] = value
            held = piece
    for block in range(UP_BLOCKS):
        first, last = (block * LANES, min(FF, (block + 1) * LANES))
        out[:, first:last] = square[block, :, : last - first].astype(BF)


def up_to_rows(matrix, square, wide, flat, base):
    groups = BLOCK // UP_GROUP
    length = groups * UP_STRIDE
    for block in range(UP_BLOCKS):
        first, last = (block * LANES, min(FF, (block + 1) * LANES))
        square[block, :, : last - first] = matrix[:, first:last].astype(F32)
    lanes = lane_index(groups)
    held = None
    for row in range(UP_GROUP):
        first, shift = divmod(row * FF, LANES)
        for block in range(UP_BLOCKS):
            piece = square[block, pl.ds(row, groups, stride=UP_GROUP), :]
            if shift:
                piece = pltpu.roll(piece, shift, 1)
                value = jnp.where(lanes < shift, held, piece)
            else:
                value = piece
            if block == UP_BLOCKS - 1 and shift + UP_TAIL < LANES:
                held = value
            else:
                wide[pl.ds(first + block, groups, stride=UP_STRIDE), :] = value
                held = piece
    flat[pl.ds(base, length), :] = wide[pl.ds(0, length), :].astype(BF)


def fetch(layout, shards, sources, flat, sem):
    origin = layout.start(shards[0])
    for shard in shards:
        for half, source, first, rows in layout.pieces(shard):
            pltpu.make_async_copy(
                sources[half].at[pl.ds(source, rows), :],
                flat.at[pl.ds(first - origin, rows), :],
                sem,
            ).start()
    whole = flat.at[pl.ds(0, layout.start(shards[-1] + 1) - origin), :]
    pltpu.make_async_copy(whole, whole, sem).wait()


def first_weights(layout, gathered):
    shards = layout.covering(ROW_QKV, ROW_OUT)
    origin = layout.start(shards[0])
    length = layout.start(shards[-1] + 1) - origin

    def kernel(source, qkv, flat, wide, sem):
        step = pl.program_id(0)

        @pl.when(step == 0)
        def _():
            fetch(layout, shards, (source,), flat, sem)

        base = pl.multiple_of(ROW_QKV - origin + step * (BLOCK * QKV_BLOCKS), TILE)
        rows_to_matrix(flat, base, BLOCK, QKV_BLOCKS, wide, qkv)

    return pl.pallas_call(
        kernel,
        name="first_weights",
        grid=(STEPS,),
        in_specs=[pl.BlockSpec(memory_space=pl.ANY)],
        out_specs=pl.BlockSpec((BLOCK, 3 * D), lambda i: (i, 0)),
        out_shape=jax.ShapeDtypeStruct((D, 3 * D), BF),
        scratch_shapes=[
            pltpu.VMEM((length, LANES), BF),
            pltpu.VMEM((BLOCK * QKV_BLOCKS, LANES), F32),
            pltpu.SemaphoreType.DMA,
        ],
        compiler_params=pltpu.CompilerParams(vmem_limit_bytes=VMEM_LIMIT),
    )(gathered)


def other_weights(layout, first_half, second_half):
    shards = layout.covering(ROW_OUT, ROW_VEC)
    origin = layout.start(shards[0])
    length = layout.start(shards[-1] + 1) - origin
    padded = max(length, ROW_DOWN - origin + STEPS * DOWN_BLOCK * D_BLOCKS)
    up_length = BLOCK // UP_GROUP * UP_STRIDE

    def kernel(first, second, out_w, up_w, down_w, flat, wide, square, sem):
        step = pl.program_id(0)

        @pl.when(step == 0)
        def _():
            fetch(layout, shards, (first, second), flat, sem)

        base = pl.multiple_of(ROW_OUT - origin + step * (BLOCK * D_BLOCKS), TILE)
        rows_to_matrix(flat, base, BLOCK, D_BLOCKS, wide, out_w)
        base = pl.multiple_of(ROW_UP - origin + step * up_length, TILE)
        rows_to_up(flat, base, wide, square, up_w)
        base = pl.multiple_of(ROW_DOWN - origin + step * (DOWN_BLOCK * D_BLOCKS), TILE)
        rows_to_matrix(flat, base, DOWN_BLOCK, D_BLOCKS, wide, down_w)

    return pl.pallas_call(
        kernel,
        name="other_weights",
        grid=(STEPS,),
        in_specs=[pl.BlockSpec(memory_space=pl.ANY)] * 2,
        out_specs=[
            pl.BlockSpec((BLOCK, D), lambda i: (i, 0)),
            pl.BlockSpec((BLOCK, FF), lambda i: (i, 0)),
            pl.BlockSpec((DOWN_BLOCK, D), lambda i: (i, 0)),
        ],
        out_shape=[
            jax.ShapeDtypeStruct((D, D), BF),
            jax.ShapeDtypeStruct((D, FF), BF),
            jax.ShapeDtypeStruct((FF, D), BF),
        ],
        scratch_shapes=[
            pltpu.VMEM((padded, LANES), BF),
            pltpu.VMEM((max(up_length + 8, DOWN_BLOCK * D_BLOCKS), LANES), F32),
            pltpu.VMEM((UP_BLOCKS, BLOCK, LANES), F32),
            pltpu.SemaphoreType.DMA,
        ],
        compiler_params=pltpu.CompilerParams(vmem_limit_bytes=VMEM_LIMIT),
    )(first_half, second_half)


def send_pieces(layout, half, origin, flat, out, sem):
    for device in range(layout.devices):
        column, within = divmod(device, 2 * layout.ctx)
        for slot in range(layout.half):
            shard = (half * layout.half + slot) * 2 * layout.ctx + within
            first = layout.start(shard) + column * layout.piece - origin
            target = (device * layout.half + slot) * layout.piece
            pltpu.make_async_copy(
                flat.at[pl.ds(first, layout.piece), :], out.at[pl.ds(target, layout.piece), :], sem
            ).start()
    pltpu.make_async_copy(out, out, sem).wait()


def late_gradients(layout, grad_qkv, grad_out, grad_up):
    count = layout.half * 2 * layout.ctx
    end = layout.start(count - 1) + layout.columns * layout.piece
    up_length = BLOCK // UP_GROUP * UP_STRIDE
    ups = -(-(end - ROW_UP) // up_length)
    padded = ROW_UP + ups * up_length
    rows = layout.devices * layout.half * layout.piece

    def kernel(qkv, out_w, up_w, pieces, flat, wide, square, sem):
        step = pl.program_id(0)
        base = pl.multiple_of(ROW_QKV + step * (BLOCK * QKV_BLOCKS), TILE)
        matrix_to_rows(qkv, BLOCK, QKV_BLOCKS, wide, flat, base)
        base = pl.multiple_of(ROW_OUT + step * (BLOCK * D_BLOCKS), TILE)
        matrix_to_rows(out_w, BLOCK, D_BLOCKS, wide, flat, base)

        @pl.when(step < ups)
        def _():
            base = pl.multiple_of(ROW_UP + step * up_length, TILE)
            up_to_rows(up_w, square, wide, flat, base)

        @pl.when(step == STEPS - 1)
        def _():
            send_pieces(layout, 0, 0, flat, pieces, sem)

    return pl.pallas_call(
        kernel,
        name="late_gradients",
        grid=(STEPS,),
        in_specs=[
            pl.BlockSpec((BLOCK, 3 * D), lambda i: (i, 0)),
            pl.BlockSpec((BLOCK, D), lambda i: (i, 0)),
            pl.BlockSpec((BLOCK, FF), lambda i: (jnp.minimum(i, ups - 1), 0)),
        ],
        out_specs=pl.BlockSpec(memory_space=pl.ANY),
        out_shape=jax.ShapeDtypeStruct((rows, LANES), BF),
        scratch_shapes=[
            pltpu.VMEM((padded, LANES), BF),
            pltpu.VMEM((max(up_length, BLOCK * QKV_BLOCKS), LANES), F32),
            pltpu.VMEM((UP_BLOCKS, BLOCK, LANES), F32),
            pltpu.SemaphoreType.DMA,
        ],
        compiler_params=pltpu.CompilerParams(vmem_limit_bytes=VMEM_LIMIT),
    )(grad_qkv, grad_out, grad_up)


def early_gradients(layout, grad_up, grad_down):
    start = layout.start(layout.half * 2 * layout.ctx)
    end = layout.start(layout.devices - 1) + layout.columns * layout.piece
    up_length = BLOCK // UP_GROUP * UP_STRIDE
    skipped = (start - ROW_UP) // up_length
    origin = ROW_UP + skipped * up_length
    padded = max(end, ROW_DOWN + STEPS * DOWN_BLOCK * D_BLOCKS) - origin
    rows = layout.devices * layout.half * layout.piece

    def kernel(up_w, down_w, pieces, flat, wide, square, sem):
        step = pl.program_id(0)

        @pl.when(step < STEPS - skipped)
        def _():
            base = pl.multiple_of(step * up_length, TILE)
            up_to_rows(up_w, square, wide, flat, base)

        base = pl.multiple_of(ROW_DOWN - origin + step * (DOWN_BLOCK * D_BLOCKS), TILE)
        matrix_to_rows(down_w, DOWN_BLOCK, D_BLOCKS, wide, flat, base)

        @pl.when(step == STEPS - 1)
        def _():
            tail = padded - (ROW_VEC - origin)
            flat[pl.ds(ROW_VEC - origin, tail), :] = jnp.zeros((tail, LANES), BF)
            send_pieces(layout, 1, origin, flat, pieces, sem)

    return pl.pallas_call(
        kernel,
        name="early_gradients",
        grid=(STEPS,),
        in_specs=[
            pl.BlockSpec((BLOCK, FF), lambda i: (jnp.minimum(i + skipped, STEPS - 1), 0)),
            pl.BlockSpec((DOWN_BLOCK, D), lambda i: (i, 0)),
        ],
        out_specs=pl.BlockSpec(memory_space=pl.ANY),
        out_shape=jax.ShapeDtypeStruct((rows, LANES), BF),
        scratch_shapes=[
            pltpu.VMEM((padded, LANES), BF),
            pltpu.VMEM((max(up_length, DOWN_BLOCK * D_BLOCKS), LANES), F32),
            pltpu.VMEM((UP_BLOCKS, BLOCK, LANES), F32),
            pltpu.SemaphoreType.DMA,
        ],
        compiler_params=pltpu.CompilerParams(vmem_limit_bytes=VMEM_LIMIT),
    )(grad_up, grad_down)


def dot_t(left, right):
    return lax.dot_general(left, right, (((1,), (1,)), ((), ())), preferred_element_type=F32)


def t_dot(left, right):
    return lax.dot_general(left, right, (((0,), (0,)), ((), ())), preferred_element_type=F32)


def dense(left, right):
    return jnp.dot(left, right, preferred_element_type=F32)


def masked(scores, count):
    columns = lax.broadcasted_iota(jnp.int32, scores.shape, 1)
    return jnp.where(columns < count, scores, masked_score)


def attend(counts, queries, keys, values, chunk):
    heads, length, _ = queries.shape

    def kernel(count, q, k, v, mixed, log_total):
        for first in range(0, length, chunk):
            scores = masked(dot_t(q[0, first : first + chunk, :], k[0]), count[0])
            top = jnp.max(scores, -1, keepdims=True)
            exponent = jnp.exp(scores - top)
            total = jnp.sum(exponent, -1, keepdims=True)
            probs = (exponent / total).astype(BF)
            mixed[0, first : first + chunk, :] = dense(probs, v[0]).astype(BF)
            log_total[0, first : first + chunk, :] = top + jnp.log(total)

    spec = pl.BlockSpec((1, length, HD), lambda h: (h, 0, 0))
    return pl.pallas_call(
        kernel,
        name="attend",
        grid=(heads,),
        in_specs=[pl.BlockSpec(memory_space=pltpu.SMEM), spec, spec, spec],
        out_specs=[spec, pl.BlockSpec((1, length, 1), lambda h: (h, 0, 0))],
        out_shape=[
            jax.ShapeDtypeStruct((heads, length, HD), BF),
            jax.ShapeDtypeStruct((heads, length, 1), F32),
        ],
        compiler_params=pltpu.CompilerParams(vmem_limit_bytes=VMEM_LIMIT),
    )(counts, queries, keys, values)


def attend_back(counts, queries, keys, values, log_total, grad_mixed, chunk):
    heads, length, _ = queries.shape
    scale = HD ** (-0.5)

    def kernel(count, q, k, v, logs, grad, dq, dk, dv, sum_q, sum_v, acc_k, acc_v):
        acc_k[...] = jnp.zeros_like(acc_k)
        acc_v[...] = jnp.zeros_like(acc_v)
        total_q = jnp.zeros((1, HD), F32)
        for first in range(0, length, chunk):
            part = slice(first, first + chunk)
            scores = masked(dot_t(q[0, part, :], k[0]), count[0])
            probs = jnp.exp(scores - logs[0, part, :])
            grad_probs = dot_t(grad[0, part, :], v[0])
            delta = jnp.sum(probs * grad_probs, -1, keepdims=True)
            grad_scores = (probs * (grad_probs - delta)).astype(BF)
            grad_query = dense(grad_scores, k[0]) * scale
            total_q = total_q + jnp.sum(grad_query, 0, keepdims=True)
            dq[0, part, :] = grad_query.astype(BF)
            acc_k[...] += t_dot(grad_scores, q[0, part, :])
            acc_v[...] += t_dot(probs.astype(BF), grad[0, part, :])
        dk[0] = acc_k[...].astype(BF)
        dv[0] = acc_v[...].astype(BF)
        sum_q[0] = total_q
        sum_v[0] = jnp.sum(acc_v[...], 0, keepdims=True)

    spec = pl.BlockSpec((1, length, HD), lambda h: (h, 0, 0))
    row = pl.BlockSpec((1, 1, HD), lambda h: (h, 0, 0))
    return pl.pallas_call(
        kernel,
        name="attend_back",
        grid=(heads,),
        in_specs=[
            pl.BlockSpec(memory_space=pltpu.SMEM),
            spec,
            spec,
            spec,
            pl.BlockSpec((1, length, 1), lambda h: (h, 0, 0)),
            spec,
        ],
        out_specs=[spec, spec, spec, row, row],
        out_shape=[jax.ShapeDtypeStruct((heads, length, HD), BF)] * 3
        + [jax.ShapeDtypeStruct((heads, 1, HD), F32)] * 2,
        scratch_shapes=[pltpu.VMEM((length, HD), F32)] * 2,
        compiler_params=pltpu.CompilerParams(vmem_limit_bytes=VMEM_LIMIT),
    )(counts, queries, keys, values, log_total, grad_mixed)


def norm_forward(residual):
    centre = residual - jnp.mean(residual, -1, keepdims=True)
    inverse = lax.rsqrt(jnp.mean(centre * centre, -1, keepdims=True) + norm_epsilon)
    return (centre * inverse, inverse)


def norm_back(grad_normed, unit, inverse, gain):
    scaled = grad_normed * gain
    return inverse * (
        scaled
        - jnp.mean(scaled, -1, keepdims=True)
        - unit * jnp.mean(scaled * unit, -1, keepdims=True)
    )


def adam_update(master, grads, first, second, index):
    matrix_part = index < 4 * D * D + 2 * D * FF
    first_new = beta_one * first + (1.0 - beta_one) * grads
    second_new = beta_two * second + (1.0 - beta_two) * grads * grads
    first_hat = first_new / (1.0 - beta_one**adam_step)
    second_hat = second_new / (1.0 - beta_two**adam_step)
    rate = jnp.where(matrix_part, rate_matrix, rate_vector)
    decay = jnp.where(matrix_part, weight_decay, 0.0)
    updated = master - rate * (first_hat / (jnp.sqrt(second_hat) + adam_epsilon) + decay * master)
    return (updated, first_new, second_new)


def to_heads(array, parts):
    ctx = lax.axis_size("ctx")
    rows = array.shape[0]
    split = array.reshape(rows, parts, ctx, D // ctx).transpose(2, 0, 1, 3)
    held = lax.all_to_all(split, "ctx", split_axis=0, concat_axis=0, tiled=True)
    held = held.reshape(rows * ctx, parts, H // ctx, HD).transpose(1, 2, 0, 3)
    return [held[part] for part in range(parts)]


def from_heads(arrays):
    ctx = lax.axis_size("ctx")
    parts, (heads, length, _) = (len(arrays), arrays[0].shape)
    stacked = jnp.stack(arrays).reshape(parts, heads, ctx, length // ctx, HD)
    split = stacked.transpose(2, 3, 0, 1, 4).reshape(ctx, length // ctx, parts, heads * HD)
    held = lax.all_to_all(split, "ctx", split_axis=0, concat_axis=0, tiled=True)
    return held.transpose(1, 2, 0, 3).reshape(length // ctx, parts * D)


def column_groups(layout):
    return [[column * 2 + core for column in range(layout.columns)] for core in range(2)]


def spread_weights(layout, flat, shard, everyone):
    last = layout.devices - 1
    before = lax.ppermute(
        flat[-TILE:], ("dp", "ctx"), [(index, index + 1) for index in range(last)]
    )
    length = layout.columns * layout.piece
    padded = jnp.concatenate([before, flat, jnp.zeros((length - layout.rows, LANES), BF)])
    offset = (shard * layout.rows) % TILE
    chunk = lax.dynamic_slice(padded, (TILE - offset, 0), (length, LANES))
    pieces = chunk.reshape(layout.columns, layout.piece, LANES)
    held = lax.all_to_all(
        pieces, "dp", split_axis=0, concat_axis=0, tiled=True, axis_index_groups=everyone
    )
    halves = held.reshape(2, layout.half * layout.piece, LANES)
    return (halves[0], halves[1])


def broadcast_vectors(layout, flat):
    first = ROW_VEC - (layout.devices - 1) * layout.rows
    assert 0 <= first and first + VEC_ROWS <= layout.rows
    held = flat[first : first + VEC_ROWS]
    for axis, size in (("dp", layout.dp), ("ctx", layout.ctx)):
        bit = 1
        while bit < size:
            other = lax.ppermute(held, axis, [(index, index ^ bit) for index in range(size)])
            mine = (lax.axis_index(axis) & bit) != 0
            held = jnp.where(mine, held, other)
            bit *= 2
    flat_vectors = held.reshape(-1).astype(F32)
    vectors = []
    offset = 0
    for length in VEC_LENGTHS:
        vectors.append(flat_vectors[offset : offset + length])
        offset += length
    return vectors


def scatter_half(pieces):
    partial = lax.psum_scatter(pieces, "dp", scatter_dimension=0, tiled=True)
    return lax.psum_scatter(partial, "ctx", scatter_dimension=0, tiled=True)


def shards(layout, inputs, counts, params, first_moment, second_moment, out_cotangent):
    local_rows = inputs.shape[1]
    shard = lax.axis_index(("dp", "ctx"))
    score_scale = HD ** (-0.5)
    everyone = column_groups(layout)
    chunk = 256

    flat = params.reshape(layout.rows, LANES).astype(BF)
    share_one, share_two = spread_weights(layout, flat, shard, everyone)
    half_one = lax.all_gather(share_one, ("dp", "ctx"), axis=0, tiled=True)
    half_two = lax.all_gather(share_two, ("dp", "ctx"), axis=0, tiled=True)
    (
        gain_one,
        shift_one,
        bias_query,
        bias_value,
        bias_out,
        gain_two,
        shift_two,
        bias_down,
        bias_up,
    ) = broadcast_vectors(layout, flat)

    residual = inputs[0].astype(F32)
    unit_one, inverse_one = norm_forward(residual)
    normed_round = (unit_one * gain_one + shift_one).astype(BF)
    qkv_weight = first_weights(layout, half_one)
    projected = dense(normed_round, qkv_weight)
    queries = ((projected[:, :D] + bias_query) * score_scale).astype(BF)
    keys = projected[:, D : 2 * D].astype(BF)
    values = (projected[:, 2 * D :] + bias_value).astype(BF)
    queries, keys, values = to_heads(jnp.concatenate([queries, keys, values], -1), 3)
    out_weight, up_weight, down_weight = other_weights(layout, half_one, half_two)
    mixed_heads, log_total = attend(counts, queries, keys, values, chunk)
    mixed = from_heads([mixed_heads])
    middle = residual + dense(mixed, out_weight) + bias_out
    unit_two, inverse_two = norm_forward(middle)
    normed_two_round = (unit_two * gain_two + shift_two).astype(BF)
    pre_gelu = dense(normed_two_round, up_weight) + bias_up
    activated = jax.nn.gelu(pre_gelu, approximate=True).astype(BF)
    output = (middle + dense(activated, down_weight) + bias_down).astype(BF)

    positions = lax.axis_index("ctx") * local_rows + jnp.arange(local_rows, dtype=jnp.int32)
    row_valid = (positions < counts[0])[:, None].astype(F32)
    grad_next = out_cotangent[0] * row_valid
    grad_bias_down = jnp.sum(grad_next, 0)
    grad_round = grad_next.astype(BF)
    grad_down = t_dot(activated, grad_round).astype(BF)
    grad_act = dot_t(grad_round, down_weight)
    gelu_back = jax.vjp(functools.partial(jax.nn.gelu, approximate=True), pre_gelu)[1]
    grad_pre = gelu_back(grad_act)[0]
    grad_bias_up = jnp.sum(grad_pre, 0)
    grad_pre_round = grad_pre.astype(BF)
    grad_up = t_dot(normed_two_round, grad_pre_round).astype(BF)
    half_two_sum = scatter_half(early_gradients(layout, grad_up, grad_down))
    grad_normed_two = dot_t(grad_pre_round, up_weight)
    grad_gain_two = jnp.sum(grad_normed_two * unit_two, 0)
    grad_shift_two = jnp.sum(grad_normed_two, 0)
    grad_middle = grad_next + norm_back(grad_normed_two, unit_two, inverse_two, gain_two)
    grad_bias_out = jnp.sum(grad_middle, 0)
    middle_round = grad_middle.astype(BF)
    grad_out = t_dot(mixed, middle_round).astype(BF)
    grad_mixed = dot_t(middle_round, out_weight).astype(BF)
    (grad_mixed_heads,) = to_heads(grad_mixed, 1)
    grad_q, grad_k, grad_v, sum_q, sum_v = attend_back(
        counts, queries, keys, values, log_total, grad_mixed_heads, chunk
    )
    grad_projected = from_heads([grad_q, grad_k, grad_v])
    grad_qkv = t_dot(normed_round, grad_projected).astype(BF)
    half_one_sum = scatter_half(late_gradients(layout, grad_qkv, grad_out, grad_up))
    grad_normed_one = dot_t(grad_projected, qkv_weight)
    grad_gain_one = jnp.sum(grad_normed_one * unit_one, 0)
    grad_shift_one = jnp.sum(grad_normed_one, 0)
    input_grad = grad_middle + norm_back(grad_normed_one, unit_one, inverse_one, gain_one)

    share = D // layout.ctx
    place = (lax.axis_index("ctx") * share,)
    grad_bias_query = lax.dynamic_update_slice(jnp.zeros((D,), F32), sum_q.reshape(-1), place)
    grad_bias_value = lax.dynamic_update_slice(jnp.zeros((D,), F32), sum_v.reshape(-1), place)
    vector_terms = [
        grad_gain_one,
        grad_shift_one,
        grad_bias_query,
        grad_bias_value,
        grad_bias_out,
        grad_gain_two,
        grad_shift_two,
        grad_bias_down,
        grad_bias_up,
    ]
    padding = jnp.zeros((VEC_ROWS * LANES - sum(VEC_LENGTHS),), F32)
    vector_grads = lax.psum(jnp.concatenate(vector_terms + [padding]), ("dp", "ctx"))

    summed = jnp.concatenate([half_one_sum, half_two_sum])
    held = lax.all_to_all(
        summed.reshape(layout.columns, layout.piece, LANES),
        "dp",
        split_axis=0,
        concat_axis=0,
        tiled=True,
        axis_index_groups=everyone,
    )
    offset = (shard * layout.rows) % TILE
    rows = lax.dynamic_slice(
        held.reshape(-1, LANES).astype(F32), (offset, 0), (layout.rows, LANES)
    )
    first = ROW_VEC - (layout.devices - 1) * layout.rows
    with_vectors = lax.dynamic_update_slice(
        rows, vector_grads.reshape(VEC_ROWS, LANES), (first, 0)
    )
    rows = jnp.where(shard == layout.devices - 1, with_vectors, rows)
    param_grads = rows.reshape(params.shape)
    index = (shard * params.shape[1] + jnp.arange(params.shape[1], dtype=jnp.int32))[None, :]
    new_params, new_first, new_second = adam_update(
        params, param_grads, first_moment, second_moment, index
    )
    return (output[None], input_grad[None], param_grads, new_params, new_first, new_second)


def solution(mesh):
    placed = (
        P("dp", "ctx", None),
        P("dp"),
        P(None, ("dp", "ctx")),
        P(None, ("dp", "ctx")),
        P(None, ("dp", "ctx")),
        P("dp", "ctx", None),
    )
    dp, ctx = (mesh.shape["dp"], mesh.shape["ctx"])

    def program(inputs, counts, params, first_moment, second_moment, out_cotangent):
        layout = Layout(dp, ctx, params.shape[1] // (dp * ctx))
        return jax.shard_map(
            functools.partial(shards, layout),
            mesh=mesh,
            in_specs=placed,
            out_specs=(
                P("dp", "ctx", None),
                P("dp", "ctx", None),
                P(None, ("dp", "ctx")),
                P(None, ("dp", "ctx")),
                P(None, ("dp", "ctx")),
                P(None, ("dp", "ctx")),
            ),
            check_vma=False,
        )(inputs, counts, params, first_moment, second_moment, out_cotangent)

    return program
```

profile of v0, /device:TPU:1, one launch (start us, length us, event | category | flops | bytes accessed | tf_op | source)
XLA Modules:
  0.0 883.0 jit_solution(9527980883846920522)
XLA Ops:
  15.8 20.7 %convert_reduce_fusion.1 = bf16[476288]{0:T(1024)(128)(2,1)} fusion(f32[1,476288]{1,0:T(1,128)S(1)} %copy-done), kind=kLoop, calls=%fused_computation.118 | loop fusion | flops 476288 | bytes 2857728 | tf_op jit(solution)/shard_map/convert_element_type | solution.py:536
  40.9 15.2 %all_to_all.30 = bf16[4,944,128]{2,1,0:T(8,128)(2,1)S(1)} all-to-all(bf16[4,944,128]{2,1,0:T(8,128)(2,1)S(1)} %bitcast.158), channel_id=1, replica_groups={{0,8,16,24},{4,12,20,28},{1,9,17,25},{5,13,21,29},{2,10,18,26},{6,14,22..., dimensions={0} | all-to-all | bytes 1933312 | tf_op jit(solution)/shard_map/all_to_all | solution.py:497
  74.1 5.1 collective-permute-done.4
  79.2 88.1 %all-gather.3.cloned.1.call-done.source.first = bf16[60416,128]{1,0:T(8,128)(2,1)} async-done(((bf16[1888,128]{1,0:T(8,128)(2,1)}), bf16[60416,128]{1,0:T(8,128)(2,1)}) %all-gather.3.cloned.1.call-update) | async-done | bytes 15466512 | tf_op jit(solution)/shard_map/all_gather | solution.py:538
  167.3 9.5 %first_weights.1 = bf16[1152,3456]{1,0:T(8,128)(2,1)} custom-call(bf16[60416,128]{1,0:T(8,128)(2,1)} %all-gather.3.cloned.1.call-done.source.first), custom_call_target="tpu_custom_call" | custom-call | tf_op jit(solution)/shard_map/first_weights/pallas_call | solution.py:180
  176.9 6.3 fusion.42
  191.4 4.6 all-to-all-start.1
  196.7 61.1 %all-to-all-done.1 = bf16[4,256,3,288]{1,3,2,0:T(8,128)(2,1)} async-done(((bf16[4,256,3,288]{1,3,2,0:T(8,128)(2,1)}), bf16[4,256,3,288]{1,3,2,0:T(8,128)(2,1)}, u32[]{:S(2)}, u32[]{:S(2)}) %all-to-all-start.1) | async-done | bytes 1769504 | tf_op jit(solution)/shard_map/all_to_all | solution.py:469
  266.1 4.4 copy.28
  274.1 12.5 %attend.1 = (bf16[4,1024,72]{2,1,0:T(8,128)(2,1)}, f32[4,1024,1]{2,1,0:T(8,128)}) custom-call(s32[1]{0:T(128)} %copy.49.count, bf16[4,1024,72]{2,1,0:T(8,128)(2,1)} %get-tuple-element.44.q, bf16[4,1024,72]{2,1,0:T(8,128)(2,1)} %get-tuple-element.43.k, bf16[4,1024,72]{2,1,0:T(8,128)(2,1)} %get-tuple-element.42.v), custom_call_target="tpu_custom_call" | custom-call | tf_op jit(solution)/shard_map/attend/pallas_call | solution.py:377
  292.3 20.0 %all-gather.5.cloned.1.call-done.second = bf16[60416,128]{1,0:T(8,128)(2,1)} async-done(((bf16[1888,128]{1,0:T(8,128)(2,1)}), bf16[60416,128]{1,0:T(8,128)(2,1)}) %all-gather.5.cloned.1.call-update) | async-done | bytes 15466512 | tf_op jit(solution)/shard_map/all_gather | solution.py:539
  312.3 21.3 %other_weights.1 = (bf16[1152,1152]{1,0:T(8,128)(2,1)}, bf16[1152,4304]{1,0:T(8,128)(2,1)}, bf16[4304,1152]{1,0:T(8,128)(2,1)}) custom-call(bf16[60416,128]{1,0:T(8,128)(2,1)} %all-gather.3.cloned.1.call-done.source.first, bf16[60416,128]{1,0:T(8,128)(2,1)} %all-gather.5.cloned.1.call-done.second), custom_call_target="tpu_custom_call" | custom-call | tf_op jit(solution)/shard_map/other_weights/pallas_call | solution.py:217
  338.0 10.4 %fusion.54 = f32[256,4304]{0,1:T(8,128)} fusion(bf16[1152,4304]{1,0:T(8,128)(2,1)} %get-tuple-element.18, f32[1152]{0:T(1024)S(1)} %get-tuple-element.50, f32[1152]{0:T(1024)S(1)} %get-tuple-element.48, f32[256,1152]{1,0:T(8,128)S(1)} %get-tuple-element.57, f32[256]{0:T(256)S(1)} %add_rsqrt_fusion, f32[256]{0:T(256)S(1)} %broadcast_multiply_fusion.4, ...), kind=kOutput, calls=%fused_computation.91 | convolution fusion | flops 2540371968 | bytes 15519232 | tf_op jit(solution)/shard_map/dot_general | solution.py:355
  348.4 8.7 convolution_convert_fusion.down_w
  357.1 14.7 %fusion.63 = (f32[4304]{0:T(1024)S(1)}, bf16[256,4304]{0,1:T(8,128)(2,1)S(1)}) fusion(f32[256,4304]{0,1:T(8,128)S(1)} %copy-done.14, f32[4304]{0:T(1024)S(1)} %slice.137, bf16[4304,1152]{1,0:T(8,128)(2,1)S(1)} %bitcast.175, f32[1,256,1152]{2,1,0:T(8,128)S(1)} %copy-done.9, f32[256]{0:T(256)S(1)} %compare_convert_fusion), kind=kOutput, calls=%fused_computation.122 | convolution fusion | flops 2563428096 | bytes 17742464 | tf_op jit(solution)/shard_map/dot_general | solution.py:347
  373.3 5.9 convolution_convert_fusion.1.up_w
  379.2 16.5 %early_gradients.1 = bf16[60416,128]{1,0:T(8,128)(2,1)} custom-call(bf16[1152,4304]{1,0:T(8,128)(2,1)} %convolution_convert_fusion.1.up_w, bf16[4304,1152]{1,0:T(8,128)(2,1)} %convolution_convert_fusion.down_w), custom_call_target="tpu_custom_call" | custom-call | tf_op jit(solution)/shard_map/early_gradients/pallas_call | solution.py:326
  395.8 8.1 multiply_reduce_fusion
  410.1 19.2 %all_to_all.31 = bf16[4,256,1,288]{1,3,2,0:T(8,128)(2,1)S(1)} all-to-all(bf16[4,256,1,288]{1,3,2,0:T(8,128)(2,1)} %bitcast.163), channel_id=1, replica_groups=mesh['dp'=8,'ctx'=4] {'ctx'}, dimensions={0} | all-to-all | bytes 1179648 | tf_op jit(solution)/shard_map/all_to_all | solution.py:469
  435.1 19.0 %attend_back.1 = (bf16[4,1024,72]{2,1,0:T(8,128)(2,1)}, bf16[4,1024,72]{2,1,0:T(8,128)(2,1)}, bf16[4,1024,72]{2,1,0:T(8,128)(2,1)}, f32[4,1,72]{2,1,0:T(1,128)}, f32[4,1,72]{2,1,0:T(1,128)}) custom-call(s32[1]{0:T(128)} %copy.49.count, bf16[4,1024,72]{2,1,0:T(8,128)(2,1)} %get-tuple-element.44.q, bf16[4,1024,72]{2,1,0:T(8,128)(2,1)} %get-tuple-element.43.k, ...), custom_call_target="tpu_custom_call" | custom-call | tf_op jit(solution)/shard_map/attend_back/pallas_call | solution.py:418
  463.4 4.4 all-to-all-start.4
  471.9 36.7 %all-to-all-done.4 = bf16[4,256,3,288]{1,3,2,0:T(8,128)(2,1)} async-done(((bf16[4,256,3,288]{1,3,2,0:T(8,128)(2,1)}), bf16[4,256,3,288]{1,3,2,0:T(8,128)(2,1)}, u32[]{:S(2)}, u32[]{:S(2)}) %all-to-all-start.4) | async-done | bytes 1769504 | tf_op jit(solution)/shard_map/all_to_all | solution.py:479
  511.5 5.8 convolution_convert_fusion.2.qkv
  517.3 16.7 %late_gradients.1 = bf16[60416,128]{1,0:T(8,128)(2,1)} custom-call(bf16[1152,3456]{1,0:T(8,128)(2,1)} %convolution_convert_fusion.2.qkv, bf16[1152,1152]{1,0:T(8,128)(2,1)} %convolution_convert_fusion.3.out_w, bf16[1152,4304]{1,0:T(8,128)(2,1)} %convolution_convert_fusion.1.up_w), custom_call_target="tpu_custom_call" | custom-call | tf_op jit(solution)/shard_map/late_gradients/pallas_call | solution.py:279
  534.6 107.8 %reduce-scatter.5.cloned.1.call-done = bf16[7552,128]{1,0:T(8,128)(2,1)} async-done(((bf16[60416,128]{1,0:T(8,128)(2,1)}), bf16[7552,128]{1,0:T(8,128)(2,1)}) %reduce-scatter.5.cloned.1.call-update) | async-done | bytes 1933328 | tf_op jit(solution)/shard_map/reduce_scatter | solution.py:525
  642.8 9.4 %fusion.39 = bf16[1,256,1152]{2,1,0:T(8,128)(2,1)} fusion(f32[1152]{0:T(1024)S(1)} %get-tuple-element.49, bf16[4304,1152]{1,0:T(8,128)(2,1)} %get-tuple-element.19, f32[256,1152]{1,0:T(8,128)S(1)} %get-tuple-element.57, f32[1152]{0:T(1024)S(1)} %get-tuple-element.51, f32[256,4304]{0,1:T(8,128)} %fusion.54, f32[4304]{0:T(1024)S(1)} %slice.137), kind=kOutput, calls=%fused_computation.78 | convolution fusion | flops 2550800384 | bytes 16119616 | tf_op jit(solution)/shard_map/dot_general | solution.py:355
  654.7 7.7 fusion.25
  663.2 22.3 %reduce-scatter.11.cloned.1.call-done = bf16[1888,128]{1,0:T(8,128)(2,1)} async-done(((bf16[7552,128]{1,0:T(8,128)(2,1)}), bf16[1888,128]{1,0:T(8,128)(2,1)}) %reduce-scatter.11.cloned.1.call-update) | async-done | bytes 483344 | tf_op jit(solution)/shard_map/reduce_scatter | solution.py:526
  685.5 42.4 %reduce-scatter.7.cloned.1.call-done = bf16[1888,128]{1,0:T(8,128)(2,1)} async-done(((bf16[7552,128]{1,0:T(8,128)(2,1)}), bf16[1888,128]{1,0:T(8,128)(2,1)}) %reduce-scatter.7.cloned.1.call-update) | async-done | bytes 483344 | tf_op jit(solution)/shard_map/reduce_scatter | solution.py:526
  736.7 9.2 %all-to-all-done.5 = bf16[4,944,128]{2,1,0:T(8,128)(2,1)S(1)} async-done(((bf16[4,944,128]{2,1,0:T(8,128)(2,1)}), bf16[4,944,128]{2,1,0:T(8,128)(2,1)S(1)}, u32[]{:S(2)}, u32[]{:S(2)}) %all-to-all-start.5) | async-done | bytes 966688 | tf_op jit(solution)/shard_map/all_to_all | solution.py:623
  747.4 108.9 %all-reduce.2.cloned.1.call-done = f32[128,128]{1,0:T(8,128)} async-done(((f32[128,128]{1,0:T(8,128)}), f32[128,128]{1,0:T(8,128)}) %all-reduce.2.cloned.1.call-update) | async-done | bytes 65552 | tf_op jit(solution)/shard_map/psum | solution.py:620
  858.7 17.0 %fusion.8 = (f32[1,476288]{1,0:T(1,128)}, f32[1,476288]{1,0:T(1,128)}, f32[1,476288]{1,0:T(1,128)}, f32[1,476288]{1,0:T(1,128)}) fusion(f32[1,476288]{1,0:T(1,128)S(1)} %copy-done, s32[]{:T(128)S(6)} %mul.281, f32[1,476288]{1,0:T(1,128)} %param.9, f32[1,476288]{1,0:T(1,128)} %param.10, f32[1,1,3721,128]{3,2,1,0:T(8,128)} %bitcast.152), kind=kLoop, calls=%fused_computation.21 | loop fusion | flops 9049472 | bytes 15241220 | tf_op jit(solution)/shard_map/sub | solution.py:461
  (129 shorter events, 107.5 us)
Async XLA Ops:
  7.2 8.6 copy-start
  7.2 160.2 %all-gather.3.cloned.1.call-start = ((), (), s32[]{:S(2)}) async-start(), calls=%async_computation.10 | async-start | bytes 15949824 | tf_op jit(solution)/shard_map/all_gather | solution.py:538
  10.5 1.3 copy-start.8
  11.8 24.8 %collective-permute-start.5 = (bf16[16,128]{1,0:T(8,128)(2,1)S(1)}, bf16[16,128]{1,0:T(8,128)(2,1)S(1)}, u32[]{:S(2)}, u32[]{:S(2)}) collective-permute-start(bf16[16,128]{1,0:T(8,128)(2,1)S(1)} %bitcast.173), channel_id=1, source_target_pairs={{0,1},{1,2},{2,3},{3,4},{4,5},{5,6},{6,7},{7,8},{8,9},{9,10},{10,1... | collective-permute-start | bytes 12296 | tf_op jit(solution)/shard_map/ppermute | solution.py:489
  56.0 6.7 copy-start.1
  57.0 255.3 %all-gather.5.cloned.1.call-start = ((), (), s32[]{:S(2)}) async-start(), calls=%async_computation.11 | async-start | bytes 15949824 | tf_op jit(solution)/shard_map/all_gather | solution.py:539
  58.8 3.4 collective-permute-start
  62.3 2.8 collective-permute-start.1
  65.0 2.8 collective-permute-start.2
  67.9 5.5 collective-permute-start.3
  73.4 5.8 collective-permute-start.4
  191.4 66.4 %all-to-all-start.1 = ((bf16[4,256,3,288]{1,3,2,0:T(8,128)(2,1)}), bf16[4,256,3,288]{1,3,2,0:T(8,128)(2,1)}, u32[]{:S(2)}, u32[]{:S(2)}) async-start(bf16[4,256,3,288]{1,3,2,0:T(8,128)(2,1)} %copy.26), calls=%async_computation.1 | async-start | bytes 3538944 | tf_op jit(solution)/shard_map/all_to_all | solution.py:469
  288.8 44.9 %all-to-all-start.2 = ((bf16[4,256,1,288]{1,3,2,0:T(8,128)(2,1)}), bf16[4,256,1,288]{1,3,2,0:T(8,128)(2,1)S(1)}, u32[]{:S(2)}, u32[]{:S(2)}) async-start(bf16[4,256,1,288]{1,3,2,0:T(8,128)(2,1)} %bitcast.16), calls=%async_computation.2 | async-start | bytes 1179648 | tf_op jit(solution)/shard_map/all_to_all | solution.py:479
  292.2 241.8 %reduce-scatter.9.cloned.1.call-start = ((), (), s32[]{:S(2)}) async-start(), calls=%async_computation.14 | async-start | bytes 17399808 | tf_op jit(solution)/shard_map/reduce_scatter | solution.py:525
  338.0 10.4 %copy-start.9 = (f32[1,256,1152]{2,1,0:T(8,128)S(1)}, f32[1,256,1152]{2,1,0:T(8,128)}, u32[]{:S(2)}) copy-start(f32[1,256,1152]{2,1,0:T(8,128)} %param.11) | copy-start | bytes 3538948
  338.0 19.1 %slice-start = ((s8[9916416]{0:T(1024)(128)(4,1)}), s8[4194304]{0:T(1024)(128)(4,1)S(1)}, s32[]{:S(2)}) async-start(s8[9916416]{0:T(1024)(128)(4,1)} %bitcast.174), calls=%async_computation.17 | async-start | bytes 8388608
  338.0 19.1 %slice-start.1 = ((s8[9916416]{0:T(1024)(128)(4,1)}), s8[4194304]{0:T(1024)(128)(4,1)S(1)}, s32[]{:S(2)}) async-start(s8[9916416]{0:T(1024)(128)(4,1)} %bitcast.174), calls=%async_computation.18 | async-start | bytes 8388608
  348.4 8.7 slice-start.2
  348.4 8.7 copy-start.14
  371.9 1.4 copy-start.7
  395.8 8.1 copy-start.10
  403.9 2.2 copy-start.13
  463.4 45.2 %all-to-all-start.4 = ((bf16[4,256,3,288]{1,3,2,0:T(8,128)(2,1)}), bf16[4,256,3,288]{1,3,2,0:T(8,128)(2,1)}, u32[]{:S(2)}, u32[]{:S(2)}) async-start(bf16[4,256,3,288]{1,3,2,0:T(8,128)(2,1)} %bitcast.155), calls=%async_computation.4 | async-start | bytes 3538944 | tf_op jit(solution)/shard_map/all_to_all | solution.py:479
  467.9 174.6 %reduce-scatter.5.cloned.1.call-start = ((), (), s32[]{:S(2)}) async-start(), calls=%async_computation.12 | async-start | bytes 17399808 | tf_op jit(solution)/shard_map/reduce_scatter | solution.py:525
  508.6 2.9 copy-start.2
  534.0 151.5 %reduce-scatter.11.cloned.1.call-start = ((), (), s32[]{:S(2)}) async-start(), calls=%async_computation.15 | async-start | bytes 2416640 | tf_op jit(solution)/shard_map/reduce_scatter | solution.py:526
  534.6 193.3 %reduce-scatter.7.cloned.1.call-start = ((), (), s32[]{:S(2)}) async-start(), calls=%async_computation.13 | async-start | bytes 2416640 | tf_op jit(solution)/shard_map/reduce_scatter | solution.py:526
  642.5 213.8 %all-reduce.2.cloned.1.call-start = ((), (), s32[]{:S(2)}) async-start(), calls=%async_computation.16 | async-start | bytes 131072 | tf_op jit(solution)/shard_map/psum | solution.py:620
  642.8 9.9 %copy-start.12 = (f32[4,1,72]{2,1,0:T(1,128)S(1)}, f32[4,1,72]{2,1,0:T(1,128)}, u32[]{:S(2)}) copy-start(f32[4,1,72]{2,1,0:T(1,128)} %get-tuple-element.24) | copy-start | bytes 3460
  642.8 10.6 %copy-start.11 = (f32[4,1,72]{2,1,0:T(1,128)S(1)}, f32[4,1,72]{2,1,0:T(1,128)}, u32[]{:S(2)}) copy-start(f32[4,1,72]{2,1,0:T(1,128)} %get-tuple-element.25) | copy-start | bytes 3460
  663.2 70.4 %copy-start.3 = (bf16[1,256,1152]{2,1,0:T(8,128)(2,1)S(1)}, bf16[1,256,1152]{2,1,0:T(8,128)(2,1)}, u32[]{:S(2)}) copy-start(bf16[1,256,1152]{2,1,0:T(8,128)(2,1)} %param.6) | copy-start | bytes 1769476
  730.0 15.9 %all-to-all-start.5 = ((bf16[4,944,128]{2,1,0:T(8,128)(2,1)}), bf16[4,944,128]{2,1,0:T(8,128)(2,1)S(1)}, u32[]{:S(2)}, u32[]{:S(2)}) async-start(bf16[4,944,128]{2,1,0:T(8,128)(2,1)} %bitcast.45), calls=%async_computation.9 | async-start | bytes 1933312 | tf_op jit(solution)/shard_map/all_to_all | solution.py:623
  (3 other events, 3.0 us)
Sparse Core Ops, SparseCore 0:
  57.2 110.1 all-gather.2
  170.8 141.5 all-gather.4
  395.9 108.5 reduce-scatter.8
  534.1 108.2 reduce-scatter.4
  644.6 40.8 reduce-scatter.10
  687.7 40.1 reduce-scatter.6
  734.0 122.2 all-reduce.1
where the time goes:
time: 892 us; the launch traced here: 883 us
  waiting for transfers between devices  512 us (57%)
  Pallas kernels  95.5 us (11%)
  matrix products  86 us (10%)
  local copies, waits for them, and re-layouts  57.4 us (6%)
  other arithmetic  55.7 us (6%)
  blocking collectives  34.3 us (4%)
  starting transfers between devices  26.1 us (3%)
  between operations  15.6 us (2%)
    psum x1, waiting for transfers between devices, shards(): lax.psum(jnp.concatenate(vector_terms + [padding]), ('dp', 'ctx'))  109 us
    reduce_scatter x2, waiting for transfers between devices, scatter_half(): partial = lax.psum_scatter(pieces, 'dp', scatter_dimension=0, tiled=True)  108 us
    all_gather x1, waiting for transfers between devices, shards(): half_one = lax.all_gather(share_one, ('dp', 'ctx'), axis=0, tiled=True)  88.1 us
    reduce_scatter x2, waiting for transfers between devices, scatter_half(): return lax.psum_scatter(partial, 'ctx', scatter_dimension=0, tiled=True)  64.7 us
    all_to_all x1, waiting for transfers between devices, to_heads(): held = lax.all_to_all(split, 'ctx', split_axis=0, concat_axis=0, tiled=True)  61.1 us
    all_to_all x2, waiting for transfers between devices, from_heads(): held = lax.all_to_all(split, 'ctx', split_axis=0, concat_axis=0, tiled=True)  36.7 us
    dot_general x4, matrix products, dot_t(): lax.dot_general(left, right, (((1,), (1,)), ((), ())), preferred_element_...  32.3 us
    dot_general x4, matrix products, dense(): return jnp.dot(left, right, preferred_element_type=F32)  29.3 us
  transfers between devices with their start and end apart: 17, of which 14 were waited for; matrix products, arithmetic and copies ran while one was open for 14% of the time, Pallas kernels for 9%

commit v1 on v0

v1 whole, which is shorter than its diff:
```python
import functools
import math

import jax
import jax.numpy as jnp
from jax import lax
from jax.experimental import pallas as pl
from jax.experimental.pallas import tpu as pltpu
from jax.sharding import PartitionSpec as P

D = 1152
H = 16
HD = 72
FF = 4304
LANES = 128
TILE = 16

norm_epsilon = 1e-06
beta_one = 0.9
beta_two = 0.95
adam_epsilon = 1e-08
adam_step = 3
rate_matrix = 0.005
rate_vector = 0.1
weight_decay = 0.1
masked_score = -1e30

BF = jnp.bfloat16
F32 = jnp.float32

QKV_BLOCKS = 3 * D // LANES
D_BLOCKS = D // LANES
ROW_QKV = 0
ROW_OUT = D * QKV_BLOCKS
ROW_UP = ROW_OUT + D * D_BLOCKS
ROW_DOWN = ROW_UP + D * FF // LANES
ROW_VEC = ROW_DOWN + FF * D_BLOCKS
VEC_ROWS = 128
VEC_LENGTHS = [D] * 8 + [FF]

UP_GROUP = LANES // math.gcd(FF, LANES)
UP_STRIDE = UP_GROUP * FF // LANES
UP_BLOCKS = -(-FF // LANES)
UP_TAIL = FF - (UP_BLOCKS - 1) * LANES
STEPS = 9
BLOCK = D // STEPS
DOWN_BLOCK = -(-FF // (STEPS * TILE)) * TILE
VMEM_LIMIT = 60 * 1024 * 1024


class Layout:
    def __init__(self, dp, ctx, shard_length):
        self.dp, self.ctx = dp, ctx
        self.devices = dp * ctx
        self.columns = dp // 2
        self.rows = shard_length // LANES
        longest = (self.rows + TILE - 1) // TILE
        self.piece = -(-longest // self.columns) * TILE
        self.group_shards = 2 * ctx
        self.first = ROW_OUT // (self.group_shards * self.rows)
        self.last_piece = self.rows // TILE * TILE - (self.columns - 1) * self.piece
        assert self.first > 0 and self.last_piece > 0

    def start(self, shard):
        return shard * self.rows // TILE * TILE

    def group_start(self, group):
        return self.start(group * self.group_shards)

    def group_end(self, group):
        return self.start(group * self.group_shards - 1) + self.columns * self.piece

    def leftover(self):
        shard = self.first * self.group_shards
        found = []
        while self.start(shard) < ROW_OUT:
            found.append((shard, min(ROW_OUT, self.start(shard + 1)) - self.start(shard)))
            shard += 1
        return found


def lane_index(rows):
    return lax.broadcasted_iota(jnp.int32, (rows, LANES), 1)


def rows_to_matrix(flat, base, rows, blocks, wide, out):
    wide[pl.ds(0, rows * blocks), :] = flat[pl.ds(base, rows * blocks), :].astype(F32)
    for block in range(blocks):
        part = wide[pl.ds(block, rows, stride=blocks), :]
        out[:, block * LANES : (block + 1) * LANES] = part.astype(BF)


def matrix_to_rows(matrix, rows, blocks, wide, flat, base):
    for block in range(blocks):
        part = matrix[:, block * LANES : (block + 1) * LANES].astype(F32)
        wide[pl.ds(block, rows, stride=blocks), :] = part
    flat[pl.ds(base, rows * blocks), :] = wide[pl.ds(0, rows * blocks), :].astype(BF)


def rows_to_up(flat, base, wide, square, out):
    groups = BLOCK // UP_GROUP
    length = groups * UP_STRIDE
    wide[pl.ds(0, length), :] = flat[pl.ds(base, length), :].astype(F32)
    lanes = lane_index(groups)
    for row in range(UP_GROUP):
        first, shift = divmod(row * FF, LANES)
        held = None
        for block in range(UP_BLOCKS + 1):
            if block == UP_BLOCKS and shift + UP_TAIL <= LANES:
                piece = held
            else:
                piece = wide[pl.ds(first + block, groups, stride=UP_STRIDE), :]
                if shift:
                    piece = pltpu.roll(piece, LANES - shift, 1)
            if block:
                value = jnp.where(lanes < LANES - shift, held, piece) if shift else held
                square[block - 1, pl.ds(row, groups, stride=UP_GROUP), :] = value
            held = piece
    for block in range(UP_BLOCKS):
        first, last = (block * LANES, min(FF, (block + 1) * LANES))
        out[:, first:last] = square[block, :, : last - first].astype(BF)


def up_to_rows(matrix, square, wide, flat, base):
    groups = BLOCK // UP_GROUP
    length = groups * UP_STRIDE
    for block in range(UP_BLOCKS):
        first, last = (block * LANES, min(FF, (block + 1) * LANES))
        square[block, :, : last - first] = matrix[:, first:last].astype(F32)
    lanes = lane_index(groups)
    held = None
    for row in range(UP_GROUP):
        first, shift = divmod(row * FF, LANES)
        for block in range(UP_BLOCKS):
            piece = square[block, pl.ds(row, groups, stride=UP_GROUP), :]
            if shift:
                piece = pltpu.roll(piece, shift, 1)
                value = jnp.where(lanes < shift, held, piece)
            else:
                value = piece
            if block == UP_BLOCKS - 1 and shift + UP_TAIL < LANES:
                held = value
            else:
                wide[pl.ds(first + block, groups, stride=UP_STRIDE), :] = value
                held = piece
    flat[pl.ds(base, length), :] = wide[pl.ds(0, length), :].astype(BF)


def fetch(layout, place, groups, origin, sources, flat, sem):
    low, high = groups
    count = high - low
    for ref, (column, core, first_row, members) in sources:
        device_column = jnp.bitwise_xor(place[0], column)
        device_core = jnp.bitwise_xor(place[1], core)

        def body(index, _, ref=ref, first_row=first_row):
            row = jnp.bitwise_xor(place[2], first_row + index // count)
            group = low + index % count
            shard = group * layout.group_shards + device_core * layout.ctx + row
            start = shard * layout.rows // TILE * TILE
            target = pl.multiple_of(start + device_column * layout.piece - origin, TILE)
            source = pl.multiple_of(index * layout.piece, TILE)

            def copy(offset, rows):
                pltpu.make_async_copy(
                    ref.at[pl.ds(source + offset, rows), :],
                    flat.at[pl.ds(target + offset, rows), :],
                    sem,
                ).start()

            is_last = device_column == layout.columns - 1
            longer = shard * layout.rows % TILE + layout.rows % TILE >= TILE

            @pl.when(jnp.logical_not(is_last))
            def _():
                copy(0, layout.piece)

            @pl.when(is_last)
            def _():
                copy(0, layout.last_piece)

            @pl.when(jnp.logical_and(is_last, longer))
            def _():
                copy(layout.last_piece, TILE)

            return 0

        lax.fori_loop(0, members * count, body, 0)


def flat_of(gathered):
    return [array for array, _ in gathered]


def first_weights(layout, place, gathered, leftover):
    inside = layout.group_start(layout.first)
    length = inside + leftover.shape[0]
    assert length == ROW_OUT
    arrays = flat_of(gathered)

    def kernel(place_ref, *refs):
        sources, (extra, qkv, flat, wide, sem) = (refs[: len(arrays)], refs[len(arrays) :])
        step = pl.program_id(0)

        @pl.when(step == 0)
        def _():
            named = [(ref, entry) for ref, (_, entry) in zip(sources, gathered)]
            fetch(layout, place_ref, (0, layout.first), 0, named, flat, sem)
            pltpu.make_async_copy(
                extra, flat.at[pl.ds(inside, leftover.shape[0]), :], sem
            ).start()
            pltpu.make_async_copy(flat, flat, sem).wait()

        base = pl.multiple_of(step * (BLOCK * QKV_BLOCKS), TILE)
        rows_to_matrix(flat, base, BLOCK, QKV_BLOCKS, wide, qkv)

    return pl.pallas_call(
        kernel,
        name="first_weights",
        grid=(STEPS,),
        in_specs=[pl.BlockSpec(memory_space=pltpu.SMEM)]
        + [pl.BlockSpec(memory_space=pl.ANY)] * (len(arrays) + 1),
        out_specs=pl.BlockSpec((BLOCK, 3 * D), lambda i: (i, 0)),
        out_shape=jax.ShapeDtypeStruct((D, 3 * D), BF),
        scratch_shapes=[
            pltpu.VMEM((length, LANES), BF),
            pltpu.VMEM((BLOCK * QKV_BLOCKS, LANES), F32),
            pltpu.SemaphoreType.DMA,
        ],
        compiler_params=pltpu.CompilerParams(vmem_limit_bytes=VMEM_LIMIT),
    )(place, *arrays, leftover)


def other_weights(layout, place, gathered):
    origin = layout.group_start(layout.first)
    length = layout.start(layout.devices) - origin
    padded = max(length, ROW_DOWN - origin + STEPS * DOWN_BLOCK * D_BLOCKS)
    up_length = BLOCK // UP_GROUP * UP_STRIDE
    arrays = flat_of(gathered)

    def kernel(place_ref, *refs):
        sources = refs[: len(arrays)]
        out_w, up_w, down_w, flat, wide, square, sem = refs[len(arrays) :]
        step = pl.program_id(0)

        @pl.when(step == 0)
        def _():
            named = [(ref, entry) for ref, (_, entry) in zip(sources, gathered)]
            fetch(layout, place_ref, (layout.first, layout.columns), origin, named, flat, sem)
            whole = flat.at[pl.ds(0, length), :]
            pltpu.make_async_copy(whole, whole, sem).wait()

        base = pl.multiple_of(ROW_OUT - origin + step * (BLOCK * D_BLOCKS), TILE)
        rows_to_matrix(flat, base, BLOCK, D_BLOCKS, wide, out_w)
        base = pl.multiple_of(ROW_UP - origin + step * up_length, TILE)
        rows_to_up(flat, base, wide, square, up_w)
        base = pl.multiple_of(ROW_DOWN - origin + step * (DOWN_BLOCK * D_BLOCKS), TILE)
        rows_to_matrix(flat, base, DOWN_BLOCK, D_BLOCKS, wide, down_w)

    return pl.pallas_call(
        kernel,
        name="other_weights",
        grid=(STEPS,),
        in_specs=[pl.BlockSpec(memory_space=pltpu.SMEM)]
        + [pl.BlockSpec(memory_space=pl.ANY)] * len(arrays),
        out_specs=[
            pl.BlockSpec((BLOCK, D), lambda i: (i, 0)),
            pl.BlockSpec((BLOCK, FF), lambda i: (i, 0)),
            pl.BlockSpec((DOWN_BLOCK, D), lambda i: (i, 0)),
        ],
        out_shape=[
            jax.ShapeDtypeStruct((D, D), BF),
            jax.ShapeDtypeStruct((D, FF), BF),
            jax.ShapeDtypeStruct((FF, D), BF),
        ],
        scratch_shapes=[
            pltpu.VMEM((padded, LANES), BF),
            pltpu.VMEM((max(up_length + 8, DOWN_BLOCK * D_BLOCKS), LANES), F32),
            pltpu.VMEM((UP_BLOCKS, BLOCK, LANES), F32),
            pltpu.SemaphoreType.DMA,
        ],
        compiler_params=pltpu.CompilerParams(vmem_limit_bytes=VMEM_LIMIT),
    )(place, *arrays)


MATRICES = {
    "qkv": (ROW_QKV, BLOCK, BLOCK * QKV_BLOCKS, 3 * D),
    "out": (ROW_OUT, BLOCK, BLOCK * D_BLOCKS, D),
    "up": (ROW_UP, BLOCK, BLOCK // UP_GROUP * UP_STRIDE, FF),
    "down": (ROW_DOWN, DOWN_BLOCK, DOWN_BLOCK * D_BLOCKS, D),
}


def gradient_pieces(layout, place, groups, matrices, leftover=False):
    low, high = layout.group_start(groups[0]), layout.group_end(groups[1])
    count = groups[1] - groups[0]
    names = list(matrices)
    plan = {}
    for name in names:
        first, _, stride, _ = MATRICES[name]
        blocks = [
            block
            for block in range(STEPS)
            if leftover
            or (first + block * stride < high and first + (block + 1) * stride > low)
        ]
        plan[name] = (first, blocks[0], len(blocks), stride)
    origin = min([low] + [first + b * stride for first, b, _, stride in plan.values()])
    end = max([high] + [first + (b + n) * stride for first, b, n, stride in plan.values()])
    steps = max(n for _, _, n, _ in plan.values())
    covered = min(first + b * stride for first, b, _, stride in plan.values())
    rows = layout.devices * count * layout.piece
    extra = ROW_OUT - layout.group_start(layout.first)

    def kernel(place_ref, *refs):
        inputs, refs = (refs[: len(names)], refs[len(names) :])
        outputs, (flat, wide, square, sem) = (refs[:-4], refs[-4:])
        step = pl.program_id(0)
        if covered > low:

            @pl.when(step == 0)
            def _():
                flat[pl.ds(low - origin, covered - low), :] = jnp.zeros((covered - low, LANES), BF)

        for ref, name in zip(inputs, names):
            first, block, number, stride = plan[name]

            def convert(ref=ref, name=name, first=first, block=block, stride=stride):
                base = pl.multiple_of(first - origin + (block + step) * stride, TILE)
                if name == "up":
                    up_to_rows(ref, square, wide, flat, base)
                else:
                    blocks = QKV_BLOCKS if name == "qkv" else D_BLOCKS
                    matrix_to_rows(ref, stride // blocks, blocks, wide, flat, base)

            if number == steps:
                convert()
            else:
                pl.when(step < number)(convert)

        @pl.when(step == steps - 1)
        def _():
            if "down" in names:
                tail = end - ROW_VEC
                flat[pl.ds(ROW_VEC - origin, tail), :] = jnp.zeros((tail, LANES), BF)

            def body(index, _):
                group = groups[0] + index % count
                key = index // count
                row = jnp.bitwise_xor(place_ref[2], key % layout.ctx)
                key = key // layout.ctx
                column = jnp.bitwise_xor(place_ref[0], key % layout.columns)
                core = jnp.bitwise_xor(place_ref[1], key // layout.columns)
                shard = group * layout.group_shards + core * layout.ctx + row
                start = shard * layout.rows // TILE * TILE
                source = pl.multiple_of(start + column * layout.piece - origin, TILE)
                target = pl.multiple_of(index * layout.piece, TILE)
                pltpu.make_async_copy(
                    flat.at[pl.ds(source, layout.piece), :],
                    outputs[0].at[pl.ds(target, layout.piece), :],
                    sem,
                ).start()
                return 0

            lax.fori_loop(0, layout.devices * count, body, 0)
            pltpu.make_async_copy(outputs[0], outputs[0], sem).wait()
            if leftover:
                copy = pltpu.make_async_copy(
                    flat.at[pl.ds(ROW_OUT - extra - origin, extra), :], outputs[1], sem
                )
                copy.start()
                copy.wait()

    def spec(name):
        _, block, number, _ = plan[name]
        _, height, _, width = MATRICES[name]
        return pl.BlockSpec(
            (height, width), lambda i: (block + jnp.minimum(i, number - 1), 0)
        )

    shapes = [jax.ShapeDtypeStruct((rows, LANES), BF)]
    if leftover:
        shapes.append(jax.ShapeDtypeStruct((extra, LANES), BF))
    wide_rows = max(stride for _, _, _, stride in plan.values())
    return pl.pallas_call(
        kernel,
        name="pieces_" + "_".join(names),
        grid=(steps,),
        in_specs=[pl.BlockSpec(memory_space=pltpu.SMEM)] + [spec(name) for name in names],
        out_specs=[pl.BlockSpec(memory_space=pl.ANY)] * len(shapes),
        out_shape=shapes,
        scratch_shapes=[
            pltpu.VMEM((end - origin, LANES), BF),
            pltpu.VMEM((wide_rows, LANES), F32),
            pltpu.VMEM((UP_BLOCKS if "up" in names else 1, BLOCK, LANES), F32),
            pltpu.SemaphoreType.DMA,
        ],
        compiler_params=pltpu.CompilerParams(vmem_limit_bytes=VMEM_LIMIT),
    )(place, *[matrices[name] for name in names])


def dot_t(left, right):
    return lax.dot_general(left, right, (((1,), (1,)), ((), ())), preferred_element_type=F32)


def t_dot(left, right):
    return lax.dot_general(left, right, (((0,), (0,)), ((), ())), preferred_element_type=F32)


def dense(left, right):
    return jnp.dot(left, right, preferred_element_type=F32)


def masked(scores, count):
    columns = lax.broadcasted_iota(jnp.int32, scores.shape, 1)
    return jnp.where(columns < count, scores, masked_score)


def unpack_heads(source, parts, heads, held):
    for part in range(parts):
        for head in range(heads):
            first = (part * heads + head) * HD
            held[part, head] = source[:, first : first + HD]


def attend(counts, packed, chunk):
    length, width = packed.shape
    heads = width // (3 * HD)

    def kernel(count, source, mixed, log_total, held, made):
        head = pl.program_id(0)

        @pl.when(head == 0)
        def _():
            unpack_heads(source, 3, heads, held)

        for first in range(0, length, chunk):
            queries = held[0, head, pl.ds(first, chunk), :]
            scores = masked(dot_t(queries, held[1, head]), count[0])
            top = jnp.max(scores, -1, keepdims=True)
            exponent = jnp.exp(scores - top)
            total = jnp.sum(exponent, -1, keepdims=True)
            probs = (exponent / total).astype(BF)
            made[head, pl.ds(first, chunk), :] = dense(probs, held[2, head]).astype(BF)
            log_total[0, first : first + chunk, :] = top + jnp.log(total)

        @pl.when(head == heads - 1)
        def _():
            mixed[...] = jnp.concatenate([made[index] for index in range(heads)], -1)

    return pl.pallas_call(
        kernel,
        name="attend",
        grid=(heads,),
        in_specs=[
            pl.BlockSpec(memory_space=pltpu.SMEM),
            pl.BlockSpec((length, width), lambda h: (0, 0)),
        ],
        out_specs=[
            pl.BlockSpec((length, heads * HD), lambda h: (0, 0)),
            pl.BlockSpec((1, length, 1), lambda h: (h, 0, 0)),
        ],
        out_shape=[
            jax.ShapeDtypeStruct((length, heads * HD), BF),
            jax.ShapeDtypeStruct((heads, length, 1), F32),
        ],
        scratch_shapes=[
            pltpu.VMEM((3, heads, length, HD), BF),
            pltpu.VMEM((heads, length, HD), BF),
        ],
        compiler_params=pltpu.CompilerParams(vmem_limit_bytes=VMEM_LIMIT),
    )(counts, packed)


def attend_back(counts, packed, log_total, grad_mixed, chunk):
    length, width = packed.shape
    heads = width // (3 * HD)
    scale = HD ** (-0.5)

    def kernel(count, source, logs, grad_source, made, sums, held, grad, results, acc_k, acc_v):
        head = pl.program_id(0)

        @pl.when(head == 0)
        def _():
            unpack_heads(source, 3, heads, held)
            unpack_heads(grad_source, 1, heads, grad)

        acc_k[...] = jnp.zeros_like(acc_k)
        acc_v[...] = jnp.zeros_like(acc_v)
        total_q = jnp.zeros((1, HD), F32)
        for first in range(0, length, chunk):
            part = pl.ds(first, chunk)
            queries = held[0, head, part, :]
            scores = masked(dot_t(queries, held[1, head]), count[0])
            probs = jnp.exp(scores - logs[0, part, :])
            grad_heads = grad[0, head, part, :]
            grad_probs = dot_t(grad_heads, held[2, head])
            delta = jnp.sum(probs * grad_probs, -1, keepdims=True)
            grad_scores = (probs * (grad_probs - delta)).astype(BF)
            grad_query = dense(grad_scores, held[1, head]) * scale
            total_q = total_q + jnp.sum(grad_query, 0, keepdims=True)
            results[0, head, part, :] = grad_query.astype(BF)
            acc_k[...] += t_dot(grad_scores, queries)
            acc_v[...] += t_dot(probs.astype(BF), grad_heads)
        results[1, head] = acc_k[...].astype(BF)
        results[2, head] = acc_v[...].astype(BF)
        sums[0, 0:1, :] = total_q
        sums[0, 1:2, :] = jnp.sum(acc_v[...], 0, keepdims=True)

        @pl.when(head == heads - 1)
        def _():
            made[...] = jnp.concatenate(
                [results[part, index] for part in range(3) for index in range(heads)], -1
            )

    return pl.pallas_call(
        kernel,
        name="attend_back",
        grid=(heads,),
        in_specs=[
            pl.BlockSpec(memory_space=pltpu.SMEM),
            pl.BlockSpec((length, width), lambda h: (0, 0)),
            pl.BlockSpec((1, length, 1), lambda h: (h, 0, 0)),
            pl.BlockSpec((length, heads * HD), lambda h: (0, 0)),
        ],
        out_specs=[
            pl.BlockSpec((length, width), lambda h: (0, 0)),
            pl.BlockSpec((1, 2, HD), lambda h: (h, 0, 0)),
        ],
        out_shape=[
            jax.ShapeDtypeStruct((length, width), BF),
            jax.ShapeDtypeStruct((heads, 2, HD), F32),
        ],
        scratch_shapes=[
            pltpu.VMEM((3, heads, length, HD), BF),
            pltpu.VMEM((1, heads, length, HD), BF),
            pltpu.VMEM((3, heads, length, HD), BF),
            pltpu.VMEM((length, HD), F32),
            pltpu.VMEM((length, HD), F32),
        ],
        compiler_params=pltpu.CompilerParams(vmem_limit_bytes=VMEM_LIMIT),
    )(counts, packed, log_total, grad_mixed)


def norm_forward(residual):
    centre = residual - jnp.mean(residual, -1, keepdims=True)
    inverse = lax.rsqrt(jnp.mean(centre * centre, -1, keepdims=True) + norm_epsilon)
    return (centre * inverse, inverse)


def norm_back(grad_normed, unit, inverse, gain):
    scaled = grad_normed * gain
    return inverse * (
        scaled
        - jnp.mean(scaled, -1, keepdims=True)
        - unit * jnp.mean(scaled * unit, -1, keepdims=True)
    )


def adam_update(master, grads, first, second, index):
    matrix_part = index < 4 * D * D + 2 * D * FF
    first_new = beta_one * first + (1.0 - beta_one) * grads
    second_new = beta_two * second + (1.0 - beta_two) * grads * grads
    first_hat = first_new / (1.0 - beta_one**adam_step)
    second_hat = second_new / (1.0 - beta_two**adam_step)
    rate = jnp.where(matrix_part, rate_matrix, rate_vector)
    decay = jnp.where(matrix_part, weight_decay, 0.0)
    updated = master - rate * (first_hat / (jnp.sqrt(second_hat) + adam_epsilon) + decay * master)
    return (updated, first_new, second_new)


def to_heads(array, parts):
    ctx = lax.axis_size("ctx")
    rows = array.shape[0]
    split = array.reshape(rows, parts, ctx, D // ctx).transpose(2, 0, 1, 3)
    split = split.reshape(ctx, rows, parts * D // ctx)
    held = lax.all_to_all(split, "ctx", split_axis=0, concat_axis=0, tiled=True)
    return held.reshape(rows * ctx, parts * D // ctx)


def from_heads(array, parts):
    ctx = lax.axis_size("ctx")
    length = array.shape[0]
    split = array.reshape(ctx, length // ctx, parts * D // ctx)
    held = lax.all_to_all(split, "ctx", split_axis=0, concat_axis=0, tiled=True)
    held = held.reshape(ctx, length // ctx, parts, D // ctx)
    return held.transpose(1, 2, 0, 3).reshape(length // ctx, parts * D)


def exchange(array, axis, bit):
    size = lax.axis_size(axis)
    return lax.ppermute(array, axis, [(index, index ^ bit) for index in range(size)])


def add(*arrays):
    return functools.reduce(jnp.add, [array.astype(F32) for array in arrays]).astype(BF)


def gather(layout, share):
    held = {0: share}
    bit = layout.ctx // 2
    while bit:
        held.update({key ^ bit: exchange(held[key], "ctx", bit) for key in list(held)})
        bit //= 2
    stack = jnp.concatenate([held[key] for key in range(layout.ctx)])
    arrays = [(stack, (0, 0, 0, layout.ctx))]
    if layout.columns == 4:
        middle, half = (stack.shape[0] // 2, layout.ctx // 2)
        by_x, by_y = (exchange(stack, "dp", 2), exchange(stack, "dp", 4))
        arrays += [(by_x, (1, 0, 0, layout.ctx)), (by_y, (2, 0, 0, layout.ctx))]
        arrays.append((exchange(by_x[:middle], "dp", 4), (3, 0, 0, half)))
        arrays.append((exchange(by_y[middle:], "dp", 2), (3, 0, half, half)))
    else:
        bit = 1
        while bit < layout.columns:
            arrays += [
                (exchange(array, "dp", 2 * bit), (place[0] ^ bit,) + place[1:])
                for array, place in arrays
            ]
            bit *= 2
    arrays += [
        (exchange(array, "dp", 1), (place[0], 1) + place[2:]) for array, place in arrays
    ]
    return arrays, stack


def scatter(layout, pieces):
    middle = pieces.shape[0] // 2
    kept = add(pieces[:middle], exchange(pieces[middle:], "dp", 1))
    size = middle // layout.columns
    parts = [kept[index * size : (index + 1) * size] for index in range(layout.columns)]
    if layout.columns == 4:
        half = size // 2
        low = add(parts[1][:half], exchange(parts[3][:half], "dp", 4))
        high = add(parts[2][half:], exchange(parts[3][half:], "dp", 2))
        halves = [
            add(parts[0][:half], exchange(low, "dp", 2), exchange(parts[2][:half], "dp", 4)),
            add(parts[0][half:], exchange(parts[1][half:], "dp", 2), exchange(high, "dp", 4)),
        ]
        summed = halves
    else:
        bit = layout.columns // 2
        while bit:
            parts = [
                add(parts[index], exchange(parts[index ^ bit], "dp", 2 * bit))
                for index in range(bit)
            ]
            bit //= 2
        half = size // 2
        summed = [parts[0][:half], parts[0][half:]]
    each = layout.ctx // 2
    length = size // layout.ctx
    held = {
        key: summed[key // each][(key % each) * length : (key % each + 1) * length]
        for key in range(layout.ctx)
    }
    bit = 1
    while bit < layout.ctx:
        for key in [key for key in held if key & bit]:
            held[key ^ bit] = add(held[key ^ bit], exchange(held.pop(key), "ctx", bit))
        bit *= 2
    return held[0]


def bits(layout):
    found = []
    for axis, size, unit in (("ctx", layout.ctx, 1), ("dp", layout.dp, layout.ctx)):
        bit = 1
        while bit < size:
            found.append((axis, bit, bit * unit))
            bit *= 2
    return found


def column_groups(layout):
    return [[column * 2 + core for column in range(layout.columns)] for core in range(2)]


def spread_weights(layout, flat, shard, everyone):
    last = layout.devices - 1
    before = lax.ppermute(
        flat[-TILE:], ("dp", "ctx"), [(index, index + 1) for index in range(last)]
    )
    length = layout.columns * layout.piece
    padded = jnp.concatenate([before, flat, jnp.zeros((length - layout.rows, LANES), BF)])
    offset = (shard * layout.rows) % TILE
    chunk = lax.dynamic_slice(padded, (TILE - offset, 0), (length, LANES))
    pieces = chunk.reshape(layout.columns, layout.piece, LANES)
    held = lax.all_to_all(
        pieces, "dp", split_axis=0, concat_axis=0, tiled=True, axis_index_groups=everyone
    )
    return chunk, held


def broadcast(layout, shard, sources):
    held = jnp.concatenate([rows for _, rows in sources])
    owner = jnp.concatenate(
        [jnp.full((rows.shape[0], 1), source, jnp.int32) for source, rows in sources]
    )
    for axis, bit, unit in bits(layout):
        other = exchange(held, axis, bit)
        held = jnp.where(((owner ^ shard) & unit) == 0, held, other)
    return held


def shards(layout, inputs, counts, params, first_moment, second_moment, out_cotangent):
    local_rows = inputs.shape[1]
    shard = lax.axis_index(("dp", "ctx"))
    score_scale = HD ** (-0.5)
    everyone = column_groups(layout)
    chunk = 256

    place = jnp.stack(
        [lax.axis_index("dp") // 2, lax.axis_index("dp") % 2, lax.axis_index("ctx")]
    ).astype(jnp.int32)
    padding = -layout.rows % 8 * LANES
    flat = jnp.pad(params[0].astype(BF), (0, padding)).reshape(-1, LANES)[: layout.rows]
    chunk_rows, pieces = spread_weights(layout, flat, shard, everyone)
    shared_first = pieces[: layout.first].reshape(-1, LANES)
    gathered_first, stack = gather(layout, shared_first)
    shared_rest = pieces[layout.first :].reshape(-1, LANES)
    shared_rest = lax.optimization_barrier((shared_rest, stack))[0]
    gathered_rest, _ = gather(layout, shared_rest)
    vector_first = ROW_VEC - layout.start(layout.devices - 1)
    assert 0 <= vector_first and vector_first + VEC_ROWS <= layout.columns * layout.piece
    sources = [(owner, chunk_rows[:rows]) for owner, rows in layout.leftover()]
    sources.append((layout.devices - 1, chunk_rows[vector_first : vector_first + VEC_ROWS]))
    spread = broadcast(layout, shard, sources)
    leftover = spread[:-VEC_ROWS]
    flat_vectors = spread[-VEC_ROWS:].reshape(-1).astype(F32)
    vectors = []
    offset = 0
    for length in VEC_LENGTHS:
        vectors.append(flat_vectors[offset : offset + length])
        offset += length
    (
        gain_one,
        shift_one,
        bias_query,
        bias_value,
        bias_out,
        gain_two,
        shift_two,
        bias_down,
        bias_up,
    ) = vectors

    residual = inputs[0].astype(F32)
    unit_one, inverse_one = norm_forward(residual)
    normed_round = (unit_one * gain_one + shift_one).astype(BF)
    qkv_weight = first_weights(layout, place, gathered_first, leftover)
    projected = dense(normed_round, qkv_weight)
    queries = ((projected[:, :D] + bias_query) * score_scale).astype(BF)
    keys = projected[:, D : 2 * D].astype(BF)
    values = (projected[:, 2 * D :] + bias_value).astype(BF)
    packed = to_heads(jnp.concatenate([queries, keys, values], -1), 3)
    out_weight, up_weight, down_weight = other_weights(layout, place, gathered_rest)
    mixed_heads, log_total = attend(counts, packed, chunk)
    mixed = from_heads(mixed_heads, 1)
    middle = residual + dense(mixed, out_weight) + bias_out
    unit_two, inverse_two = norm_forward(middle)
    normed_two_round = (unit_two * gain_two + shift_two).astype(BF)
    pre_gelu = dense(normed_two_round, up_weight) + bias_up
    activated = jax.nn.gelu(pre_gelu, approximate=True).astype(BF)
    output = (middle + dense(activated, down_weight) + bias_down).astype(BF)

    positions = lax.axis_index("ctx") * local_rows + jnp.arange(local_rows, dtype=jnp.int32)
    row_valid = (positions < counts[0])[:, None].astype(F32)
    grad_next = out_cotangent[0] * row_valid
    grad_bias_down = jnp.sum(grad_next, 0)
    grad_round = grad_next.astype(BF)
    grad_down = t_dot(activated, grad_round).astype(BF)
    grad_act = dot_t(grad_round, down_weight)
    gelu_back = jax.vjp(functools.partial(jax.nn.gelu, approximate=True), pre_gelu)[1]
    grad_pre = gelu_back(grad_act)[0]
    grad_bias_up = jnp.sum(grad_pre, 0)
    grad_pre_round = grad_pre.astype(BF)
    grad_up = t_dot(normed_two_round, grad_pre_round).astype(BF)
    middle_group = layout.columns // 2
    (terms,) = gradient_pieces(
        layout, place, (middle_group, layout.columns), {"up": grad_up, "down": grad_down}
    )
    sum_last = scatter(layout, terms)
    grad_normed_two = dot_t(grad_pre_round, up_weight)
    grad_gain_two = jnp.sum(grad_normed_two * unit_two, 0)
    grad_shift_two = jnp.sum(grad_normed_two, 0)
    grad_middle = grad_next + norm_back(grad_normed_two, unit_two, inverse_two, gain_two)
    grad_bias_out = jnp.sum(grad_middle, 0)
    middle_round = grad_middle.astype(BF)
    grad_out = t_dot(mixed, middle_round).astype(BF)
    grad_mixed = dot_t(middle_round, out_weight).astype(BF)
    grad_mixed_heads = to_heads(grad_mixed, 1)
    (terms,) = gradient_pieces(
        layout, place, (layout.first, middle_group), {"out": grad_out, "up": grad_up}
    )
    sum_middle = scatter(layout, terms)
    grad_packed, sums = attend_back(counts, packed, log_total, grad_mixed_heads, chunk)
    grad_projected = from_heads(grad_packed, 3)
    grad_qkv = t_dot(normed_round, grad_projected).astype(BF)
    terms, leftover_terms = gradient_pieces(
        layout, place, (0, layout.first), {"qkv": grad_qkv}, leftover=True
    )
    sum_first = scatter(layout, terms)
    grad_normed_one = dot_t(grad_projected, qkv_weight)
    grad_gain_one = jnp.sum(grad_normed_one * unit_one, 0)
    grad_shift_one = jnp.sum(grad_normed_one, 0)
    input_grad = grad_middle + norm_back(grad_normed_one, unit_one, inverse_one, gain_one)

    share = D // layout.ctx
    where = (lax.axis_index("ctx") * share,)
    sum_q, sum_v = (sums[:, 0].reshape(-1), sums[:, 1].reshape(-1))
    grad_bias_query = lax.dynamic_update_slice(jnp.zeros((D,), F32), sum_q, where)
    grad_bias_value = lax.dynamic_update_slice(jnp.zeros((D,), F32), sum_v, where)
    vector_terms = [
        grad_gain_one,
        grad_shift_one,
        grad_bias_query,
        grad_bias_value,
        grad_bias_out,
        grad_gain_two,
        grad_shift_two,
        grad_bias_down,
        grad_bias_up,
    ]
    padding = jnp.zeros((VEC_ROWS * LANES - sum(VEC_LENGTHS),), F32)
    vector_grads = jnp.concatenate(vector_terms + [padding]).reshape(VEC_ROWS, LANES)
    for axis, bit, _ in bits(layout):
        vector_grads = vector_grads + exchange(vector_grads, axis, bit)
    for axis, bit, _ in bits(layout):
        leftover_terms = add(leftover_terms, exchange(leftover_terms, axis, bit))

    summed = jnp.concatenate([sum_first, sum_middle, sum_last])
    held = lax.all_to_all(
        summed.reshape(layout.columns, layout.piece, LANES),
        "dp",
        split_axis=0,
        concat_axis=0,
        tiled=True,
        axis_index_groups=everyone,
    )
    chunk_sum = held.reshape(-1, LANES).astype(F32)
    extra = jnp.zeros_like(chunk_sum)
    used = 0
    for owner, rows in layout.leftover():
        placed = jnp.pad(
            leftover_terms[used : used + rows].astype(F32), ((0, chunk_sum.shape[0] - rows), (0, 0))
        )
        extra = jnp.where(shard == owner, placed, extra)
        used += rows
    after = chunk_sum.shape[0] - vector_first - VEC_ROWS
    placed = jnp.pad(vector_grads, ((vector_first, after), (0, 0)))
    chunk_sum = chunk_sum + jnp.where(shard == layout.devices - 1, placed, extra)
    offset = (shard * layout.rows) % TILE
    rows = lax.dynamic_slice(chunk_sum, (offset, 0), (layout.rows, LANES))
    param_grads = rows.reshape(params.shape)
    index = (shard * params.shape[1] + jnp.arange(params.shape[1], dtype=jnp.int32))[None, :]
    new_params, new_first, new_second = adam_update(
        params, param_grads, first_moment, second_moment, index
    )
    return (output[None], input_grad[None], param_grads, new_params, new_first, new_second)


def solution(mesh):
    placed = (
        P("dp", "ctx", None),
        P("dp"),
        P(None, ("dp", "ctx")),
        P(None, ("dp", "ctx")),
        P(None, ("dp", "ctx")),
        P("dp", "ctx", None),
    )
    dp, ctx = (mesh.shape["dp"], mesh.shape["ctx"])

    def program(inputs, counts, params, first_moment, second_moment, out_cotangent):
        layout = Layout(dp, ctx, params.shape[1] // (dp * ctx))
        return jax.shard_map(
            functools.partial(shards, layout),
            mesh=mesh,
            in_specs=placed,
            out_specs=(
                P("dp", "ctx", None),
                P("dp", "ctx", None),
                P(None, ("dp", "ctx")),
                P(None, ("dp", "ctx")),
                P(None, ("dp", "ctx")),
                P(None, ("dp", "ctx")),
            ),
            check_vma=False,
        )(inputs, counts, params, first_moment, second_moment, out_cotangent)

    return program
```

time: 892 us -> 734 us (0.82)
  waiting for transfers between devices: 512 us -> 318 us
  starting transfers between devices: 26.1 us -> 96 us
  blocking collectives: 34.3 us -> 0 us
  other arithmetic: 55.7 us -> 70.6 us
  Pallas kernels: 95.5 us -> 109 us
  between operations: 15.6 us -> 2.97 us
  matrix products: 86 us -> 76.3 us
  local copies, waits for them, and re-layouts: 57.4 us -> 47.9 us
    ppermute x5 -> x69, waiting for transfers between devices: 14.3 us -> 288 us  [exchange(): lax.ppermute(array, axis, [(index, index ^ bit) for index in range(size)])]
    reduce_scatter x4 -> x0, waiting for transfers between devices: 173 us -> none  [the longest x2 108 us: scatter_half(): partial = lax.psum_scatter(pieces, 'dp', scatter_dimension=0, tiled=True)]
    psum x1 -> x0, waiting for transfers between devices: 109 us -> none  [shards(): lax.psum(jnp.concatenate(vector_terms + [padding]), ('dp', 'ctx'))]
    all_gather x2 -> x0, waiting for transfers between devices: 108 us -> none  [the longest x1 88.1 us: shards(): half_one = lax.all_gather(share_one, ('dp', 'ctx'), axis=0, tiled=True)]
    ppermute x5 -> x69, starting transfers between devices: 5.54 us -> 67.8 us  [exchange(): lax.ppermute(array, axis, [(index, index ^ bit) for index in range(size)])]
    all_to_all x1 -> x2, waiting for transfers between devices: 61.1 us -> 15.6 us  [to_heads(): held = lax.all_to_all(split, 'ctx', split_axis=0, concat_axis=0, tiled=True)]
    all_to_all x2 -> x0, blocking collectives: 34.3 us -> none  [the longest x1 19.2 us: to_heads(): held = lax.all_to_all(split, 'ctx', split_axis=0, concat_axis=0, tiled=True)]
    all_to_all x2, waiting for transfers between devices: 36.7 us -> 4.46 us  [from_heads(): held = lax.all_to_all(split, 'ctx', split_axis=0, concat_axis=0, tiled=True)]
  transfers between devices with their start and end apart: 17 -> 76, of which waited for: 14 -> 37; matrix products, arithmetic and copies ran while one was open for 14% -> 18% of each run, Pallas kernels for 9% -> 12%
where the time goes in v1:
time: 734 us; the launch traced here: 721 us
  waiting for transfers between devices  318 us (43%)
  Pallas kernels  109 us (15%)
  starting transfers between devices  96 us (13%)
  matrix products  76.3 us (10%)
  other arithmetic  70.6 us (10%)
  local copies, waits for them, and re-layouts  47.9 us (7%)
    ppermute x69, waiting for transfers between devices, exchange(): lax.ppermute(array, axis, [(index, index ^ bit) for index in range(size)])  288 us
    ppermute x69, starting transfers between devices, exchange(): lax.ppermute(array, axis, [(index, index ^ bit) for index in range(size)])  67.8 us
    pallas_call x3, Pallas kernels, gradient_pieces(): pl.pallas_call(kernel, name='pieces_' + '_'.join(names), grid=(steps,), i...  39.4 us
    dot_general x4, matrix products, dense(): return jnp.dot(left, right, preferred_element_type=F32)  28.6 us
    dot_general x4, matrix products, t_dot(): lax.dot_general(left, right, (((0,), (0,)), ((), ())), preferred_element_...  24 us
    dot_general x4, matrix products, dot_t(): lax.dot_general(left, right, (((1,), (1,)), ((), ())), preferred_element_...  23.7 us
    convert_element_type x2, other arithmetic, shards(): params[0].astype(BF)  23.1 us
    pallas_call x1, Pallas kernels, attend_back(): pl.pallas_call(kernel, name='attend_back', grid=(heads,), in_specs=[pl.Bl...  22.6 us
  transfers between devices with their start and end apart: 76, of which 37 were waited for; matrix products, arithmetic and copies ran while one was open for 18% of the time, Pallas kernels for 12%

profile of v1, /device:TPU:1, one launch (start us, length us, event | category | flops | bytes accessed | tf_op | source)
XLA Modules:
  0.0 720.8 jit_solution(11926662936262211881)
XLA Ops:
  8.0 19.8 %convert_reduce_fusion.1 = bf16[476288]{0:T(1024)(128)(2,1)S(1)} fusion(f32[1,476288]{1,0:T(1,128)S(1)} %copy-done), kind=kLoop, calls=%fused_computation.171 | loop fusion | flops 476288 | bytes 2857728 | tf_op jit(solution)/shard_map/convert_element_type | solution.py:717
  51.7 11.8 %collective-permute-done.2 = bf16[1472,128]{1,0:T(8,128)(2,1)S(1)} collective-permute-done((bf16[1472,128]{1,0:T(8,128)(2,1)S(1)}, bf16[1472,128]{1,0:T(8,128)(2,1)S(1)}, u32[]{:S(2)}, u32[]{:S(2)}) %collective-permute-start.2) | collective-permute-done | bytes 376864 | tf_op jit(solution)/shard_map/ppermute | solution.py:592
  90.1 25.8 %collective-permute-done.19 = bf16[2832,128]{1,0:T(8,128)(2,1)S(1)} collective-permute-done((bf16[2832,128]{1,0:T(8,128)(2,1)S(1)}, bf16[2832,128]{1,0:T(8,128)(2,1)S(1)}, u32[]{:S(2)}, u32[]{:S(2)}) %collective-permute-start.19) | collective-permute-done | bytes 725024 | tf_op jit(solution)/shard_map/ppermute | solution.py:592
  121.0 9.0 %collective-permute-done.12.refs_4_ = bf16[1888,128]{1,0:T(8,128)(2,1)S(1)} collective-permute-done((bf16[1888,128]{1,0:T(8,128)(2,1)S(1)}, bf16[1888,128]{1,0:T(8,128)(2,1)S(1)}, u32[]{:S(2)}, u32[]{:S(2)}) %collective-permute-start.12) | collective-permute-done | bytes 483360 | tf_op jit(solution)/shard_map/ppermute | solution.py:592
  142.0 10.2 %first_weights.1 = bf16[1152,3456]{1,0:T(8,128)(2,1)} custom-call(s32[3]{0:T(128)} %pad_add_fusion.place_ref, bf16[3776,128]{1,0:T(8,128)(2,1)} %copy-done.5, bf16[3776,128]{1,0:T(8,128)(2,1)} %copy-done.9, bf16[3776,128]{1,0:T(8,128)(2,1)} %copy-done.8, bf16[1888,128]{1,0:T(8,128)(2,1)} %copy-done.16, bf16[1888,128]{1,0:T(8,128)(2,1)} %copy-done.15, ...), custom_call_target="tpu_custom_call" | custom-call | tf_op jit(solution)/shard_map/first_weights/pallas_call | solution.py:217
  167.7 34.1 %collective-permute-done.22.refs_2_ = bf16[11328,128]{1,0:T(8,128)(2,1)} collective-permute-done((bf16[11328,128]{1,0:T(8,128)(2,1)}, bf16[11328,128]{1,0:T(8,128)(2,1)}, u32[]{:S(2)}, u32[]{:S(2)}) %collective-permute-start.22) | collective-permute-done | bytes 2900000 | tf_op jit(solution)/shard_map/ppermute | solution.py:592
  207.5 28.4 %collective-permute-done.24.refs_4_ = bf16[5664,128]{1,0:T(8,128)(2,1)} collective-permute-done((bf16[5664,128]{1,0:T(8,128)(2,1)S(1)}, bf16[5664,128]{1,0:T(8,128)(2,1)}, u32[]{:S(2)}, u32[]{:S(2)}) %collective-permute-start.24) | collective-permute-done | bytes 1450016 | tf_op jit(solution)/shard_map/ppermute | solution.py:592
  244.2 15.0 %attend.1 = (bf16[1024,288]{1,0:T(8,128)(2,1)}, f32[4,1024,1]{2,1,0:T(8,128)}) custom-call(s32[1]{0:T(128)} %copy.33.count, bf16[1024,864]{1,0:T(8,128)(2,1)} %bitcast.139), custom_call_target="tpu_custom_call" | custom-call | tf_op jit(solution)/shard_map/attend/pallas_call | solution.py:451
  266.0 22.3 %other_weights.1 = (bf16[1152,1152]{1,0:T(8,128)(2,1)}, bf16[1152,4304]{1,0:T(8,128)(2,1)}, bf16[4304,1152]{1,0:T(8,128)(2,1)}) custom-call(s32[3]{0:T(128)} %pad_add_fusion.place_ref, bf16[11328,128]{1,0:T(8,128)(2,1)} %constant_dynamic-update-slice_fusion.refs_0_, bf16[11328,128]{1,0:T(8,128)(2,1)} %collective-permute-done.21.refs_1_, ...), custom_call_target="tpu_custom_call" | custom-call | tf_op jit(solution)/shard_map/other_weights/pallas_call | solution.py:260
  291.5 10.6 %convolution_add_fusion = f32[256,4304]{0,1:T(8,128)} fusion(bf16[1152,4304]{1,0:T(8,128)(2,1)} %get-tuple-element.19, f32[4304]{0:T(1024)S(1)} %slice.370, f32[256,1152]{1,0:T(8,128)S(1)} %get-tuple-element.79, f32[1152]{0:T(1024)S(1)} %copy-done.22, f32[1152]{0:T(1024)S(1)} %get-tuple-element.65, f32[256]{0:T(256)S(1)} %add_rsqrt_fusion, ...), kind=kOutput, calls=%fused_computation.7 | convolution fusion | flops 2541178880 | bytes 15531840 | tf_op jit(solution)/shard_map/dot_general | solution.py:411
  302.1 10.2 %fusion.77 = (f32[4304]{0:T(1024)}, bf16[256,4304]{0,1:T(8,128)(2,1)S(1)}) fusion(f32[256,4304]{0,1:T(8,128)} %convolution_add_fusion, bf16[4304,1152]{1,0:T(8,128)(2,1)} %get-tuple-element.20, f32[1,256,1152]{2,1,0:T(8,128)S(1)} %copy-done.11, f32[256]{0:T(256)S(1)} %compare_convert_fusion), kind=kOutput, calls=%fused_computation.178 | convolution fusion | flops 2562326272 | bytes 17725248 | tf_op jit(solution)/shard_map/dot_general | solution.py:403
  326.6 15.6 %all-to-all-done.3 = bf16[4,256,288]{1,2,0:T(8,128)(2,1)} async-done(((bf16[4,256,288]{1,2,0:T(8,128)(2,1)}), bf16[4,256,288]{1,2,0:T(8,128)(2,1)}, u32[]{:S(2)}, u32[]{:S(2)}) %all-to-all-start.3) | async-done | bytes 589856 | tf_op jit(solution)/shard_map/all_to_all | solution.py:577
  344.4 22.6 %attend_back.1 = (bf16[1024,864]{1,0:T(8,128)(2,1)}, f32[4,2,72]{2,1,0:T(2,128)}) custom-call(s32[1]{0:T(128)} %copy.33.count, bf16[1024,864]{1,0:T(8,128)(2,1)} %bitcast.140, f32[4,1024,1]{2,1,0:T(8,128)} %get-tuple-element.21.logs, bf16[1024,288]{1,0:T(8,128)(2,1)} %bitcast.149), custom_call_target="tpu_custom_call" | custom-call | tf_op jit(solution)/shard_map/attend_back/pallas_call | solution.py:516
  383.4 12.0 %pieces_out_up.1 = bf16[30208,128]{1,0:T(8,128)(2,1)} custom-call(s32[3]{0:T(128)} %pad_add_fusion.place_ref, bf16[1152,1152]{1,0:T(8,128)(2,1)} %convolution_convert_fusion.3.refs_0_, bf16[1152,4304]{1,0:T(8,128)(2,1)} %convolution_convert_fusion.1.refs_1_.refs_0_), custom_call_target="tpu_custom_call" | custom-call | tf_op jit(solution)/shard_map/pieces_out_up/pallas_call | solution.py:385
  400.5 10.0 %convolution_convert_fusion.refs_1_ = bf16[4304,1152]{1,0:T(8,128)(2,1)} fusion(f32[1,256,1152]{2,1,0:T(8,128)S(1)} %copy-done.12, f32[256]{0:T(256)S(1)} %copy-done.42, f32[256,4304]{0,1:T(8,128)} %convolution_add_fusion), kind=kOutput, calls=%fused_computation | convolution fusion | flops 2554066944 | bytes 15504384 | tf_op jit(solution)/shard_map/dot_general | solution.py:407
  417.5 7.7 %fusion.32 = (f32[1152]{0:T(1024)S(1)}, f32[256]{0:T(256)S(1)}, f32[256]{0:T(256)S(1)}, f32[1152]{0:T(1024)S(1)}, f32[256,1152]{1,0:T(8,128)}) fusion(bf16[1,256,1152]{2,1,0:T(8,128)(2,1)S(1)} %copy-done.2, f32[256]{0:T(256)S(1)} %copy-done.32, f32[256]{0:T(256)S(1)} %copy-done.27, f32[1152]{0:T(1024)S(1)} %get-tuple-element.72, ...), kind=kOutput, calls=%fused_computation.60 | convolution fusion | flops 2041378048 | bytes 11519488 | tf_op jit(solution)/shard_map/dot_general | solution.py:403
  425.4 9.1 %fusion.9 = bf16[1,256,1152]{2,1,0:T(8,128)(2,1)} fusion(f32[256,1152]{1,0:T(8,128)S(1)} %get-tuple-element.79, bf16[4304,1152]{1,0:T(8,128)(2,1)} %get-tuple-element.20, f32[1152]{0:T(1024)S(1)} %copy-done.35, f32[256,4304]{0,1:T(8,128)} %convolution_add_fusion), kind=kOutput, calls=%fused_computation.26 | convolution fusion | flops 2549403648 | bytes 16097792 | tf_op jit(solution)/shard_map/dot_general | solution.py:411
  434.5 16.5 %pieces_up_down.1 = bf16[60416,128]{1,0:T(8,128)(2,1)} custom-call(s32[3]{0:T(128)} %pad_add_fusion.place_ref, bf16[1152,4304]{1,0:T(8,128)(2,1)} %convolution_convert_fusion.1.refs_1_.refs_0_, bf16[4304,1152]{1,0:T(8,128)(2,1)} %convolution_convert_fusion.refs_1_), custom_call_target="tpu_custom_call" | custom-call | tf_op jit(solution)/shard_map/pieces_up_down/pallas_call | solution.py:385
  451.0 6.9 slice.399
  472.0 10.9 %pieces_qkv.1 = (bf16[30208,128]{1,0:T(8,128)(2,1)}, bf16[1344,128]{1,0:T(8,128)(2,1)}) custom-call(s32[3]{0:T(128)} %pad_add_fusion.place_ref, bf16[1152,3456]{1,0:T(8,128)(2,1)} %convolution_convert_fusion.2.refs_0_), custom_call_target="tpu_custom_call" | custom-call | tf_op jit(solution)/shard_map/pieces_qkv/pallas_call | solution.py:385
  496.5 13.7 %collective-permute-done.66 = bf16[1344,128]{1,0:T(8,128)(2,1)S(1)} collective-permute-done((bf16[1344,128]{1,0:T(8,128)(2,1)S(1)}, bf16[1344,128]{1,0:T(8,128)(2,1)S(1)}, u32[]{:S(2)}, u32[]{:S(2)}) %collective-permute-start.66) | collective-permute-done | bytes 344096 | tf_op jit(solution)/shard_map/ppermute | solution.py:592
  533.2 19.5 %collective-permute-done.51 = bf16[3776,128]{1,0:T(8,128)(2,1)S(1)} collective-permute-done((bf16[3776,128]{1,0:T(8,128)(2,1)S(1)}, bf16[3776,128]{1,0:T(8,128)(2,1)S(1)}, u32[]{:S(2)}, u32[]{:S(2)}) %collective-permute-start.51) | collective-permute-done | bytes 966688 | tf_op jit(solution)/shard_map/ppermute | solution.py:592
  563.4 11.4 %collective-permute-done.32 = bf16[1888,128]{1,0:T(8,128)(2,1)S(1)} collective-permute-done((bf16[1888,128]{1,0:T(8,128)(2,1)S(1)}, bf16[1888,128]{1,0:T(8,128)(2,1)S(1)}, u32[]{:S(2)}, u32[]{:S(2)}) %collective-permute-start.32) | collective-permute-done | bytes 483360 | tf_op jit(solution)/shard_map/ppermute | solution.py:592
  577.3 6.5 collective-permute-done.53
  584.8 10.7 %collective-permute-done.52 = bf16[3776,128]{1,0:T(8,128)(2,1)S(1)} collective-permute-done((bf16[3776,128]{1,0:T(8,128)(2,1)S(1)}, bf16[3776,128]{1,0:T(8,128)(2,1)S(1)}, u32[]{:S(2)}, u32[]{:S(2)}) %collective-permute-start.52) | collective-permute-done | bytes 966688 | tf_op jit(solution)/shard_map/ppermute | solution.py:592
  597.2 8.6 %collective-permute-done.45 = bf16[1888,128]{1,0:T(8,128)(2,1)S(1)} collective-permute-done((bf16[1888,128]{1,0:T(8,128)(2,1)S(1)}, bf16[1888,128]{1,0:T(8,128)(2,1)S(1)}, u32[]{:S(2)}, u32[]{:S(2)}) %collective-permute-start.45) | collective-permute-done | bytes 483360 | tf_op jit(solution)/shard_map/ppermute | solution.py:592
  607.6 8.6 %collective-permute-done.35 = bf16[1888,128]{1,0:T(8,128)(2,1)S(1)} collective-permute-done((bf16[1888,128]{1,0:T(8,128)(2,1)S(1)}, bf16[1888,128]{1,0:T(8,128)(2,1)S(1)}, u32[]{:S(2)}, u32[]{:S(2)}) %collective-permute-start.35) | collective-permute-done | bytes 483360 | tf_op jit(solution)/shard_map/ppermute | solution.py:592
  617.9 19.0 %collective-permute-done.55 = bf16[3776,128]{1,0:T(8,128)(2,1)S(1)} collective-permute-done((bf16[3776,128]{1,0:T(8,128)(2,1)S(1)}, bf16[3776,128]{1,0:T(8,128)(2,1)S(1)}, u32[]{:S(2)}, u32[]{:S(2)}) %collective-permute-start.55) | collective-permute-done | bytes 966688 | tf_op jit(solution)/shard_map/ppermute | solution.py:592
  639.2 9.1 %collective-permute-done.38 = bf16[944,128]{1,0:T(8,128)(2,1)S(1)} collective-permute-done((bf16[944,128]{1,0:T(8,128)(2,1)S(1)}, bf16[944,128]{1,0:T(8,128)(2,1)S(1)}, u32[]{:S(2)}, u32[]{:S(2)}) %collective-permute-start.38) | collective-permute-done | bytes 241696 | tf_op jit(solution)/shard_map/ppermute | solution.py:592
  648.4 10.2 %collective-permute-done.58 = bf16[1888,128]{1,0:T(8,128)(2,1)S(1)} collective-permute-done((bf16[1888,128]{1,0:T(8,128)(2,1)S(1)}, bf16[1888,128]{1,0:T(8,128)(2,1)S(1)}, u32[]{:S(2)}, u32[]{:S(2)}) %collective-permute-start.58) | collective-permute-done | bytes 483360 | tf_op jit(solution)/shard_map/ppermute | solution.py:592
  668.1 19.5 %collective-permute-done.54 = bf16[1888,128]{1,0:T(8,128)(2,1)S(1)} collective-permute-done((bf16[1888,128]{1,0:T(8,128)(2,1)S(1)}, bf16[1888,128]{1,0:T(8,128)(2,1)S(1)}, u32[]{:S(2)}, u32[]{:S(2)}) %collective-permute-start.54) | collective-permute-done | bytes 483360 | tf_op jit(solution)/shard_map/ppermute | solution.py:592
  702.2 18.1 %fusion.15 = (f32[1,476288]{1,0:T(1,128)}, f32[1,476288]{1,0:T(1,128)}, f32[1,476288]{1,0:T(1,128)}, f32[1,476288]{1,0:T(1,128)}) fusion(f32[1,476288]{1,0:T(1,128)S(1)} %copy-done.1, s32[]{:T(128)S(6)} %mul.281, f32[1,476288]{1,0:T(1,128)S(1)} %copy-done.10, f32[1,476288]{1,0:T(1,128)} %param.10, f32[1,1,3721,128]{3,2,1,0:T(8,128)S(1)} %fusion.12), kind=kLoop, calls=%fused_computation.37 | loop fusion | flops 9049472 | bytes 15241220 | tf_op jit(solution)/shard_map/sub | solution.py:568
  (357 shorter events, 254.7 us)
Async XLA Ops:
  80.6 36.8 %collective-permute-start.10 = (bf16[3776,128]{1,0:T(8,128)(2,1)S(1)}, bf16[3776,128]{1,0:T(8,128)(2,1)S(1)}, u32[]{:S(2)}, u32[]{:S(2)}) collective-permute-start(bf16[3776,128]{1,0:T(8,128)(2,1)S(1)} %pad_maximum_fusion.1.refs_0_), channel_id=1, source_target_pairs={{0,16},{4,20},{8,24},{12,28},{16,0},{20,4},{24,8},{28,12},{1,17},{... | collective-permute-start | bytes 2899976 | tf_op jit(solution)/shard_map/ppermute | solution.py:592
  82.2 33.8 %collective-permute-start.19 = (bf16[2832,128]{1,0:T(8,128)(2,1)S(1)}, bf16[2832,128]{1,0:T(8,128)(2,1)S(1)}, u32[]{:S(2)}, u32[]{:S(2)}) collective-permute-start(bf16[2832,128]{1,0:T(8,128)(2,1)S(1)} %bitcast.150), channel_id=1, source_target_pairs={{0,2},{1,3},{2,0},{3,1},{4,6},{5,7},{6,4},{7,5},{8,10},{9,11},{10,... | collective-permute-start | bytes 2174984 | tf_op jit(solution)/shard_map/ppermute | solution.py:592
  84.8 32.6 %collective-permute-start.5 = (bf16[1472,128]{1,0:T(8,128)(2,1)S(1)}, bf16[1472,128]{1,0:T(8,128)(2,1)S(1)}, u32[]{:S(2)}, u32[]{:S(2)}) collective-permute-start(bf16[1472,128]{1,0:T(8,128)(2,1)S(1)} %broadcast_select_fusion.3), channel_id=1, source_target_pairs={{0,16},{4,20},{8,24},{12,28},{16,0},{20,4},{24,8},{28,12},{1,17},{... | collective-permute-start | bytes 1130504 | tf_op jit(solution)/shard_map/ppermute | solution.py:592
  85.7 33.5 %collective-permute-start.18 = (bf16[2832,128]{1,0:T(8,128)(2,1)S(1)}, bf16[2832,128]{1,0:T(8,128)(2,1)S(1)}, u32[]{:S(2)}, u32[]{:S(2)}) collective-permute-start(bf16[2832,128]{1,0:T(8,128)(2,1)S(1)} %bitcast.151), channel_id=1, source_target_pairs={{0,1},{1,0},{2,3},{3,2},{4,5},{5,4},{6,7},{7,6},{8,9},{9,8},{10,11... | collective-permute-start | bytes 2174984 | tf_op jit(solution)/shard_map/ppermute | solution.py:592
  88.0 32.1 %collective-permute-start.9 = (bf16[3776,128]{1,0:T(8,128)(2,1)S(1)}, bf16[3776,128]{1,0:T(8,128)(2,1)S(1)}, u32[]{:S(2)}, u32[]{:S(2)}) collective-permute-start(bf16[3776,128]{1,0:T(8,128)(2,1)S(1)} %pad_maximum_fusion.1.refs_0_), channel_id=1, source_target_pairs={{0,8},{4,12},{8,0},{12,4},{16,24},{20,28},{24,16},{28,20},{1,9},{5... | collective-permute-start | bytes 2899976 | tf_op jit(solution)/shard_map/ppermute | solution.py:592
  137.0 64.8 %collective-permute-start.22 = (bf16[11328,128]{1,0:T(8,128)(2,1)}, bf16[11328,128]{1,0:T(8,128)(2,1)}, u32[]{:S(2)}, u32[]{:S(2)}) collective-permute-start(bf16[11328,128]{1,0:T(8,128)(2,1)} %constant_dynamic-update-slice_fusion.refs_0_), channel_id=1, source_target_pairs={{0,16},{4,20},{8,24},{12,28},{16,0},{20,4},{24,8},{28,12},{1,17},{... | collective-permute-start | bytes 8699912 | tf_op jit(solution)/shard_map/ppermute | solution.py:592
  137.3 68.1 %collective-permute-start.21 = (bf16[11328,128]{1,0:T(8,128)(2,1)}, bf16[11328,128]{1,0:T(8,128)(2,1)}, u32[]{:S(2)}, u32[]{:S(2)}) collective-permute-start(bf16[11328,128]{1,0:T(8,128)(2,1)} %constant_dynamic-update-slice_fusion.refs_0_), channel_id=1, source_target_pairs={{0,8},{4,12},{8,0},{12,4},{16,24},{20,28},{24,16},{28,20},{1,9},{5... | collective-permute-start | bytes 8699912 | tf_op jit(solution)/shard_map/ppermute | solution.py:592
  163.7 78.3 %all-to-all-start.1 = ((bf16[4,256,864]{1,2,0:T(8,128)(2,1)}), bf16[4,256,864]{1,2,0:T(8,128)(2,1)S(1)}, u32[]{:S(2)}, u32[]{:S(2)}) async-start(bf16[4,256,864]{1,2,0:T(8,128)(2,1)} %bitcast.145), calls=%async_computation.1 | async-start | bytes 3538944 | tf_op jit(solution)/shard_map/all_to_all | solution.py:577
  167.5 98.5 %collective-permute-start.25 = (bf16[11328,128]{1,0:T(8,128)(2,1)}, bf16[11328,128]{1,0:T(8,128)(2,1)}, u32[]{:S(2)}, u32[]{:S(2)}) collective-permute-start(bf16[11328,128]{1,0:T(8,128)(2,1)} %constant_dynamic-update-slice_fusion.refs_0_), channel_id=1, source_target_pairs={{0,4},{4,0},{8,12},{12,8},{16,20},{20,16},{24,28},{28,24},{1,5},{5... | collective-permute-start | bytes 8699912 | tf_op jit(solution)/shard_map/ppermute | solution.py:592
  203.2 32.6 %collective-permute-start.24 = (bf16[5664,128]{1,0:T(8,128)(2,1)S(1)}, bf16[5664,128]{1,0:T(8,128)(2,1)}, u32[]{:S(2)}, u32[]{:S(2)}) collective-permute-start(bf16[5664,128]{1,0:T(8,128)(2,1)S(1)} %slice.366), channel_id=1, source_target_pairs={{0,8},{4,12},{8,0},{12,4},{16,24},{20,28},{24,16},{28,20},{1,9},{5... | collective-permute-start | bytes 4349960 | tf_op jit(solution)/shard_map/ppermute | solution.py:592
  204.3 61.7 %collective-permute-start.27 = (bf16[11328,128]{1,0:T(8,128)(2,1)}, bf16[11328,128]{1,0:T(8,128)(2,1)}, u32[]{:S(2)}, u32[]{:S(2)}) collective-permute-start(bf16[11328,128]{1,0:T(8,128)(2,1)} %collective-permute-done.22.refs_2_), channel_id=1, source_target_pairs={{0,4},{4,0},{8,12},{12,8},{16,20},{20,16},{24,28},{28,24},{1,5},{5... | collective-permute-start | bytes 8699912 | tf_op jit(solution)/shard_map/ppermute | solution.py:592
  206.9 59.1 %collective-permute-start.26 = (bf16[11328,128]{1,0:T(8,128)(2,1)}, bf16[11328,128]{1,0:T(8,128)(2,1)}, u32[]{:S(2)}, u32[]{:S(2)}) collective-permute-start(bf16[11328,128]{1,0:T(8,128)(2,1)} %collective-permute-done.21.refs_1_), channel_id=1, source_target_pairs={{0,4},{4,0},{8,12},{12,8},{16,20},{20,16},{24,28},{28,24},{1,5},{5... | collective-permute-start | bytes 8699912 | tf_op jit(solution)/shard_map/ppermute | solution.py:592
  206.9 33.1 %collective-permute-start.23 = (bf16[5664,128]{1,0:T(8,128)(2,1)S(1)}, bf16[5664,128]{1,0:T(8,128)(2,1)}, u32[]{:S(2)}, u32[]{:S(2)}) collective-permute-start(bf16[5664,128]{1,0:T(8,128)(2,1)S(1)} %slice.365), channel_id=1, source_target_pairs={{0,16},{4,20},{8,24},{12,28},{16,0},{20,4},{24,8},{28,12},{1,17},{... | collective-permute-start | bytes 4349960 | tf_op jit(solution)/shard_map/ppermute | solution.py:592
  235.8 30.1 %collective-permute-start.29 = (bf16[5664,128]{1,0:T(8,128)(2,1)}, bf16[5664,128]{1,0:T(8,128)(2,1)}, u32[]{:S(2)}, u32[]{:S(2)}) collective-permute-start(bf16[5664,128]{1,0:T(8,128)(2,1)} %collective-permute-done.24.refs_4_), channel_id=1, source_target_pairs={{0,4},{4,0},{8,12},{12,8},{16,20},{20,16},{24,28},{28,24},{1,5},{5... | collective-permute-start | bytes 4349960 | tf_op jit(solution)/shard_map/ppermute | solution.py:592
  370.4 45.4 %all-to-all-start.4 = ((bf16[4,256,864]{1,2,0:T(8,128)(2,1)}), bf16[4,256,864]{1,2,0:T(8,128)(2,1)}, u32[]{:S(2)}, u32[]{:S(2)}) async-start(bf16[4,256,864]{1,2,0:T(8,128)(2,1)} %copy.21), calls=%async_computation.4 | async-start | bytes 3538944 | tf_op jit(solution)/shard_map/all_to_all | solution.py:585
  399.1 89.0 %collective-permute-start.40 = (bf16[15104,128]{1,0:T(8,128)(2,1)}, bf16[15104,128]{1,0:T(8,128)(2,1)}, u32[]{:S(2)}, u32[]{:S(2)}) collective-permute-start(bf16[15104,128]{1,0:T(8,128)(2,1)} %slice.385), channel_id=1, source_target_pairs={{0,4},{4,0},{8,12},{12,8},{16,20},{20,16},{24,28},{28,24},{1,5},{5... | collective-permute-start | bytes 11599880 | tf_op jit(solution)/shard_map/ppermute | solution.py:592
  425.4 33.9 %collective-permute-start.60 = (f32[128,128]{1,0:T(8,128)S(1)}, f32[128,128]{1,0:T(8,128)S(1)}, u32[]{:S(2)}, u32[]{:S(2)}) collective-permute-start(f32[128,128]{1,0:T(8,128)S(1)} %bitcast.158), channel_id=1, source_target_pairs={{0,1},{1,0},{2,3},{3,2},{4,5},{5,4},{6,7},{7,6},{8,9},{9,8},{10,11... | collective-permute-start | bytes 196616 | tf_op jit(solution)/shard_map/ppermute | solution.py:592
  457.9 58.6 %collective-permute-start.50 = (bf16[30208,128]{1,0:T(8,128)(2,1)}, bf16[30208,128]{1,0:T(8,128)(2,1)}, u32[]{:S(2)}, u32[]{:S(2)}) collective-permute-start(bf16[30208,128]{1,0:T(8,128)(2,1)} %slice.399), channel_id=1, source_target_pairs={{0,4},{4,0},{8,12},{12,8},{16,20},{20,16},{24,28},{28,24},{1,5},{5... | collective-permute-start | bytes 23199752 | tf_op jit(solution)/shard_map/ppermute | solution.py:592
  514.9 38.4 %collective-permute-start.68 = (bf16[1344,128]{1,0:T(8,128)(2,1)S(1)}, bf16[1344,128]{1,0:T(8,128)(2,1)}, u32[]{:S(2)}, u32[]{:S(2)}) collective-permute-start(bf16[1344,128]{1,0:T(8,128)(2,1)S(1)} %add_convert_fusion.21), channel_id=1, source_target_pairs={{0,8},{4,12},{8,0},{12,4},{16,24},{20,28},{24,16},{28,20},{1,9},{5... | collective-permute-start | bytes 1032200 | tf_op jit(solution)/shard_map/ppermute | solution.py:592
  522.9 29.8 %collective-permute-start.51 = (bf16[3776,128]{1,0:T(8,128)(2,1)S(1)}, bf16[3776,128]{1,0:T(8,128)(2,1)S(1)}, u32[]{:S(2)}, u32[]{:S(2)}) collective-permute-start(bf16[3776,128]{1,0:T(8,128)(2,1)S(1)} %get-tuple-element.44), channel_id=1, source_target_pairs={{0,16},{4,20},{8,24},{12,28},{16,0},{20,4},{24,8},{28,12},{1,17},{... | collective-permute-start | bytes 2899976 | tf_op jit(solution)/shard_map/ppermute | solution.py:592
  527.4 35.6 %collective-permute-start.33 = (bf16[1888,128]{1,0:T(8,128)(2,1)S(1)}, bf16[1888,128]{1,0:T(8,128)(2,1)S(1)}, u32[]{:S(2)}, u32[]{:S(2)}) collective-permute-start(bf16[1888,128]{1,0:T(8,128)(2,1)S(1)} %get-tuple-element.53), channel_id=1, source_target_pairs={{0,16},{4,20},{8,24},{12,28},{16,0},{20,4},{24,8},{28,12},{1,17},{... | collective-permute-start | bytes 1449992 | tf_op jit(solution)/shard_map/ppermute | solution.py:592
  532.1 44.1 %collective-permute-start.56 = (bf16[3776,128]{1,0:T(8,128)(2,1)S(1)}, bf16[3776,128]{1,0:T(8,128)(2,1)S(1)}, u32[]{:S(2)}, u32[]{:S(2)}) collective-permute-start(bf16[3776,128]{1,0:T(8,128)(2,1)S(1)} %get-tuple-element.45), channel_id=1, source_target_pairs={{0,8},{4,12},{8,0},{12,4},{16,24},{20,28},{24,16},{28,20},{1,9},{5... | collective-permute-start | bytes 2899976 | tf_op jit(solution)/shard_map/ppermute | solution.py:592
  552.7 31.1 %collective-permute-start.53 = (bf16[3776,128]{1,0:T(8,128)(2,1)S(1)}, bf16[3776,128]{1,0:T(8,128)(2,1)S(1)}, u32[]{:S(2)}, u32[]{:S(2)}) collective-permute-start(bf16[3776,128]{1,0:T(8,128)(2,1)S(1)} %get-tuple-element.47), channel_id=1, source_target_pairs={{0,16},{4,20},{8,24},{12,28},{16,0},{20,4},{24,8},{28,12},{1,17},{... | collective-permute-start | bytes 2899976 | tf_op jit(solution)/shard_map/ppermute | solution.py:592
  554.5 41.0 %collective-permute-start.52 = (bf16[3776,128]{1,0:T(8,128)(2,1)S(1)}, bf16[3776,128]{1,0:T(8,128)(2,1)S(1)}, u32[]{:S(2)}, u32[]{:S(2)}) collective-permute-start(bf16[3776,128]{1,0:T(8,128)(2,1)S(1)} %add_convert_fusion.6), channel_id=1, source_target_pairs={{0,8},{4,12},{8,0},{12,4},{16,24},{20,28},{24,16},{28,20},{1,9},{5... | collective-permute-start | bytes 2899976 | tf_op jit(solution)/shard_map/ppermute | solution.py:592
  563.1 132.5 %collective-permute-start.64 = (f32[128,128]{1,0:T(8,128)S(1)}, f32[128,128]{1,0:T(8,128)S(1)}, u32[]{:S(2)}, u32[]{:S(2)}) collective-permute-start(f32[128,128]{1,0:T(8,128)S(1)} %add.354), channel_id=1, source_target_pairs={{0,16},{4,20},{8,24},{12,28},{16,0},{20,4},{24,8},{28,12},{1,17},{... | collective-permute-start | bytes 196616 | tf_op jit(solution)/shard_map/ppermute | solution.py:592
  574.7 31.1 %collective-permute-start.45 = (bf16[1888,128]{1,0:T(8,128)(2,1)S(1)}, bf16[1888,128]{1,0:T(8,128)(2,1)S(1)}, u32[]{:S(2)}, u32[]{:S(2)}) collective-permute-start(bf16[1888,128]{1,0:T(8,128)(2,1)S(1)} %get-tuple-element.58), channel_id=1, source_target_pairs={{0,8},{4,12},{8,0},{12,4},{16,24},{20,28},{24,16},{28,20},{1,9},{5... | collective-permute-start | bytes 1449992 | tf_op jit(solution)/shard_map/ppermute | solution.py:592
  576.2 30.8 %collective-permute-start.47 = (bf16[1888,128]{1,0:T(8,128)(2,1)S(1)}, bf16[1888,128]{1,0:T(8,128)(2,1)S(1)}, u32[]{:S(2)}, u32[]{:S(2)}) collective-permute-start(bf16[1888,128]{1,0:T(8,128)(2,1)S(1)} %get-tuple-element.55), channel_id=1, source_target_pairs={{0,16},{4,20},{8,24},{12,28},{16,0},{20,4},{24,8},{28,12},{1,17},{... | collective-permute-start | bytes 1449992 | tf_op jit(solution)/shard_map/ppermute | solution.py:592
  583.8 32.4 %collective-permute-start.35 = (bf16[1888,128]{1,0:T(8,128)(2,1)S(1)}, bf16[1888,128]{1,0:T(8,128)(2,1)S(1)}, u32[]{:S(2)}, u32[]{:S(2)}) collective-permute-start(bf16[1888,128]{1,0:T(8,128)(2,1)S(1)} %get-tuple-element.52), channel_id=1, source_target_pairs={{0,8},{4,12},{8,0},{12,4},{16,24},{20,28},{24,16},{28,20},{1,9},{5... | collective-permute-start | bytes 1449992 | tf_op jit(solution)/shard_map/ppermute | solution.py:592
  595.5 41.4 %collective-permute-start.55 = (bf16[3776,128]{1,0:T(8,128)(2,1)S(1)}, bf16[3776,128]{1,0:T(8,128)(2,1)S(1)}, u32[]{:S(2)}, u32[]{:S(2)}) collective-permute-start(bf16[3776,128]{1,0:T(8,128)(2,1)S(1)} %get-tuple-element.46), channel_id=1, source_target_pairs={{0,8},{4,12},{8,0},{12,4},{16,24},{20,28},{24,16},{28,20},{1,9},{5... | collective-permute-start | bytes 2899976 | tf_op jit(solution)/shard_map/ppermute | solution.py:592
  606.9 30.1 %collective-permute-start.57 = (bf16[3776,128]{1,0:T(8,128)(2,1)S(1)}, bf16[3776,128]{1,0:T(8,128)(2,1)S(1)}, u32[]{:S(2)}, u32[]{:S(2)}) collective-permute-start(bf16[3776,128]{1,0:T(8,128)(2,1)S(1)} %get-tuple-element.43), channel_id=1, source_target_pairs={{0,16},{4,20},{8,24},{12,28},{16,0},{20,4},{24,8},{28,12},{1,17},{... | collective-permute-start | bytes 2899976 | tf_op jit(solution)/shard_map/ppermute | solution.py:592
  616.2 42.6 %collective-permute-start.44 = (bf16[944,128]{1,0:T(8,128)(2,1)S(1)}, bf16[944,128]{1,0:T(8,128)(2,1)S(1)}, u32[]{:S(2)}, u32[]{:S(2)}) collective-permute-start(bf16[944,128]{1,0:T(8,128)(2,1)S(1)} %slice.391), channel_id=1, source_target_pairs={{0,1},{1,0},{2,3},{3,2},{4,5},{5,4},{6,7},{7,6},{8,9},{9,8},{10,11... | collective-permute-start | bytes 725000 | tf_op jit(solution)/shard_map/ppermute | solution.py:592
  666.8 28.8 %collective-permute-start.69 = (bf16[1344,128]{1,0:T(8,128)(2,1)}, bf16[1344,128]{1,0:T(8,128)(2,1)}, u32[]{:S(2)}, u32[]{:S(2)}) collective-permute-start(bf16[1344,128]{1,0:T(8,128)(2,1)} %add_convert_fusion.20), channel_id=1, source_target_pairs={{0,16},{4,20},{8,24},{12,28},{16,0},{20,4},{24,8},{28,12},{1,17},{... | collective-permute-start | bytes 1032200 | tf_op jit(solution)/shard_map/ppermute | solution.py:592
  (98 other events, 1410.7 us)

commit v2 on v1

--- a/solution.py
+++ b/solution.py
@@ -8,8 +8,8 @@
 from jax.experimental.pallas import tpu as pltpu
 from jax.sharding import PartitionSpec as P
 
+
 D = 1152
-H = 16
 HD = 72
 FF = 4304
 LANES = 128
@@ -384,7 +384,6 @@
     wide_rows = max(stride for _, _, _, stride in plan.values())
     return pl.pallas_call(
         kernel,
-        name="pieces_" + "_".join(names),
         grid=(steps,),
         in_specs=[pl.BlockSpec(memory_space=pltpu.SMEM)] + [spec(name) for name in names],
         out_specs=[pl.BlockSpec(memory_space=pl.ANY)] * len(shapes),
@@ -557,8 +556,7 @@
     )
 
 
-def adam_update(master, grads, first, second, index):
-    matrix_part = index < 4 * D * D + 2 * D * FF
+def adam_update(master, grads, first, second, matrix_part):
     first_new = beta_one * first + (1.0 - beta_one) * grads
     second_new = beta_two * second + (1.0 - beta_two) * grads * grads
     first_hat = first_new / (1.0 - beta_one**adam_step)
@@ -596,32 +594,38 @@
     return functools.reduce(jnp.add, [array.astype(F32) for array in arrays]).astype(BF)
 
 
-def gather(layout, share):
+def gather(layout, share, batches):
     held = {0: share}
-    bit = layout.ctx // 2
-    while bit:
+    bit = 1
+    while bit < layout.ctx:
         held.update({key ^ bit: exchange(held[key], "ctx", bit) for key in list(held)})
-        bit //= 2
-    stack = jnp.concatenate([held[key] for key in range(layout.ctx)])
-    arrays = [(stack, (0, 0, 0, layout.ctx))]
-    if layout.columns == 4:
-        middle, half = (stack.shape[0] // 2, layout.ctx // 2)
-        by_x, by_y = (exchange(stack, "dp", 2), exchange(stack, "dp", 4))
-        arrays += [(by_x, (1, 0, 0, layout.ctx)), (by_y, (2, 0, 0, layout.ctx))]
-        arrays.append((exchange(by_x[:middle], "dp", 4), (3, 0, 0, half)))
-        arrays.append((exchange(by_y[middle:], "dp", 2), (3, 0, half, half)))
-    else:
-        bit = 1
-        while bit < layout.columns:
-            arrays += [
-                (exchange(array, "dp", 2 * bit), (place[0] ^ bit,) + place[1:])
-                for array, place in arrays
-            ]
-            bit *= 2
-    arrays += [
-        (exchange(array, "dp", 1), (place[0], 1) + place[2:]) for array, place in arrays
-    ]
-    return arrays, stack
+        bit *= 2
+    arrays = []
+    members = layout.ctx // batches
+    for batch in range(batches):
+        first = batch * members
+        stack = jnp.concatenate([held[key] for key in range(first, first + members)])
+        found = [(stack, (0, 0, first, members))]
+        if layout.columns == 4:
+            middle, half = (stack.shape[0] // 2, members // 2)
+            by_x = exchange(stack, "dp", 2)
+            by_y = exchange(stack, "dp", 4)
+            found += [(by_x, (1, 0, first, members)), (by_y, (2, 0, first, members))]
+            across = exchange(by_x[:middle], "dp", 4)
+            found.append((across, (3, 0, first, half)))
+            across = exchange(by_y[middle:], "dp", 2)
+            found.append((across, (3, 0, first + half, half)))
+        else:
+            bit = 1
+            while bit < layout.columns:
+                found += [
+                    (exchange(array, "dp", 2 * bit), (place[0] ^ bit,) + place[1:])
+                    for array, place in found
+                ]
+                bit *= 2
+        arrays += found
+    arrays += [(exchange(array, "dp", 1), (place[0], 1) + place[2:]) for array, place in arrays]
+    return arrays, held[layout.ctx - 1]
 
 
 def scatter(layout, pieces):
@@ -629,15 +633,14 @@
     kept = add(pieces[:middle], exchange(pieces[middle:], "dp", 1))
     size = middle // layout.columns
     parts = [kept[index * size : (index + 1) * size] for index in range(layout.columns)]
+    half = size // 2
     if layout.columns == 4:
-        half = size // 2
         low = add(parts[1][:half], exchange(parts[3][:half], "dp", 4))
         high = add(parts[2][half:], exchange(parts[3][half:], "dp", 2))
-        halves = [
+        summed = [
             add(parts[0][:half], exchange(low, "dp", 2), exchange(parts[2][:half], "dp", 4)),
             add(parts[0][half:], exchange(parts[1][half:], "dp", 2), exchange(high, "dp", 4)),
         ]
-        summed = halves
     else:
         bit = layout.columns // 2
         while bit:
@@ -646,7 +649,6 @@
                 for index in range(bit)
             ]
             bit //= 2
-        half = size // 2
         summed = [parts[0][:half], parts[0][half:]]
     each = layout.ctx // 2
     length = size // layout.ctx
@@ -657,50 +659,146 @@
     bit = 1
     while bit < layout.ctx:
         for key in [key for key in held if key & bit]:
-            held[key ^ bit] = add(held[key ^ bit], exchange(held.pop(key), "ctx", bit))
+            moved = exchange(held.pop(key), "ctx", bit)
+            held[key ^ bit] = add(held[key ^ bit], moved)
         bit *= 2
     return held[0]
 
 
 def bits(layout):
     found = []
-    for axis, size, unit in (("ctx", layout.ctx, 1), ("dp", layout.dp, layout.ctx)):
+    for unit, size in ((1, layout.ctx), (2 * layout.ctx, layout.columns), (layout.ctx, 2)):
         bit = 1
         while bit < size:
-            found.append((axis, bit, bit * unit))
+            found.append(bit * unit)
             bit *= 2
     return found
 
 
+def broadcast(layout, shard, owner, held):
+    have = [owner]
+    for bit in bits(layout):
+        other = lax.ppermute(held, ("dp", "ctx"), [(index, index ^ bit) for index in have])
+        have += [index ^ bit for index in have]
+        held = jnp.where((shard & bit) != (owner & bit), other, held)
+    return held
+
+
+def sum_to(layout, owner, held):
+    have = list(range(layout.devices))
+    for bit in reversed(bits(layout)):
+        senders = [index for index in have if (index & bit) != (owner & bit)]
+        other = lax.ppermute(held, ("dp", "ctx"), [(index, index ^ bit) for index in senders])
+        have = [index for index in have if index not in senders]
+        held = (held.astype(F32) + other.astype(F32)).astype(held.dtype)
+    return held
+
+
 def column_groups(layout):
     return [[column * 2 + core for column in range(layout.columns)] for core in range(2)]
 
 
-def spread_weights(layout, flat, shard, everyone):
-    last = layout.devices - 1
-    before = lax.ppermute(
-        flat[-TILE:], ("dp", "ctx"), [(index, index + 1) for index in range(last)]
-    )
+SWEEP = 512
+
+
+def align(layout, params, before, offset):
     length = layout.columns * layout.piece
-    padded = jnp.concatenate([before, flat, jnp.zeros((length - layout.rows, LANES), BF)])
-    offset = (shard * layout.rows) % TILE
-    chunk = lax.dynamic_slice(padded, (TILE - offset, 0), (length, LANES))
-    pieces = chunk.reshape(layout.columns, layout.piece, LANES)
-    held = lax.all_to_all(
-        pieces, "dp", split_axis=0, concat_axis=0, tiled=True, axis_index_groups=everyone
-    )
-    return chunk, held
-
-
-def broadcast(layout, shard, sources):
-    held = jnp.concatenate([rows for _, rows in sources])
-    owner = jnp.concatenate(
-        [jnp.full((rows.shape[0], 1), source, jnp.int32) for source, rows in sources]
-    )
-    for axis, bit, unit in bits(layout):
-        other = exchange(held, axis, bit)
-        held = jnp.where(((owner ^ shard) & unit) == 0, held, other)
-    return held
+    steps = pl.cdiv(layout.rows, SWEEP)
+    held = max(TILE + steps * SWEEP, TILE + length)
+
+    def kernel(offset_ref, rows, previous, chunk, wide):
+        step = pl.program_id(0)
+
+        @pl.when(step == 0)
+        def _():
+            wide[0:TILE, :] = previous[...]
+
+        base = pl.multiple_of(TILE + step * SWEEP, TILE)
+        wide[pl.ds(base, SWEEP), :] = rows[...].reshape(SWEEP, LANES)
+
+        @pl.when(step == steps - 1)
+        def _():
+            chunk[...] = wide[pl.ds(TILE - offset_ref[0], length), :].astype(BF)
+
+    return pl.pallas_call(
+        kernel,
+        name="align",
+        grid=(steps,),
+        in_specs=[
+            pl.BlockSpec(memory_space=pltpu.SMEM),
+            pl.BlockSpec((1, SWEEP * LANES), lambda i: (0, i)),
+            pl.BlockSpec((TILE, LANES), lambda i: (0, 0)),
+        ],
+        out_specs=pl.BlockSpec((length, LANES), lambda i: (0, 0)),
+        out_shape=jax.ShapeDtypeStruct((length, LANES), BF),
+        scratch_shapes=[pltpu.VMEM((held, LANES), F32)],
+        compiler_params=pltpu.CompilerParams(vmem_limit_bytes=VMEM_LIMIT),
+    )(offset, params, before)
+
+
+def finish(layout, where, chunk, leftover, vectors, params, first, second):
+    length = layout.columns * layout.piece
+    steps = pl.cdiv(layout.rows, SWEEP)
+    held = max(length, TILE + steps * SWEEP)
+    vector_first = ROW_VEC - layout.start(layout.devices - 1)
+
+    def kernel(place, sums, rest, vector, master, one, two, grads, new, new_one, new_two, wide):
+        step = pl.program_id(0)
+        shard = place[0]
+
+        @pl.when(step == 0)
+        def _():
+            wide[pl.ds(0, length), :] = sums[...].astype(F32)
+            used = 0
+            for owner, rows in layout.leftover():
+
+                @pl.when(shard == owner)
+                def _(used=used, rows=rows):
+                    wide[pl.ds(0, rows), :] += rest[pl.ds(used, rows), :].astype(F32)
+
+                used += rows
+
+            @pl.when(shard == layout.devices - 1)
+            def _():
+                wide[pl.ds(vector_first, VEC_ROWS), :] += vector[...]
+
+        grad = wide[pl.ds(place[1] + step * SWEEP, SWEEP), :]
+        row = lax.broadcasted_iota(jnp.int32, (SWEEP, LANES), 0)
+        matrix_part = row < ROW_VEC - shard * layout.rows - step * SWEEP
+        value = master[...].reshape(SWEEP, LANES)
+        results = adam_update(
+            value,
+            grad,
+            one[...].reshape(SWEEP, LANES),
+            two[...].reshape(SWEEP, LANES),
+            matrix_part,
+        )
+        for ref, result in zip((grads, new, new_one, new_two), (grad,) + results):
+            ref[...] = result.reshape(1, SWEEP * LANES)
+
+    flat = pl.BlockSpec((1, SWEEP * LANES), lambda i: (0, i))
+
+    def whole(array):
+        return pl.BlockSpec(array.shape, lambda i: (0, 0))
+
+    return pl.pallas_call(
+        kernel,
+        name="finish",
+        grid=(steps,),
+        in_specs=[
+            pl.BlockSpec(memory_space=pltpu.SMEM),
+            whole(chunk),
+            whole(leftover),
+            whole(vectors),
+            flat,
+            flat,
+            flat,
+        ],
+        out_specs=[flat] * 4,
+        out_shape=[jax.ShapeDtypeStruct(params.shape, F32)] * 4,
+        scratch_shapes=[pltpu.VMEM((held, LANES), F32)],
+        compiler_params=pltpu.CompilerParams(vmem_limit_bytes=VMEM_LIMIT),
+    )(where, chunk, leftover, vectors, params, first, second)
 
 
 def shards(layout, inputs, counts, params, first_moment, second_moment, out_cotangent):
@@ -713,26 +811,37 @@
     place = jnp.stack(
         [lax.axis_index("dp") // 2, lax.axis_index("dp") % 2, lax.axis_index("ctx")]
     ).astype(jnp.int32)
-    padding = -layout.rows % 8 * LANES
-    flat = jnp.pad(params[0].astype(BF), (0, padding)).reshape(-1, LANES)[: layout.rows]
-    chunk_rows, pieces = spread_weights(layout, flat, shard, everyone)
+    last = layout.devices - 1
+    ending = params[0, -TILE * LANES :].reshape(TILE, LANES)
+    before = lax.ppermute(ending, ("dp", "ctx"), [(index, index + 1) for index in range(last)])
+    offset = ((shard * layout.rows) % TILE).astype(jnp.int32)
+    chunk_rows = align(layout, params, before, offset.reshape(1))
+    pieces = lax.all_to_all(
+        chunk_rows.reshape(layout.columns, layout.piece, LANES),
+        "dp",
+        split_axis=0,
+        concat_axis=0,
+        tiled=True,
+        axis_index_groups=everyone,
+    )
     shared_first = pieces[: layout.first].reshape(-1, LANES)
-    gathered_first, stack = gather(layout, shared_first)
+    gathered_first, along = gather(layout, shared_first, 2)
     shared_rest = pieces[layout.first :].reshape(-1, LANES)
-    shared_rest = lax.optimization_barrier((shared_rest, stack))[0]
-    gathered_rest, _ = gather(layout, shared_rest)
-    vector_first = ROW_VEC - layout.start(layout.devices - 1)
+    shared_rest = lax.optimization_barrier((shared_rest, along))[0]
+    gathered_rest, _ = gather(layout, shared_rest, 1)
+    vector_first = ROW_VEC - layout.start(last)
     assert 0 <= vector_first and vector_first + VEC_ROWS <= layout.columns * layout.piece
-    sources = [(owner, chunk_rows[:rows]) for owner, rows in layout.leftover()]
-    sources.append((layout.devices - 1, chunk_rows[vector_first : vector_first + VEC_ROWS]))
-    spread = broadcast(layout, shard, sources)
-    leftover = spread[:-VEC_ROWS]
-    flat_vectors = spread[-VEC_ROWS:].reshape(-1).astype(F32)
+    leftover = jnp.concatenate(
+        [broadcast(layout, shard, owner, chunk_rows[:rows]) for owner, rows in layout.leftover()]
+    )
+    spread = chunk_rows[vector_first : vector_first + VEC_ROWS]
+    spread = broadcast(layout, shard, last, spread)
+    flat_vectors = spread.reshape(-1).astype(F32)
     vectors = []
-    offset = 0
+    used = 0
     for length in VEC_LENGTHS:
-        vectors.append(flat_vectors[offset : offset + length])
-        offset += length
+        vectors.append(flat_vectors[used : used + length])
+        used += length
     (
         gain_one,
         shift_one,
@@ -780,6 +889,7 @@
     (terms,) = gradient_pieces(
         layout, place, (middle_group, layout.columns), {"up": grad_up, "down": grad_down}
     )
+    grad_pre_round, terms = lax.optimization_barrier((grad_pre_round, terms))
     sum_last = scatter(layout, terms)
     grad_normed_two = dot_t(grad_pre_round, up_weight)
     grad_gain_two = jnp.sum(grad_normed_two * unit_two, 0)
@@ -824,10 +934,14 @@
     ]
     padding = jnp.zeros((VEC_ROWS * LANES - sum(VEC_LENGTHS),), F32)
     vector_grads = jnp.concatenate(vector_terms + [padding]).reshape(VEC_ROWS, LANES)
-    for axis, bit, _ in bits(layout):
-        vector_grads = vector_grads + exchange(vector_grads, axis, bit)
-    for axis, bit, _ in bits(layout):
-        leftover_terms = add(leftover_terms, exchange(leftover_terms, axis, bit))
+    vector_grads = sum_to(layout, last, vector_grads)
+    used = 0
+    sums_left = []
+    for owner, rows in layout.leftover():
+        part = leftover_terms[used : used + rows]
+        sums_left.append(sum_to(layout, owner, part))
+        used += rows
+    leftover_sum = jnp.concatenate(sums_left)
 
     summed = jnp.concatenate([sum_first, sum_middle, sum_last])
     held = lax.all_to_all(
@@ -838,24 +952,15 @@
         tiled=True,
         axis_index_groups=everyone,
     )
-    chunk_sum = held.reshape(-1, LANES).astype(F32)
-    extra = jnp.zeros_like(chunk_sum)
-    used = 0
-    for owner, rows in layout.leftover():
-        placed = jnp.pad(
-            leftover_terms[used : used + rows].astype(F32), ((0, chunk_sum.shape[0] - rows), (0, 0))
-        )
-        extra = jnp.where(shard == owner, placed, extra)
-        used += rows
-    after = chunk_sum.shape[0] - vector_first - VEC_ROWS
-    placed = jnp.pad(vector_grads, ((vector_first, after), (0, 0)))
-    chunk_sum = chunk_sum + jnp.where(shard == layout.devices - 1, placed, extra)
-    offset = (shard * layout.rows) % TILE
-    rows = lax.dynamic_slice(chunk_sum, (offset, 0), (layout.rows, LANES))
-    param_grads = rows.reshape(params.shape)
-    index = (shard * params.shape[1] + jnp.arange(params.shape[1], dtype=jnp.int32))[None, :]
-    new_params, new_first, new_second = adam_update(
-        params, param_grads, first_moment, second_moment, index
+    param_grads, new_params, new_first, new_second = finish(
+        layout,
+        jnp.stack([shard.astype(jnp.int32), offset]),
+        held.reshape(-1, LANES),
+        leftover_sum,
+        vector_grads,
+        params,
+        first_moment,
+        second_moment,
     )
     return (output[None], input_grad[None], param_grads, new_params, new_first, new_second)
 
@@ -873,8 +978,12 @@
 
     def program(inputs, counts, params, first_moment, second_moment, out_cotangent):
         layout = Layout(dp, ctx, params.shape[1] // (dp * ctx))
+
+        def body(*arguments):
+            return shards(layout, *arguments)
+
         return jax.shard_map(
-            functools.partial(shards, layout),
+            body,
             mesh=mesh,
             in_specs=placed,
             out_specs=(

time: 734 us -> 796 us (1.084)
  starting transfers between devices: 96 us -> 163 us
  other arithmetic: 70.6 us -> 26.8 us
  blocking collectives: 0 us -> 19.9 us
  Pallas kernels: 109 us -> 124 us
    ppermute x69 -> x63, starting transfers between devices: 67.8 us -> 104 us  [exchange(): lax.ppermute(array, axis, [(index, index ^ bit) for index in range(size)])]
    convert_element_type x3 -> x6, other arithmetic: 23.7 us -> 1.21 us  [the longest x5 1.2 us: sum_to(): held = (held.astype(F32) + other.astype(F32)).astype(held.dtype)]
    all_to_all x0 -> x1, blocking collectives: none -> 19.9 us  [to_heads(): held = lax.all_to_all(split, 'ctx', split_axis=0, concat_axis=0, tiled=True)]
    ppermute x1 -> x21, starting transfers between devices: 4.02 us -> 23.6 us  [the longest x10 11 us: sum_to(): lax.ppermute(held, ('dp', 'ctx'), [(index, index ^ bit) for index in send...]
    sub x1 -> x0, other arithmetic: 18.1 us -> none  [adam_update(): master - rate * (first_hat / (jnp.sqrt(second_hat) + adam_epsilon) + deca...]
    all_to_all x2 -> x1, waiting for transfers between devices: 15.6 us -> 0.01 us  [to_heads(): held = lax.all_to_all(split, 'ctx', split_axis=0, concat_axis=0, tiled=True)]
    all_to_all x2, waiting for transfers between devices: 4.46 us -> 19.9 us  [from_heads(): held = lax.all_to_all(split, 'ctx', split_axis=0, concat_axis=0, tiled=True)]
    pallas_call x3 -> x5, Pallas kernels: 39.4 us -> 53.9 us  [the longest x3 39.6 us: gradient_pieces(): pl.pallas_call(kernel, grid=(steps,), in_specs=[pl.BlockSpec(memory_space...]
  transfers between devices with their start and end apart: 76 -> 89, of which waited for: 37 -> 32; matrix products, arithmetic and copies ran while one was open for 18% -> 12% of each run, Pallas kernels for 12% -> 9%
where the time goes in v2:
time: 796 us; the launch traced here: 781 us
  waiting for transfers between devices  315 us (40%)
  starting transfers between devices  163 us (20%)
  Pallas kernels  124 us (16%)
  matrix products  79.6 us (10%)
  local copies, waits for them, and re-layouts  49.7 us (6%)
  other arithmetic  26.8 us (3%)
  blocking collectives  19.9 us (2%)
    ppermute x63, waiting for transfers between devices, exchange(): lax.ppermute(array, axis, [(index, index ^ bit) for index in range(size)])  283 us
    ppermute x63, starting transfers between devices, exchange(): lax.ppermute(array, axis, [(index, index ^ bit) for index in range(size)])  104 us
    pallas_call x3, Pallas kernels, gradient_pieces(): pl.pallas_call(kernel, grid=(steps,), in_specs=[pl.BlockSpec(memory_space...  39.6 us
    dot_general x4, matrix products, dense(): return jnp.dot(left, right, preferred_element_type=F32)  28.6 us
    dot_general x4, matrix products, dot_t(): lax.dot_general(left, right, (((1,), (1,)), ((), ())), preferred_element_...  26.8 us
    dot_general x4, matrix products, t_dot(): lax.dot_general(left, right, (((0,), (0,)), ((), ())), preferred_element_...  24.2 us
    pallas_call x1, Pallas kernels, attend_back(): pl.pallas_call(kernel, name='attend_back', grid=(heads,), in_specs=[pl.Bl...  22.6 us
    pallas_call x1, Pallas kernels, other_weights(): pl.pallas_call(kernel, name='other_weights', grid=(STEPS,), in_specs=[pl....  22.2 us
  transfers between devices with their start and end apart: 89, of which 32 were waited for; matrix products, arithmetic and copies ran while one was open for 12% of the time, Pallas kernels for 9%

profile of v2, /device:TPU:1, one launch (start us, length us, event | category | flops | bytes accessed | tf_op | source)
XLA Modules:
  0.0 780.8 jit_solution(13571917594399199812)
XLA Ops:
  22.5 9.2 %all-to-all-start = ((bf16[4,944,128]{2,1,0:T(8,128)(2,1)}), bf16[4,944,128]{2,1,0:T(8,128)(2,1)S(1)}, u32[]{:S(2)}, u32[]{:S(2)}) async-start(bf16[4,944,128]{2,1,0:T(8,128)(2,1)} %bitcast.136), calls=%async_computation | async-start | bytes 1933312 | tf_op jit(solution)/shard_map/all_to_all | solution.py:819
  42.7 9.6 %collective-permute-done.6 = bf16[944,128]{1,0:T(8,128)(2,1)S(1)} collective-permute-done((bf16[944,128]{1,0:T(8,128)(2,1)S(1)}, bf16[944,128]{1,0:T(8,128)(2,1)S(1)}, u32[]{:S(2)}, u32[]{:S(2)}) %collective-permute-start.6) | collective-permute-done | bytes 241696 | tf_op jit(solution)/shard_map/ppermute | solution.py:590
  54.0 11.3 %collective-permute-done.12 = bf16[944,128]{1,0:T(8,128)(2,1)S(1)} collective-permute-done((bf16[944,128]{1,0:T(8,128)(2,1)S(1)}, bf16[944,128]{1,0:T(8,128)(2,1)S(1)}, u32[]{:S(2)}, u32[]{:S(2)}) %collective-permute-start.12) | collective-permute-done | bytes 241696 | tf_op jit(solution)/shard_map/ppermute | solution.py:590
  67.3 13.1 %collective-permute-start.17 = (bf16[1888,128]{1,0:T(8,128)(2,1)S(1)}, bf16[1888,128]{1,0:T(8,128)(2,1)S(1)}, u32[]{:S(2)}, u32[]{:S(2)}) collective-permute-start(bf16[1888,128]{1,0:T(8,128)(2,1)S(1)} %pad_maximum_fusion.2.refs_0_), channel_id=1, source_target_pairs={{0,4},{4,0},{8,12},{12,8},{16,20},{20,16},{24,28},{28,24},{1,5},{5... | collective-permute-start | bytes 1449992 | tf_op jit(solution)/shard_map/ppermute | solution.py:590
  98.3 31.8 %collective-permute-done.33 = bf16[2832,128]{1,0:T(8,128)(2,1)S(1)} collective-permute-done((bf16[2832,128]{1,0:T(8,128)(2,1)S(1)}, bf16[2832,128]{1,0:T(8,128)(2,1)S(1)}, u32[]{:S(2)}, u32[]{:S(2)}) %collective-permute-start.33) | collective-permute-done | bytes 725024 | tf_op jit(solution)/shard_map/ppermute | solution.py:590
  155.3 10.2 %first_weights.1 = bf16[1152,3456]{1,0:T(8,128)(2,1)} custom-call(s32[3]{0:T(128)} %pad_add_fusion.place_ref, bf16[1888,128]{1,0:T(8,128)(2,1)} %copy-done.5, bf16[1888,128]{1,0:T(8,128)(2,1)} %copy-done.8, bf16[1888,128]{1,0:T(8,128)(2,1)} %copy-done.9, bf16[944,128]{1,0:T(8,128)(2,1)} %copy-done.22, bf16[944,128]{1,0:T(8,128)(2,1)} %copy-done.23, ...), custom_call_target="tpu_custom_call" | custom-call | tf_op jit(solution)/shard_map/first_weights/pallas_call | solution.py:217
  176.9 15.2 %all-to-all-start.1 = ((bf16[4,256,864]{1,2,0:T(8,128)(2,1)}), bf16[4,256,864]{1,2,0:T(8,128)(2,1)S(1)}, u32[]{:S(2)}, u32[]{:S(2)}) async-start(bf16[4,256,864]{1,2,0:T(8,128)(2,1)} %bitcast.137), calls=%async_computation.1 | async-start | bytes 3538944 | tf_op jit(solution)/shard_map/all_to_all | solution.py:575
  192.6 19.5 %collective-permute-done.35.refs_1_ = bf16[11328,128]{1,0:T(8,128)(2,1)} collective-permute-done((bf16[11328,128]{1,0:T(8,128)(2,1)}, bf16[11328,128]{1,0:T(8,128)(2,1)}, u32[]{:S(2)}, u32[]{:S(2)}) %collective-permute-start.35) | collective-permute-done | bytes 2900000 | tf_op jit(solution)/shard_map/ppermute | solution.py:590
  219.7 27.2 %collective-permute-done.37.refs_3_ = bf16[5664,128]{1,0:T(8,128)(2,1)} collective-permute-done((bf16[5664,128]{1,0:T(8,128)(2,1)S(1)}, bf16[5664,128]{1,0:T(8,128)(2,1)}, u32[]{:S(2)}, u32[]{:S(2)}) %collective-permute-start.37) | collective-permute-done | bytes 1450016 | tf_op jit(solution)/shard_map/ppermute | solution.py:590
  255.5 14.9 %attend.1 = (bf16[1024,288]{1,0:T(8,128)(2,1)}, f32[4,1024,1]{2,1,0:T(8,128)}) custom-call(s32[1]{0:T(128)} %copy.31.count, bf16[1024,864]{1,0:T(8,128)(2,1)} %bitcast.132), custom_call_target="tpu_custom_call" | custom-call | tf_op jit(solution)/shard_map/attend/pallas_call | solution.py:450
  277.0 22.2 %other_weights.1 = (bf16[1152,1152]{1,0:T(8,128)(2,1)}, bf16[1152,4304]{1,0:T(8,128)(2,1)}, bf16[4304,1152]{1,0:T(8,128)(2,1)}) custom-call(s32[3]{0:T(128)} %pad_add_fusion.place_ref, bf16[11328,128]{1,0:T(8,128)(2,1)} %constant_dynamic-update-slice_fusion.2.refs_0_, bf16[11328,128]{1,0:T(8,128)(2,1)} %collective-permute-done.35.refs_1_, ...), custom_call_target="tpu_custom_call" | custom-call | tf_op jit(solution)/shard_map/other_weights/pallas_call | solution.py:260
  302.5 10.6 %convolution_add_fusion = f32[256,4304]{0,1:T(8,128)} fusion(bf16[1152,4304]{1,0:T(8,128)(2,1)} %get-tuple-element.25, f32[4304]{0:T(1024)S(1)} %slice.357, f32[256,1152]{1,0:T(8,128)S(1)} %get-tuple-element.82, f32[1152]{0:T(1024)S(1)} %copy-done.32, f32[1152]{0:T(1024)S(1)} %get-tuple-element.73, f32[256]{0:T(256)S(1)} %add_rsqrt_fusion, ...), kind=kOutput, calls=%fused_computation.7 | convolution fusion | flops 2541178880 | bytes 15531840 | tf_op jit(solution)/shard_map/dot_general | solution.py:410
  313.1 10.0 %convolution_convert_fusion.refs_1_ = bf16[4304,1152]{1,0:T(8,128)(2,1)} fusion(f32[1,256,1152]{2,1,0:T(8,128)S(1)} %copy-done.6, f32[256]{0:T(256)S(1)} %compare_convert_fusion, f32[256,4304]{0,1:T(8,128)} %convolution_add_fusion), kind=kOutput, calls=%fused_computation | convolution fusion | flops 2554066944 | bytes 15504384 | tf_op jit(solution)/shard_map/dot_general | solution.py:406
  339.1 16.5 %shard_map.109 = bf16[60416,128]{1,0:T(8,128)(2,1)} custom-call(s32[3]{0:T(128)} %pad_add_fusion.place_ref, bf16[1152,4304]{1,0:T(8,128)(2,1)} %convolution_convert_fusion.1.refs_0_.refs_1_, bf16[4304,1152]{1,0:T(8,128)(2,1)} %convolution_convert_fusion.refs_1_), custom_call_target="tpu_custom_call" | custom-call | tf_op jit(solution)/shard_map/pallas_call | solution.py:385
  355.6 8.6 %multiply_reduce_fusion = (f32[1152]{0:T(1024)}, f32[256]{0:T(256)S(1)}, f32[256]{0:T(256)S(1)}, f32[1152]{0:T(1024)}, f32[256,1152]{1,0:T(8,128)S(1)}) fusion(f32[256,1152]{1,0:T(8,128)S(1)} %get-tuple-element.82, f32[256]{0:T(256)S(1)} %add_rsqrt_fusion, f32[256]{0:T(256)S(1)} %broadcast_multiply_fusion.4, f32[1152]{0:T(1024)S(1)} %get-tuple-element.73, ...), kind=kOutput, calls=%fused_computation.59 | convolution fusion | flops 2541254144 | bytes 14497280 | tf_op jit(solution)/shard_map/dot_general | solution.py:402
  370.0 19.9 %all_to_all.30 = bf16[4,256,288]{1,2,0:T(8,128)(2,1)} all-to-all(bf16[4,256,288]{1,2,0:T(8,128)(2,1)} %bitcast.149), channel_id=1, replica_groups=mesh['dp'=8,'ctx'=4] {'ctx'}, dimensions={0} | all-to-all | bytes 1179648 | tf_op jit(solution)/shard_map/all_to_all | solution.py:575
  392.2 22.6 %attend_back.1 = (bf16[1024,864]{1,0:T(8,128)(2,1)}, f32[4,2,72]{2,1,0:T(2,128)}) custom-call(s32[1]{0:T(128)} %copy.31.count, bf16[1024,864]{1,0:T(8,128)(2,1)} %bitcast.133, f32[4,1024,1]{2,1,0:T(8,128)} %get-tuple-element.28.logs, bf16[1024,288]{1,0:T(8,128)(2,1)} %bitcast.143), custom_call_target="tpu_custom_call" | custom-call | tf_op jit(solution)/shard_map/attend_back/pallas_call | solution.py:515
  425.3 12.1 %shard_map.111 = bf16[30208,128]{1,0:T(8,128)(2,1)} custom-call(s32[3]{0:T(128)} %pad_add_fusion.place_ref, bf16[1152,1152]{1,0:T(8,128)(2,1)} %convolution_convert_fusion.3.refs_0_, bf16[1152,4304]{1,0:T(8,128)(2,1)} %convolution_convert_fusion.1.refs_0_.refs_1_), custom_call_target="tpu_custom_call" | custom-call | tf_op jit(solution)/shard_map/pallas_call | solution.py:385
  443.7 19.9 %all-to-all-done.4 = bf16[4,256,864]{1,2,0:T(8,128)(2,1)} async-done(((bf16[4,256,864]{1,2,0:T(8,128)(2,1)}), bf16[4,256,864]{1,2,0:T(8,128)(2,1)}, u32[]{:S(2)}, u32[]{:S(2)}) %all-to-all-start.4) | async-done | bytes 1769504 | tf_op jit(solution)/shard_map/all_to_all | solution.py:583
  474.5 9.1 %fusion.9 = bf16[1,256,1152]{2,1,0:T(8,128)(2,1)} fusion(f32[256,1152]{1,0:T(8,128)S(1)} %get-tuple-element.82, bf16[4304,1152]{1,0:T(8,128)(2,1)} %get-tuple-element.26, f32[1152]{0:T(1024)S(1)} %copy-done.41, f32[256,4304]{0,1:T(8,128)} %convolution_add_fusion), kind=kOutput, calls=%fused_computation.23 | convolution fusion | flops 2549403648 | bytes 16097792 | tf_op jit(solution)/shard_map/dot_general | solution.py:410
  500.7 11.0 %shard_map.110 = (bf16[30208,128]{1,0:T(8,128)(2,1)}, bf16[1344,128]{1,0:T(8,128)(2,1)}) custom-call(s32[3]{0:T(128)} %pad_add_fusion.place_ref, bf16[1152,3456]{1,0:T(8,128)(2,1)} %convolution_convert_fusion.2.refs_0_), custom_call_target="tpu_custom_call" | custom-call | tf_op jit(solution)/shard_map/pallas_call | solution.py:385
  528.8 19.6 %collective-permute-done.55 = bf16[1888,128]{1,0:T(8,128)(2,1)S(1)} collective-permute-done((bf16[1888,128]{1,0:T(8,128)(2,1)S(1)}, bf16[1888,128]{1,0:T(8,128)(2,1)S(1)}, u32[]{:S(2)}, u32[]{:S(2)}) %collective-permute-start.55) | collective-permute-done | bytes 483360 | tf_op jit(solution)/shard_map/ppermute | solution.py:590
  559.1 19.5 %collective-permute-start.65 = (bf16[3776,128]{1,0:T(8,128)(2,1)S(1)}, bf16[3776,128]{1,0:T(8,128)(2,1)S(1)}, u32[]{:S(2)}, u32[]{:S(2)}) collective-permute-start(bf16[3776,128]{1,0:T(8,128)(2,1)S(1)} %get-tuple-element.52), channel_id=1, source_target_pairs={{0,16},{4,20},{8,24},{12,28},{16,0},{20,4},{24,8},{28,12},{1,17},{... | collective-permute-start | bytes 2899976 | tf_op jit(solution)/shard_map/ppermute | solution.py:590
  582.1 19.3 %collective-permute-done.65 = bf16[3776,128]{1,0:T(8,128)(2,1)S(1)} collective-permute-done((bf16[3776,128]{1,0:T(8,128)(2,1)S(1)}, bf16[3776,128]{1,0:T(8,128)(2,1)S(1)}, u32[]{:S(2)}, u32[]{:S(2)}) %collective-permute-start.65) | collective-permute-done | bytes 966688 | tf_op jit(solution)/shard_map/ppermute | solution.py:590
  614.4 26.0 %collective-permute-done.46 = bf16[1888,128]{1,0:T(8,128)(2,1)S(1)} collective-permute-done((bf16[1888,128]{1,0:T(8,128)(2,1)S(1)}, bf16[1888,128]{1,0:T(8,128)(2,1)S(1)}, u32[]{:S(2)}, u32[]{:S(2)}) %collective-permute-start.46) | collective-permute-done | bytes 483360 | tf_op jit(solution)/shard_map/ppermute | solution.py:590
  643.4 17.7 %collective-permute-done.66 = bf16[3776,128]{1,0:T(8,128)(2,1)S(1)} collective-permute-done((bf16[3776,128]{1,0:T(8,128)(2,1)S(1)}, bf16[3776,128]{1,0:T(8,128)(2,1)S(1)}, u32[]{:S(2)}, u32[]{:S(2)}) %collective-permute-start.66) | collective-permute-done | bytes 966688 | tf_op jit(solution)/shard_map/ppermute | solution.py:590
  662.0 9.3 %collective-permute-done.59 = bf16[1888,128]{1,0:T(8,128)(2,1)S(1)} collective-permute-done((bf16[1888,128]{1,0:T(8,128)(2,1)S(1)}, bf16[1888,128]{1,0:T(8,128)(2,1)S(1)}, u32[]{:S(2)}, u32[]{:S(2)}) %collective-permute-start.59) | collective-permute-done | bytes 483360 | tf_op jit(solution)/shard_map/ppermute | solution.py:590
  673.1 8.6 %collective-permute-done.49 = bf16[1888,128]{1,0:T(8,128)(2,1)S(1)} collective-permute-done((bf16[1888,128]{1,0:T(8,128)(2,1)S(1)}, bf16[1888,128]{1,0:T(8,128)(2,1)S(1)}, u32[]{:S(2)}, u32[]{:S(2)}) %collective-permute-start.49) | collective-permute-done | bytes 483360 | tf_op jit(solution)/shard_map/ppermute | solution.py:590
  683.9 18.6 %collective-permute-done.69 = bf16[3776,128]{1,0:T(8,128)(2,1)S(1)} collective-permute-done((bf16[3776,128]{1,0:T(8,128)(2,1)S(1)}, bf16[3776,128]{1,0:T(8,128)(2,1)S(1)}, u32[]{:S(2)}, u32[]{:S(2)}) %collective-permute-start.69) | collective-permute-done | bytes 966688 | tf_op jit(solution)/shard_map/ppermute | solution.py:590
  714.2 13.7 %collective-permute-done.72 = bf16[1888,128]{1,0:T(8,128)(2,1)S(1)} collective-permute-done((bf16[1888,128]{1,0:T(8,128)(2,1)S(1)}, bf16[1888,128]{1,0:T(8,128)(2,1)S(1)}, u32[]{:S(2)}, u32[]{:S(2)}) %collective-permute-start.72) | collective-permute-done | bytes 483360 | tf_op jit(solution)/shard_map/ppermute | solution.py:590
  737.9 19.9 %collective-permute-done.68 = bf16[1888,128]{1,0:T(8,128)(2,1)S(1)} collective-permute-done((bf16[1888,128]{1,0:T(8,128)(2,1)S(1)}, bf16[1888,128]{1,0:T(8,128)(2,1)S(1)}, u32[]{:S(2)}, u32[]{:S(2)}) %collective-permute-start.68) | collective-permute-done | bytes 483360 | tf_op jit(solution)/shard_map/ppermute | solution.py:590
  771.3 9.3 %finish.1 = (f32[1,476288]{1,0:T(1,128)}, f32[1,476288]{1,0:T(1,128)}, f32[1,476288]{1,0:T(1,128)}, f32[1,476288]{1,0:T(1,128)}) custom-call(s32[2]{0:T(128)} %pad_add_fusion.1.place, bf16[3776,128]{1,0:T(8,128)(2,1)} %bitcast.141, bf16[1344,128]{1,0:T(8,128)(2,1)} %add_convert_fusion.19.rest, f32[128,128]{1,0:T(8,128)} %add.312.vector, f32[1,476288]{1,0:T(1,128)} %master.1, ...), custom_call_target="tpu_custom_call" | custom-call | tf_op jit(solution)/shard_map/finish/pallas_call | solution.py:784
  (393 shorter events, 271.5 us)
Async XLA Ops:
  80.5 49.6 %collective-permute-start.33 = (bf16[2832,128]{1,0:T(8,128)(2,1)S(1)}, bf16[2832,128]{1,0:T(8,128)(2,1)S(1)}, u32[]{:S(2)}, u32[]{:S(2)}) collective-permute-start(bf16[2832,128]{1,0:T(8,128)(2,1)S(1)} %bitcast.146), channel_id=1, source_target_pairs={{0,2},{1,3},{2,0},{3,1},{4,6},{5,7},{6,4},{7,5},{8,10},{9,11},{10,... | collective-permute-start | bytes 2174984 | tf_op jit(solution)/shard_map/ppermute | solution.py:590
  82.9 62.7 %collective-permute-start.34 = (bf16[2832,128]{1,0:T(8,128)(2,1)S(1)}, bf16[2832,128]{1,0:T(8,128)(2,1)S(1)}, u32[]{:S(2)}, u32[]{:S(2)}) collective-permute-start(bf16[2832,128]{1,0:T(8,128)(2,1)S(1)} %collective-permute-done.32), channel_id=1, source_target_pairs={{0,2},{1,3},{2,0},{3,1},{4,6},{5,7},{6,4},{7,5},{8,10},{9,11},{10,... | collective-permute-start | bytes 2174984 | tf_op jit(solution)/shard_map/ppermute | solution.py:590
  95.1 52.2 %collective-permute-start.18 = (bf16[1888,128]{1,0:T(8,128)(2,1)S(1)}, bf16[1888,128]{1,0:T(8,128)(2,1)S(1)}, u32[]{:S(2)}, u32[]{:S(2)}) collective-permute-start(bf16[1888,128]{1,0:T(8,128)(2,1)S(1)} %collective-permute-done.7.refs_1_), channel_id=1, source_target_pairs={{0,4},{4,0},{8,12},{12,8},{16,20},{20,16},{24,28},{28,24},{1,5},{5... | collective-permute-start | bytes 1449992 | tf_op jit(solution)/shard_map/ppermute | solution.py:590
  96.9 51.9 %collective-permute-start.19 = (bf16[1888,128]{1,0:T(8,128)(2,1)S(1)}, bf16[1888,128]{1,0:T(8,128)(2,1)S(1)}, u32[]{:S(2)}, u32[]{:S(2)}) collective-permute-start(bf16[1888,128]{1,0:T(8,128)(2,1)S(1)} %collective-permute-done.8.refs_2_), channel_id=1, source_target_pairs={{0,4},{4,0},{8,12},{12,8},{16,20},{20,16},{24,28},{28,24},{1,5},{5... | collective-permute-start | bytes 1449992 | tf_op jit(solution)/shard_map/ppermute | solution.py:590
  97.0 35.4 %collective-permute-start.15 = (bf16[944,128]{1,0:T(8,128)(2,1)S(1)}, bf16[944,128]{1,0:T(8,128)(2,1)S(1)}, u32[]{:S(2)}, u32[]{:S(2)}) collective-permute-start(bf16[944,128]{1,0:T(8,128)(2,1)S(1)} %slice.343), channel_id=1, source_target_pairs={{0,16},{4,20},{8,24},{12,28},{16,0},{20,4},{24,8},{28,12},{1,17},{... | collective-permute-start | bytes 725000 | tf_op jit(solution)/shard_map/ppermute | solution.py:590
  147.3 64.8 %collective-permute-start.35 = (bf16[11328,128]{1,0:T(8,128)(2,1)}, bf16[11328,128]{1,0:T(8,128)(2,1)}, u32[]{:S(2)}, u32[]{:S(2)}) collective-permute-start(bf16[11328,128]{1,0:T(8,128)(2,1)} %constant_dynamic-update-slice_fusion.2.refs_0_), channel_id=1, source_target_pairs={{0,8},{4,12},{8,0},{12,4},{16,24},{20,28},{24,16},{28,20},{1,9},{5... | collective-permute-start | bytes 8699912 | tf_op jit(solution)/shard_map/ppermute | solution.py:590
  148.8 67.9 %collective-permute-start.36 = (bf16[11328,128]{1,0:T(8,128)(2,1)}, bf16[11328,128]{1,0:T(8,128)(2,1)}, u32[]{:S(2)}, u32[]{:S(2)}) collective-permute-start(bf16[11328,128]{1,0:T(8,128)(2,1)} %constant_dynamic-update-slice_fusion.2.refs_0_), channel_id=1, source_target_pairs={{0,16},{4,20},{8,24},{12,28},{16,0},{20,4},{24,8},{28,12},{1,17},{... | collective-permute-start | bytes 8699912 | tf_op jit(solution)/shard_map/ppermute | solution.py:590
  176.9 76.4 %all-to-all-start.1 = ((bf16[4,256,864]{1,2,0:T(8,128)(2,1)}), bf16[4,256,864]{1,2,0:T(8,128)(2,1)S(1)}, u32[]{:S(2)}, u32[]{:S(2)}) async-start(bf16[4,256,864]{1,2,0:T(8,128)(2,1)} %bitcast.137), calls=%async_computation.1 | async-start | bytes 3538944 | tf_op jit(solution)/shard_map/all_to_all | solution.py:575
  192.1 84.8 %collective-permute-start.39 = (bf16[11328,128]{1,0:T(8,128)(2,1)}, bf16[11328,128]{1,0:T(8,128)(2,1)}, u32[]{:S(2)}, u32[]{:S(2)}) collective-permute-start(bf16[11328,128]{1,0:T(8,128)(2,1)} %constant_dynamic-update-slice_fusion.2.refs_0_), channel_id=1, source_target_pairs={{0,4},{4,0},{8,12},{12,8},{16,20},{20,16},{24,28},{28,24},{1,5},{5... | collective-permute-start | bytes 8699912 | tf_op jit(solution)/shard_map/ppermute | solution.py:590
  213.6 33.3 %collective-permute-start.37 = (bf16[5664,128]{1,0:T(8,128)(2,1)S(1)}, bf16[5664,128]{1,0:T(8,128)(2,1)}, u32[]{:S(2)}, u32[]{:S(2)}) collective-permute-start(bf16[5664,128]{1,0:T(8,128)(2,1)S(1)} %slice.352), channel_id=1, source_target_pairs={{0,16},{4,20},{8,24},{12,28},{16,0},{20,4},{24,8},{28,12},{1,17},{... | collective-permute-start | bytes 4349960 | tf_op jit(solution)/shard_map/ppermute | solution.py:590
  215.5 61.4 %collective-permute-start.40 = (bf16[11328,128]{1,0:T(8,128)(2,1)}, bf16[11328,128]{1,0:T(8,128)(2,1)}, u32[]{:S(2)}, u32[]{:S(2)}) collective-permute-start(bf16[11328,128]{1,0:T(8,128)(2,1)} %collective-permute-done.35.refs_1_), channel_id=1, source_target_pairs={{0,4},{4,0},{8,12},{12,8},{16,20},{20,16},{24,28},{28,24},{1,5},{5... | collective-permute-start | bytes 8699912 | tf_op jit(solution)/shard_map/ppermute | solution.py:590
  218.2 58.8 %collective-permute-start.41 = (bf16[11328,128]{1,0:T(8,128)(2,1)}, bf16[11328,128]{1,0:T(8,128)(2,1)}, u32[]{:S(2)}, u32[]{:S(2)}) collective-permute-start(bf16[11328,128]{1,0:T(8,128)(2,1)} %collective-permute-done.36.refs_2_), channel_id=1, source_target_pairs={{0,4},{4,0},{8,12},{12,8},{16,20},{20,16},{24,28},{28,24},{1,5},{5... | collective-permute-start | bytes 8699912 | tf_op jit(solution)/shard_map/ppermute | solution.py:590
  218.2 33.1 %collective-permute-start.38 = (bf16[5664,128]{1,0:T(8,128)(2,1)S(1)}, bf16[5664,128]{1,0:T(8,128)(2,1)}, u32[]{:S(2)}, u32[]{:S(2)}) collective-permute-start(bf16[5664,128]{1,0:T(8,128)(2,1)S(1)} %slice.353), channel_id=1, source_target_pairs={{0,8},{4,12},{8,0},{12,4},{16,24},{20,28},{24,16},{28,20},{1,9},{5... | collective-permute-start | bytes 4349960 | tf_op jit(solution)/shard_map/ppermute | solution.py:590
  418.3 45.4 %all-to-all-start.4 = ((bf16[4,256,864]{1,2,0:T(8,128)(2,1)}), bf16[4,256,864]{1,2,0:T(8,128)(2,1)}, u32[]{:S(2)}, u32[]{:S(2)}) async-start(bf16[4,256,864]{1,2,0:T(8,128)(2,1)} %copy.22), calls=%async_computation.4 | async-start | bytes 3538944 | tf_op jit(solution)/shard_map/all_to_all | solution.py:583
  440.9 75.7 %collective-permute-start.54 = (bf16[15104,128]{1,0:T(8,128)(2,1)}, bf16[15104,128]{1,0:T(8,128)(2,1)}, u32[]{:S(2)}, u32[]{:S(2)}) collective-permute-start(bf16[15104,128]{1,0:T(8,128)(2,1)} %slice.372), channel_id=1, source_target_pairs={{0,4},{4,0},{8,12},{12,8},{16,20},{20,16},{24,28},{28,24},{1,5},{5... | collective-permute-start | bytes 11599880 | tf_op jit(solution)/shard_map/ppermute | solution.py:590
  490.4 63.5 %collective-permute-start.64 = (bf16[30208,128]{1,0:T(8,128)(2,1)}, bf16[30208,128]{1,0:T(8,128)(2,1)}, u32[]{:S(2)}, u32[]{:S(2)}) collective-permute-start(bf16[30208,128]{1,0:T(8,128)(2,1)} %slice.322), channel_id=1, source_target_pairs={{0,4},{4,0},{8,12},{12,8},{16,20},{20,16},{24,28},{28,24},{1,5},{5... | collective-permute-start | bytes 23199752 | tf_op jit(solution)/shard_map/ppermute | solution.py:590
  514.1 37.8 %collective-permute-start.44 = (bf16[15104,128]{1,0:T(8,128)(2,1)S(1)}, bf16[15104,128]{1,0:T(8,128)(2,1)S(1)}, u32[]{:S(2)}, u32[]{:S(2)}) collective-permute-start(bf16[15104,128]{1,0:T(8,128)(2,1)S(1)} %slice.294), channel_id=1, source_target_pairs={{0,4},{4,0},{8,12},{12,8},{16,20},{20,16},{24,28},{28,24},{1,5},{5... | collective-permute-start | bytes 11599880 | tf_op jit(solution)/shard_map/ppermute | solution.py:590
  523.0 36.1 %collective-permute-start.57 = (bf16[1888,128]{1,0:T(8,128)(2,1)}, bf16[1888,128]{1,0:T(8,128)(2,1)S(1)}, u32[]{:S(2)}, u32[]{:S(2)}) collective-permute-start(bf16[1888,128]{1,0:T(8,128)(2,1)} %get-tuple-element.69), channel_id=1, source_target_pairs={{0,16},{4,20},{8,24},{12,28},{16,0},{20,4},{24,8},{28,12},{1,17},{... | collective-permute-start | bytes 1449992 | tf_op jit(solution)/shard_map/ppermute | solution.py:590
  526.3 52.4 %collective-permute-start.60 = (bf16[1888,128]{1,0:T(8,128)(2,1)}, bf16[1888,128]{1,0:T(8,128)(2,1)S(1)}, u32[]{:S(2)}, u32[]{:S(2)}) collective-permute-start(bf16[1888,128]{1,0:T(8,128)(2,1)} %get-tuple-element.67), channel_id=1, source_target_pairs={{0,8},{4,12},{8,0},{12,4},{16,24},{20,28},{24,16},{28,20},{1,9},{5... | collective-permute-start | bytes 1449992 | tf_op jit(solution)/shard_map/ppermute | solution.py:590
  551.9 55.6 %collective-permute-start.77 = (bf16[1344,128]{1,0:T(8,128)(2,1)S(1)}, bf16[1344,128]{1,0:T(8,128)(2,1)S(1)}, u32[]{:S(2)}, u32[]{:S(2)}) collective-permute-start(bf16[1344,128]{1,0:T(8,128)(2,1)S(1)} %add_convert_fusion.21), channel_id=1, source_target_pairs={{10,8},{11,9}} | collective-permute-start | bytes 1032200 | tf_op jit(solution)/shard_map/ppermute | solution.py:691
  559.1 42.3 %collective-permute-start.65 = (bf16[3776,128]{1,0:T(8,128)(2,1)S(1)}, bf16[3776,128]{1,0:T(8,128)(2,1)S(1)}, u32[]{:S(2)}, u32[]{:S(2)}) collective-permute-start(bf16[3776,128]{1,0:T(8,128)(2,1)S(1)} %get-tuple-element.52), channel_id=1, source_target_pairs={{0,16},{4,20},{8,24},{12,28},{16,0},{20,4},{24,8},{28,12},{1,17},{... | collective-permute-start | bytes 2899976 | tf_op jit(solution)/shard_map/ppermute | solution.py:590
  579.1 32.7 %collective-permute-start.47 = (bf16[1888,128]{1,0:T(8,128)(2,1)S(1)}, bf16[1888,128]{1,0:T(8,128)(2,1)S(1)}, u32[]{:S(2)}, u32[]{:S(2)}) collective-permute-start(bf16[1888,128]{1,0:T(8,128)(2,1)S(1)} %get-tuple-element.63), channel_id=1, source_target_pairs={{0,16},{4,20},{8,24},{12,28},{16,0},{20,4},{24,8},{28,12},{1,17},{... | collective-permute-start | bytes 1449992 | tf_op jit(solution)/shard_map/ppermute | solution.py:590
  580.5 32.5 %collective-permute-start.50 = (bf16[1888,128]{1,0:T(8,128)(2,1)S(1)}, bf16[1888,128]{1,0:T(8,128)(2,1)S(1)}, u32[]{:S(2)}, u32[]{:S(2)}) collective-permute-start(bf16[1888,128]{1,0:T(8,128)(2,1)S(1)} %get-tuple-element.61), channel_id=1, source_target_pairs={{0,8},{4,12},{8,0},{12,4},{16,24},{20,28},{24,16},{28,20},{1,9},{5... | collective-permute-start | bytes 1449992 | tf_op jit(solution)/shard_map/ppermute | solution.py:590
  581.7 59.3 %collective-permute-start.67 = (bf16[3776,128]{1,0:T(8,128)(2,1)S(1)}, bf16[3776,128]{1,0:T(8,128)(2,1)S(1)}, u32[]{:S(2)}, u32[]{:S(2)}) collective-permute-start(bf16[3776,128]{1,0:T(8,128)(2,1)S(1)} %get-tuple-element.55), channel_id=1, source_target_pairs={{0,16},{4,20},{8,24},{12,28},{16,0},{20,4},{24,8},{28,12},{1,17},{... | collective-permute-start | bytes 2899976 | tf_op jit(solution)/shard_map/ppermute | solution.py:590
  601.4 40.8 %collective-permute-start.70 = (bf16[3776,128]{1,0:T(8,128)(2,1)S(1)}, bf16[3776,128]{1,0:T(8,128)(2,1)S(1)}, u32[]{:S(2)}, u32[]{:S(2)}) collective-permute-start(bf16[3776,128]{1,0:T(8,128)(2,1)S(1)} %get-tuple-element.53), channel_id=1, source_target_pairs={{0,8},{4,12},{8,0},{12,4},{16,24},{20,28},{24,16},{28,20},{1,9},{5... | collective-permute-start | bytes 2899976 | tf_op jit(solution)/shard_map/ppermute | solution.py:590
  607.5 32.8 %collective-permute-start.46 = (bf16[1888,128]{1,0:T(8,128)(2,1)S(1)}, bf16[1888,128]{1,0:T(8,128)(2,1)S(1)}, u32[]{:S(2)}, u32[]{:S(2)}) collective-permute-start(bf16[1888,128]{1,0:T(8,128)(2,1)S(1)} %add_convert_fusion.18), channel_id=1, source_target_pairs={{0,8},{4,12},{8,0},{12,4},{16,24},{20,28},{24,16},{28,20},{1,9},{5... | collective-permute-start | bytes 1449992 | tf_op jit(solution)/shard_map/ppermute | solution.py:590
  611.8 49.3 %collective-permute-start.66 = (bf16[3776,128]{1,0:T(8,128)(2,1)S(1)}, bf16[3776,128]{1,0:T(8,128)(2,1)S(1)}, u32[]{:S(2)}, u32[]{:S(2)}) collective-permute-start(bf16[3776,128]{1,0:T(8,128)(2,1)S(1)} %add_convert_fusion.6), channel_id=1, source_target_pairs={{0,8},{4,12},{8,0},{12,4},{16,24},{20,28},{24,16},{28,20},{1,9},{5... | collective-permute-start | bytes 2899976 | tf_op jit(solution)/shard_map/ppermute | solution.py:590
  613.1 152.2 %collective-permute-start.83 = (f32[128,128]{1,0:T(8,128)S(1)}, f32[128,128]{1,0:T(8,128)}, u32[]{:S(2)}, u32[]{:S(2)}) collective-permute-start(f32[128,128]{1,0:T(8,128)S(1)} %add.311), channel_id=1, source_target_pairs={{30,31}} | collective-permute-start | bytes 196616 | tf_op jit(solution)/shard_map/ppermute | solution.py:691
  641.0 31.5 %collective-permute-start.61 = (bf16[1888,128]{1,0:T(8,128)(2,1)S(1)}, bf16[1888,128]{1,0:T(8,128)(2,1)S(1)}, u32[]{:S(2)}, u32[]{:S(2)}) collective-permute-start(bf16[1888,128]{1,0:T(8,128)(2,1)S(1)} %get-tuple-element.65), channel_id=1, source_target_pairs={{0,16},{4,20},{8,24},{12,28},{16,0},{20,4},{24,8},{28,12},{1,17},{... | collective-permute-start | bytes 1449992 | tf_op jit(solution)/shard_map/ppermute | solution.py:590
  642.2 39.6 %collective-permute-start.49 = (bf16[1888,128]{1,0:T(8,128)(2,1)S(1)}, bf16[1888,128]{1,0:T(8,128)(2,1)S(1)}, u32[]{:S(2)}, u32[]{:S(2)}) collective-permute-start(bf16[1888,128]{1,0:T(8,128)(2,1)S(1)} %get-tuple-element.62), channel_id=1, source_target_pairs={{0,8},{4,12},{8,0},{12,4},{16,24},{20,28},{24,16},{28,20},{1,9},{5... | collective-permute-start | bytes 1449992 | tf_op jit(solution)/shard_map/ppermute | solution.py:590
  661.0 41.4 %collective-permute-start.69 = (bf16[3776,128]{1,0:T(8,128)(2,1)S(1)}, bf16[3776,128]{1,0:T(8,128)(2,1)S(1)}, u32[]{:S(2)}, u32[]{:S(2)}) collective-permute-start(bf16[3776,128]{1,0:T(8,128)(2,1)S(1)} %get-tuple-element.54), channel_id=1, source_target_pairs={{0,8},{4,12},{8,0},{12,4},{16,24},{20,28},{24,16},{28,20},{1,9},{5... | collective-permute-start | bytes 2899976 | tf_op jit(solution)/shard_map/ppermute | solution.py:590
  681.7 46.4 %collective-permute-start.58 = (bf16[944,128]{1,0:T(8,128)(2,1)S(1)}, bf16[944,128]{1,0:T(8,128)(2,1)S(1)}, u32[]{:S(2)}, u32[]{:S(2)}) collective-permute-start(bf16[944,128]{1,0:T(8,128)(2,1)S(1)} %slice.378), channel_id=1, source_target_pairs={{0,1},{1,0},{2,3},{3,2},{4,5},{5,4},{6,7},{7,6},{8,9},{9,8},{10,11... | collective-permute-start | bytes 725000 | tf_op jit(solution)/shard_map/ppermute | solution.py:590
  (115 other events, 2279.9 us)

commit v3 on v2

--- a/solution.py
+++ b/solution.py
@@ -148,15 +148,13 @@
 
 def fetch(layout, place, groups, origin, sources, flat, sem):
     low, high = groups
-    count = high - low
-    for ref, (column, core, first_row, members) in sources:
+    for ref, (column, core, key) in sources:
         device_column = jnp.bitwise_xor(place[0], column)
         device_core = jnp.bitwise_xor(place[1], core)
-
-        def body(index, _, ref=ref, first_row=first_row):
-            row = jnp.bitwise_xor(place[2], first_row + index // count)
-            group = low + index % count
-            shard = group * layout.group_shards + device_core * layout.ctx + row
+        row = jnp.bitwise_xor(place[2], key)
+
+        def body(index, _, ref=ref, device_column=device_column, device_core=device_core, row=row):
+            shard = (low + index) * layout.group_shards + device_core * layout.ctx + row
             start = shard * layout.rows // TILE * TILE
             target = pl.multiple_of(start + device_column * layout.piece - origin, TILE)
             source = pl.multiple_of(index * layout.piece, TILE)
@@ -185,7 +183,7 @@
 
             return 0
 
-        lax.fori_loop(0, members * count, body, 0)
+        lax.fori_loop(0, high - low, body, 0)
 
 
 def flat_of(gathered):
@@ -309,7 +307,7 @@
     end = max([high] + [first + (b + n) * stride for first, b, n, stride in plan.values()])
     steps = max(n for _, _, n, _ in plan.values())
     covered = min(first + b * stride for first, b, _, stride in plan.values())
-    rows = layout.devices * count * layout.piece
+    rows = layout.devices // 2 * count * layout.piece
     extra = ROW_OUT - layout.group_start(layout.first)
 
     def kernel(place_ref, *refs):
@@ -348,25 +346,26 @@
                 group = groups[0] + index % count
                 key = index // count
                 row = jnp.bitwise_xor(place_ref[2], key % layout.ctx)
-                key = key // layout.ctx
-                column = jnp.bitwise_xor(place_ref[0], key % layout.columns)
-                core = jnp.bitwise_xor(place_ref[1], key // layout.columns)
-                shard = group * layout.group_shards + core * layout.ctx + row
-                start = shard * layout.rows // TILE * TILE
-                source = pl.multiple_of(start + column * layout.piece - origin, TILE)
-                target = pl.multiple_of(index * layout.piece, TILE)
-                pltpu.make_async_copy(
-                    flat.at[pl.ds(source, layout.piece), :],
-                    outputs[0].at[pl.ds(target, layout.piece), :],
-                    sem,
-                ).start()
+                column = jnp.bitwise_xor(place_ref[0], key // layout.ctx)
+                for bit in range(2):
+                    core = jnp.bitwise_xor(place_ref[1], bit)
+                    shard = group * layout.group_shards + core * layout.ctx + row
+                    start = shard * layout.rows // TILE * TILE
+                    source = pl.multiple_of(start + column * layout.piece - origin, TILE)
+                    target = pl.multiple_of(index * layout.piece, TILE)
+                    pltpu.make_async_copy(
+                        flat.at[pl.ds(source, layout.piece), :],
+                        outputs[bit].at[pl.ds(target, layout.piece), :],
+                        sem,
+                    ).start()
                 return 0
 
-            lax.fori_loop(0, layout.devices * count, body, 0)
+            lax.fori_loop(0, layout.devices // 2 * count, body, 0)
             pltpu.make_async_copy(outputs[0], outputs[0], sem).wait()
+            pltpu.make_async_copy(outputs[1], outputs[1], sem).wait()
             if leftover:
                 copy = pltpu.make_async_copy(
-                    flat.at[pl.ds(ROW_OUT - extra - origin, extra), :], outputs[1], sem
+                    flat.at[pl.ds(ROW_OUT - extra - origin, extra), :], outputs[2], sem
                 )
                 copy.start()
                 copy.wait()
@@ -378,7 +377,7 @@
             (height, width), lambda i: (block + jnp.minimum(i, number - 1), 0)
         )
 
-    shapes = [jax.ShapeDtypeStruct((rows, LANES), BF)]
+    shapes = [jax.ShapeDtypeStruct((rows, LANES), BF)] * 2
     if leftover:
         shapes.append(jax.ShapeDtypeStruct((extra, LANES), BF))
     wide_rows = max(stride for _, _, _, stride in plan.values())
@@ -415,23 +414,39 @@
     return jnp.where(columns < count, scores, masked_score)
 
 
-def unpack_heads(source, parts, heads, held):
-    for part in range(parts):
-        for head in range(heads):
-            first = (part * heads + head) * HD
-            held[part, head] = source[:, first : first + HD]
-
-
-def attend(counts, packed, chunk):
-    length, width = packed.shape
-    heads = width // (3 * HD)
-
-    def kernel(count, source, mixed, log_total, held, made):
+def unpack_heads(place, blocks, parts, heads, held):
+    for key, block in enumerate(blocks):
+        rows = block.shape[0]
+        row = pl.multiple_of(jnp.bitwise_xor(place[2], key) * rows, TILE)
+        for part in range(parts):
+            for head in range(heads):
+                first = (part * heads + head) * HD
+                held[part, head, pl.ds(row, rows), :] = block[:, first : first + HD]
+
+
+def pack_heads(place, held, parts, heads, blocks):
+    for key, block in enumerate(blocks):
+        rows = block.shape[0]
+        row = pl.multiple_of(jnp.bitwise_xor(place[2], key) * rows, TILE)
+        block[...] = jnp.concatenate(
+            [held[part, head, pl.ds(row, rows), :] for part in range(parts) for head in range(heads)],
+            -1,
+        )
+
+
+def attend(counts, place, blocks, chunk):
+    rows, width = blocks[0].shape
+    heads, ctx = (width // (3 * HD), len(blocks))
+    length = rows * ctx
+
+    def kernel(count, place_ref, *refs):
+        sources, mixed = (refs[:ctx], refs[ctx : 2 * ctx])
+        log_total, held, made = refs[2 * ctx :]
         head = pl.program_id(0)
 
         @pl.when(head == 0)
         def _():
-            unpack_heads(source, 3, heads, held)
+            unpack_heads(place_ref, sources, 3, heads, held)
 
         for first in range(0, length, chunk):
             queries = held[0, head, pl.ds(first, chunk), :]
@@ -440,49 +455,47 @@
             exponent = jnp.exp(scores - top)
             total = jnp.sum(exponent, -1, keepdims=True)
             probs = (exponent / total).astype(BF)
-            made[head, pl.ds(first, chunk), :] = dense(probs, held[2, head]).astype(BF)
+            made[0, head, pl.ds(first, chunk), :] = dense(probs, held[2, head]).astype(BF)
             log_total[0, first : first + chunk, :] = top + jnp.log(total)
 
         @pl.when(head == heads - 1)
         def _():
-            mixed[...] = jnp.concatenate([made[index] for index in range(heads)], -1)
-
-    return pl.pallas_call(
+            pack_heads(place_ref, made, 1, heads, mixed)
+
+    outputs = pl.pallas_call(
         kernel,
         name="attend",
         grid=(heads,),
-        in_specs=[
-            pl.BlockSpec(memory_space=pltpu.SMEM),
-            pl.BlockSpec((length, width), lambda h: (0, 0)),
-        ],
-        out_specs=[
-            pl.BlockSpec((length, heads * HD), lambda h: (0, 0)),
-            pl.BlockSpec((1, length, 1), lambda h: (h, 0, 0)),
-        ],
-        out_shape=[
-            jax.ShapeDtypeStruct((length, heads * HD), BF),
-            jax.ShapeDtypeStruct((heads, length, 1), F32),
-        ],
+        in_specs=[pl.BlockSpec(memory_space=pltpu.SMEM)] * 2
+        + [pl.BlockSpec((rows, width), lambda h: (0, 0))] * ctx,
+        out_specs=[pl.BlockSpec((rows, heads * HD), lambda h: (0, 0))] * ctx
+        + [pl.BlockSpec((1, length, 1), lambda h: (h, 0, 0))],
+        out_shape=[jax.ShapeDtypeStruct((rows, heads * HD), BF)] * ctx
+        + [jax.ShapeDtypeStruct((heads, length, 1), F32)],
         scratch_shapes=[
             pltpu.VMEM((3, heads, length, HD), BF),
-            pltpu.VMEM((heads, length, HD), BF),
+            pltpu.VMEM((1, heads, length, HD), BF),
         ],
         compiler_params=pltpu.CompilerParams(vmem_limit_bytes=VMEM_LIMIT),
-    )(counts, packed)
-
-
-def attend_back(counts, packed, log_total, grad_mixed, chunk):
-    length, width = packed.shape
-    heads = width // (3 * HD)
+    )(counts, place, *blocks)
+    return outputs[:ctx], outputs[ctx]
+
+
+def attend_back(counts, place, blocks, log_total, grad_blocks, chunk):
+    rows, width = blocks[0].shape
+    heads, ctx = (width // (3 * HD), len(blocks))
+    length = rows * ctx
     scale = HD ** (-0.5)
 
-    def kernel(count, source, logs, grad_source, made, sums, held, grad, results, acc_k, acc_v):
+    def kernel(count, place_ref, logs, *refs):
+        sources, grads, made = (refs[:ctx], refs[ctx : 2 * ctx], refs[2 * ctx : 3 * ctx])
+        sums, held, grad, results, acc_k, acc_v = refs[3 * ctx :]
         head = pl.program_id(0)
 
         @pl.when(head == 0)
         def _():
-            unpack_heads(source, 3, heads, held)
-            unpack_heads(grad_source, 1, heads, grad)
+            unpack_heads(place_ref, sources, 3, heads, held)
+            unpack_heads(place_ref, grads, 1, heads, grad)
 
         acc_k[...] = jnp.zeros_like(acc_k)
         acc_v[...] = jnp.zeros_like(acc_v)
@@ -508,28 +521,20 @@
 
         @pl.when(head == heads - 1)
         def _():
-            made[...] = jnp.concatenate(
-                [results[part, index] for part in range(3) for index in range(heads)], -1
-            )
-
-    return pl.pallas_call(
+            pack_heads(place_ref, results, 3, heads, made)
+
+    wide = pl.BlockSpec((rows, width), lambda h: (0, 0))
+    outputs = pl.pallas_call(
         kernel,
         name="attend_back",
         grid=(heads,),
-        in_specs=[
-            pl.BlockSpec(memory_space=pltpu.SMEM),
-            pl.BlockSpec((length, width), lambda h: (0, 0)),
-            pl.BlockSpec((1, length, 1), lambda h: (h, 0, 0)),
-            pl.BlockSpec((length, heads * HD), lambda h: (0, 0)),
-        ],
-        out_specs=[
-            pl.BlockSpec((length, width), lambda h: (0, 0)),
-            pl.BlockSpec((1, 2, HD), lambda h: (h, 0, 0)),
-        ],
-        out_shape=[
-            jax.ShapeDtypeStruct((length, width), BF),
-            jax.ShapeDtypeStruct((heads, 2, HD), F32),
-        ],
+        in_specs=[pl.BlockSpec(memory_space=pltpu.SMEM)] * 2
+        + [pl.BlockSpec((1, length, 1), lambda h: (h, 0, 0))]
+        + [wide] * ctx
+        + [pl.BlockSpec((rows, heads * HD), lambda h: (0, 0))] * ctx,
+        out_specs=[wide] * ctx + [pl.BlockSpec((1, 2, HD), lambda h: (h, 0, 0))],
+        out_shape=[jax.ShapeDtypeStruct((rows, width), BF)] * ctx
+        + [jax.ShapeDtypeStruct((heads, 2, HD), F32)],
         scratch_shapes=[
             pltpu.VMEM((3, heads, length, HD), BF),
             pltpu.VMEM((1, heads, length, HD), BF),
@@ -538,7 +543,8 @@
             pltpu.VMEM((length, HD), F32),
         ],
         compiler_params=pltpu.CompilerParams(vmem_limit_bytes=VMEM_LIMIT),
-    )(counts, packed, log_total, grad_mixed)
+    )(counts, place, log_total, *blocks, *grad_blocks)
+    return outputs[:ctx], outputs[ctx]
 
 
 def norm_forward(residual):
@@ -567,91 +573,109 @@
     return (updated, first_new, second_new)
 
 
+def exchange(array, axis, bit):
+    size = lax.axis_size(axis)
+    return lax.ppermute(array, axis, [(index, index ^ bit) for index in range(size)])
+
+
+def pick(index, choices):
+    picked = choices[0]
+    for position, choice in enumerate(choices[1:], 1):
+        picked = jnp.where(index == position, choice, picked)
+    return picked
+
+
 def to_heads(array, parts):
     ctx = lax.axis_size("ctx")
     rows = array.shape[0]
     split = array.reshape(rows, parts, ctx, D // ctx).transpose(2, 0, 1, 3)
     split = split.reshape(ctx, rows, parts * D // ctx)
-    held = lax.all_to_all(split, "ctx", split_axis=0, concat_axis=0, tiled=True)
-    return held.reshape(rows * ctx, parts * D // ctx)
-
-
-def from_heads(array, parts):
-    ctx = lax.axis_size("ctx")
-    length = array.shape[0]
-    split = array.reshape(ctx, length // ctx, parts * D // ctx)
-    held = lax.all_to_all(split, "ctx", split_axis=0, concat_axis=0, tiled=True)
-    held = held.reshape(ctx, length // ctx, parts, D // ctx)
-    return held.transpose(1, 2, 0, 3).reshape(length // ctx, parts * D)
-
-
-def exchange(array, axis, bit):
-    size = lax.axis_size(axis)
-    return lax.ppermute(array, axis, [(index, index ^ bit) for index in range(size)])
+    place = lax.axis_index("ctx")
+    blocks = [
+        lax.dynamic_index_in_dim(split, place ^ key, keepdims=False) for key in range(ctx)
+    ]
+    return blocks[:1] + [exchange(blocks[key], "ctx", key) for key in range(1, ctx)]
+
+
+def from_heads(blocks, parts):
+    ctx = len(blocks)
+    held = list(blocks[:1]) + [exchange(blocks[key], "ctx", key) for key in range(1, ctx)]
+    place = lax.axis_index("ctx")
+    ordered = [
+        pick(place, [held[index ^ position] for position in range(ctx)]) for index in range(ctx)
+    ]
+    share = D // ctx
+    return jnp.concatenate(
+        [block[:, part * share : (part + 1) * share] for part in range(parts) for block in ordered],
+        -1,
+    )
 
 
 def add(*arrays):
     return functools.reduce(jnp.add, [array.astype(F32) for array in arrays]).astype(BF)
 
 
-def gather(layout, share, batches):
+def gather(layout, share, behind=None):
     held = {0: share}
     bit = 1
     while bit < layout.ctx:
         held.update({key ^ bit: exchange(held[key], "ctx", bit) for key in list(held)})
         bit *= 2
     arrays = []
-    members = layout.ctx // batches
-    for batch in range(batches):
-        first = batch * members
-        stack = jnp.concatenate([held[key] for key in range(first, first + members)])
-        found = [(stack, (0, 0, first, members))]
+    for key in range(layout.ctx):
+        own = held[key]
+        if behind is not None:
+            own = lax.optimization_barrier((own, behind))[0]
+        found = [(own, (0, 0, key))]
         if layout.columns == 4:
-            middle, half = (stack.shape[0] // 2, members // 2)
-            by_x = exchange(stack, "dp", 2)
-            by_y = exchange(stack, "dp", 4)
-            found += [(by_x, (1, 0, first, members)), (by_y, (2, 0, first, members))]
-            across = exchange(by_x[:middle], "dp", 4)
-            found.append((across, (3, 0, first, half)))
-            across = exchange(by_y[middle:], "dp", 2)
-            found.append((across, (3, 0, first + half, half)))
+            by_x = exchange(own, "dp", 2)
+            by_y = exchange(own, "dp", 4)
+            if key % 2:
+                across = exchange(by_y, "dp", 2)
+            else:
+                across = exchange(by_x, "dp", 4)
+            found += [(by_x, (1, 0, key)), (by_y, (2, 0, key)), (across, (3, 0, key))]
         else:
             bit = 1
             while bit < layout.columns:
                 found += [
-                    (exchange(array, "dp", 2 * bit), (place[0] ^ bit,) + place[1:])
+                    (exchange(array, "dp", 2 * bit), (place[0] ^ bit, 0, key))
                     for array, place in found
                 ]
                 bit *= 2
         arrays += found
-    arrays += [(exchange(array, "dp", 1), (place[0], 1) + place[2:]) for array, place in arrays]
-    return arrays, held[layout.ctx - 1]
-
-
-def scatter(layout, pieces):
-    middle = pieces.shape[0] // 2
-    kept = add(pieces[:middle], exchange(pieces[middle:], "dp", 1))
-    size = middle // layout.columns
-    parts = [kept[index * size : (index + 1) * size] for index in range(layout.columns)]
-    half = size // 2
+    last = arrays[-2][0]
+    arrays += [(exchange(array, "dp", 1), (place[0], 1, place[2])) for array, place in arrays]
+    return arrays, held[layout.ctx - 1], last
+
+
+def scatter(layout, kept, sent):
+    received = exchange(sent, "dp", 1)
+    half = kept.shape[0] // layout.columns // 2
+    parts = lax.optimization_barrier(
+        [
+            add(kept[index * half : (index + 1) * half], received[index * half : (index + 1) * half])
+            for index in range(2 * layout.columns)
+        ]
+    )
     if layout.columns == 4:
-        low = add(parts[1][:half], exchange(parts[3][:half], "dp", 4))
-        high = add(parts[2][half:], exchange(parts[3][half:], "dp", 2))
-        summed = [
-            add(parts[0][:half], exchange(low, "dp", 2), exchange(parts[2][:half], "dp", 4)),
-            add(parts[0][half:], exchange(parts[1][half:], "dp", 2), exchange(high, "dp", 4)),
-        ]
+        low = add(parts[2], exchange(parts[6], "dp", 4))
+        high = add(parts[5], exchange(parts[7], "dp", 2))
+        over_x = exchange(parts[3], "dp", 2)
+        over_y = exchange(parts[4], "dp", 4)
+        low, high = (exchange(low, "dp", 2), exchange(high, "dp", 4))
+        summed = [add(parts[0], low, over_y), add(parts[1], over_x, high)]
     else:
-        bit = layout.columns // 2
-        while bit:
+        bit = layout.columns
+        while bit > 1:
             parts = [
-                add(parts[index], exchange(parts[index ^ bit], "dp", 2 * bit))
+                add(parts[index], exchange(parts[index ^ bit], "dp", bit))
                 for index in range(bit)
             ]
             bit //= 2
-        summed = [parts[0][:half], parts[0][half:]]
+        summed = parts
     each = layout.ctx // 2
-    length = size // layout.ctx
+    length = half // each
     held = {
         key: summed[key // each][(key % each) * length : (key % each + 1) * length]
         for key in range(layout.ctx)
@@ -694,19 +718,19 @@
     return held
 
 
-def column_groups(layout):
-    return [[column * 2 + core for column in range(layout.columns)] for core in range(2)]
-
-
 SWEEP = 512
 
 
-def align(layout, params, before, offset):
+def align(layout, place, params, before):
     length = layout.columns * layout.piece
     steps = pl.cdiv(layout.rows, SWEEP)
     held = max(TILE + steps * SWEEP, TILE + length)
-
-    def kernel(offset_ref, rows, previous, chunk, wide):
+    vector_first = ROW_VEC - layout.start(layout.devices - 1)
+    assert 0 <= vector_first and vector_first + VEC_ROWS <= length
+    starts = max(rows for _, rows in layout.leftover())
+
+    def kernel(place_ref, rows, previous, *refs):
+        outputs, wide = (refs[:-1], refs[-1])
         step = pl.program_id(0)
 
         @pl.when(step == 0)
@@ -718,8 +742,14 @@
 
         @pl.when(step == steps - 1)
         def _():
-            chunk[...] = wide[pl.ds(TILE - offset_ref[0], length), :].astype(BF)
-
+            first = TILE - place_ref[3]
+            for key in range(layout.columns):
+                row = first + jnp.bitwise_xor(place_ref[0], key) * layout.piece
+                outputs[key][...] = wide[pl.ds(row, layout.piece), :].astype(BF)
+            outputs[-2][...] = wide[pl.ds(first, starts), :].astype(BF)
+            outputs[-1][...] = wide[pl.ds(first + vector_first, VEC_ROWS), :].astype(BF)
+
+    heights = [layout.piece] * layout.columns + [starts, VEC_ROWS]
     return pl.pallas_call(
         kernel,
         name="align",
@@ -729,26 +759,32 @@
             pl.BlockSpec((1, SWEEP * LANES), lambda i: (0, i)),
             pl.BlockSpec((TILE, LANES), lambda i: (0, 0)),
         ],
-        out_specs=pl.BlockSpec((length, LANES), lambda i: (0, 0)),
-        out_shape=jax.ShapeDtypeStruct((length, LANES), BF),
+        out_specs=[pl.BlockSpec((height, LANES), lambda i: (0, 0)) for height in heights],
+        out_shape=[jax.ShapeDtypeStruct((height, LANES), BF) for height in heights],
         scratch_shapes=[pltpu.VMEM((held, LANES), F32)],
         compiler_params=pltpu.CompilerParams(vmem_limit_bytes=VMEM_LIMIT),
-    )(offset, params, before)
-
-
-def finish(layout, where, chunk, leftover, vectors, params, first, second):
+    )(place, params, before)
+
+
+def finish(layout, place, pieces, leftover, vectors, params, first, second):
     length = layout.columns * layout.piece
     steps = pl.cdiv(layout.rows, SWEEP)
     held = max(length, TILE + steps * SWEEP)
     vector_first = ROW_VEC - layout.start(layout.devices - 1)
-
-    def kernel(place, sums, rest, vector, master, one, two, grads, new, new_one, new_two, wide):
+    columns = layout.columns
+
+    def kernel(place_ref, *refs):
+        sums, refs = (refs[:columns], refs[columns:])
+        rest, vector, master, one, two, grads, new, new_one, new_two, wide = refs
         step = pl.program_id(0)
-        shard = place[0]
+        shard = place_ref[4]
 
         @pl.when(step == 0)
         def _():
-            wide[pl.ds(0, length), :] = sums[...].astype(F32)
+            for key in range(columns):
+                row = jnp.bitwise_xor(place_ref[0], key) * layout.piece
+                row = pl.multiple_of(row, TILE)
+                wide[pl.ds(row, layout.piece), :] = sums[key][...].astype(F32)
             used = 0
             for owner, rows in layout.leftover():
 
@@ -762,12 +798,11 @@
             def _():
                 wide[pl.ds(vector_first, VEC_ROWS), :] += vector[...]
 
-        grad = wide[pl.ds(place[1] + step * SWEEP, SWEEP), :]
+        grad = wide[pl.ds(place_ref[3] + step * SWEEP, SWEEP), :]
         row = lax.broadcasted_iota(jnp.int32, (SWEEP, LANES), 0)
         matrix_part = row < ROW_VEC - shard * layout.rows - step * SWEEP
-        value = master[...].reshape(SWEEP, LANES)
         results = adam_update(
-            value,
+            master[...].reshape(SWEEP, LANES),
             grad,
             one[...].reshape(SWEEP, LANES),
             two[...].reshape(SWEEP, LANES),
@@ -785,57 +820,46 @@
         kernel,
         name="finish",
         grid=(steps,),
-        in_specs=[
-            pl.BlockSpec(memory_space=pltpu.SMEM),
-            whole(chunk),
-            whole(leftover),
-            whole(vectors),
-            flat,
-            flat,
-            flat,
-        ],
+        in_specs=[pl.BlockSpec(memory_space=pltpu.SMEM)]
+        + [whole(piece) for piece in pieces]
+        + [whole(leftover), whole(vectors), flat, flat, flat],
         out_specs=[flat] * 4,
         out_shape=[jax.ShapeDtypeStruct(params.shape, F32)] * 4,
         scratch_shapes=[pltpu.VMEM((held, LANES), F32)],
         compiler_params=pltpu.CompilerParams(vmem_limit_bytes=VMEM_LIMIT),
-    )(where, chunk, leftover, vectors, params, first, second)
+    )(place, *pieces, leftover, vectors, params, first, second)
 
 
 def shards(layout, inputs, counts, params, first_moment, second_moment, out_cotangent):
     local_rows = inputs.shape[1]
     shard = lax.axis_index(("dp", "ctx"))
     score_scale = HD ** (-0.5)
-    everyone = column_groups(layout)
     chunk = 256
 
+    column = lax.axis_index("dp") // 2
+    offset = (shard * layout.rows) % TILE
     place = jnp.stack(
-        [lax.axis_index("dp") // 2, lax.axis_index("dp") % 2, lax.axis_index("ctx")]
+        [column, lax.axis_index("dp") % 2, lax.axis_index("ctx"), offset, shard]
     ).astype(jnp.int32)
     last = layout.devices - 1
     ending = params[0, -TILE * LANES :].reshape(TILE, LANES)
     before = lax.ppermute(ending, ("dp", "ctx"), [(index, index + 1) for index in range(last)])
-    offset = ((shard * layout.rows) % TILE).astype(jnp.int32)
-    chunk_rows = align(layout, params, before, offset.reshape(1))
-    pieces = lax.all_to_all(
-        chunk_rows.reshape(layout.columns, layout.piece, LANES),
-        "dp",
-        split_axis=0,
-        concat_axis=0,
-        tiled=True,
-        axis_index_groups=everyone,
+    aligned = align(layout, place, params, before)
+    shares = list(aligned[:1]) + [
+        exchange(aligned[key], "dp", 2 * key) for key in range(1, layout.columns)
+    ]
+    groups = [
+        pick(column, [shares[index ^ position] for position in range(layout.columns)])
+        for index in range(layout.columns)
+    ]
+    gathered_first, along, behind = gather(layout, jnp.concatenate(groups[: layout.first]))
+    shared_rest = jnp.concatenate(groups[layout.first :])
+    shared_rest = lax.optimization_barrier((shared_rest, along))[0]
+    gathered_rest, _, _ = gather(layout, shared_rest, behind)
+    leftover = jnp.concatenate(
+        [broadcast(layout, shard, owner, aligned[-2][:rows]) for owner, rows in layout.leftover()]
     )
-    shared_first = pieces[: layout.first].reshape(-1, LANES)
-    gathered_first, along = gather(layout, shared_first, 2)
-    shared_rest = pieces[layout.first :].reshape(-1, LANES)
-    shared_rest = lax.optimization_barrier((shared_rest, along))[0]
-    gathered_rest, _ = gather(layout, shared_rest, 1)
-    vector_first = ROW_VEC - layout.start(last)
-    assert 0 <= vector_first and vector_first + VEC_ROWS <= layout.columns * layout.piece
-    leftover = jnp.concatenate(
-        [broadcast(layout, shard, owner, chunk_rows[:rows]) for owner, rows in layout.leftover()]
-    )
-    spread = chunk_rows[vector_first : vector_first + VEC_ROWS]
-    spread = broadcast(layout, shard, last, spread)
+    spread = broadcast(layout, shard, last, aligned[-1])
     flat_vectors = spread.reshape(-1).astype(F32)
     vectors = []
     used = 0
@@ -864,7 +888,7 @@
     values = (projected[:, 2 * D :] + bias_value).astype(BF)
     packed = to_heads(jnp.concatenate([queries, keys, values], -1), 3)
     out_weight, up_weight, down_weight = other_weights(layout, place, gathered_rest)
-    mixed_heads, log_total = attend(counts, packed, chunk)
+    mixed_heads, log_total = attend(counts, place, packed, chunk)
     mixed = from_heads(mixed_heads, 1)
     middle = residual + dense(mixed, out_weight) + bias_out
     unit_two, inverse_two = norm_forward(middle)
@@ -886,11 +910,11 @@
     grad_pre_round = grad_pre.astype(BF)
     grad_up = t_dot(normed_two_round, grad_pre_round).astype(BF)
     middle_group = layout.columns // 2
-    (terms,) = gradient_pieces(
+    terms = gradient_pieces(
         layout, place, (middle_group, layout.columns), {"up": grad_up, "down": grad_down}
     )
     grad_pre_round, terms = lax.optimization_barrier((grad_pre_round, terms))
-    sum_last = scatter(layout, terms)
+    sum_last = scatter(layout, *terms)
     grad_normed_two = dot_t(grad_pre_round, up_weight)
     grad_gain_two = jnp.sum(grad_normed_two * unit_two, 0)
     grad_shift_two = jnp.sum(grad_normed_two, 0)
@@ -900,17 +924,22 @@
     grad_out = t_dot(mixed, middle_round).astype(BF)
     grad_mixed = dot_t(middle_round, out_weight).astype(BF)
     grad_mixed_heads = to_heads(grad_mixed, 1)
-    (terms,) = gradient_pieces(
+    terms = gradient_pieces(
         layout, place, (layout.first, middle_group), {"out": grad_out, "up": grad_up}
     )
-    sum_middle = scatter(layout, terms)
-    grad_packed, sums = attend_back(counts, packed, log_total, grad_mixed_heads, chunk)
+    sum_middle = scatter(layout, *terms)
+    grad_packed, sums = attend_back(
+        counts, place, packed, log_total, grad_mixed_heads, chunk
+    )
     grad_projected = from_heads(grad_packed, 3)
     grad_qkv = t_dot(normed_round, grad_projected).astype(BF)
-    terms, leftover_terms = gradient_pieces(
+    *terms, leftover_terms = gradient_pieces(
         layout, place, (0, layout.first), {"qkv": grad_qkv}, leftover=True
     )
-    sum_first = scatter(layout, terms)
+    grad_projected, leftover_terms, *terms = lax.optimization_barrier(
+        (grad_projected, leftover_terms, *terms)
+    )
+    sum_first = scatter(layout, *terms)
     grad_normed_one = dot_t(grad_projected, qkv_weight)
     grad_gain_one = jnp.sum(grad_normed_one * unit_one, 0)
     grad_shift_one = jnp.sum(grad_normed_one, 0)
@@ -944,23 +973,14 @@
     leftover_sum = jnp.concatenate(sums_left)
 
     summed = jnp.concatenate([sum_first, sum_middle, sum_last])
-    held = lax.all_to_all(
-        summed.reshape(layout.columns, layout.piece, LANES),
-        "dp",
-        split_axis=0,
-        concat_axis=0,
-        tiled=True,
-        axis_index_groups=everyone,
-    )
+    summed = summed.reshape(layout.columns, layout.piece, LANES)
+    pieces = [
+        lax.dynamic_index_in_dim(summed, column ^ key, keepdims=False)
+        for key in range(layout.columns)
+    ]
+    pieces = pieces[:1] + [exchange(pieces[key], "dp", 2 * key) for key in range(1, layout.columns)]
     param_grads, new_params, new_first, new_second = finish(
-        layout,
-        jnp.stack([shard.astype(jnp.int32), offset]),
-        held.reshape(-1, LANES),
-        leftover_sum,
-        vector_grads,
-        params,
-        first_moment,
-        second_moment,
+        layout, place, pieces, leftover_sum, vector_grads, params, first_moment, second_moment
     )
     return (output[None], input_grad[None], param_grads, new_params, new_first, new_second)
 

time: 796 us -> 844 us (1.060)
  the two profiles are of different devices: /device:TPU:1 before, /device:TPU:0 now
where the time goes in v3:
time: 844 us; the launch traced here: 834 us
  waiting for transfers between devices  397 us (47%)
  starting transfers between devices  162 us (19%)
  Pallas kernels  125 us (15%)
  matrix products  81 us (10%)
  local copies, waits for them, and re-layouts  46 us (5%)
  other arithmetic  19.9 us (2%)
    ppermute x110, waiting for transfers between devices, exchange(): lax.ppermute(array, axis, [(index, index ^ bit) for index in range(size)])  380 us
    ppermute x110, starting transfers between devices, exchange(): lax.ppermute(array, axis, [(index, index ^ bit) for index in range(size)])  134 us
    pallas_call x3, Pallas kernels, gradient_pieces(): pl.pallas_call(kernel, grid=(steps,), in_specs=[pl.BlockSpec(memory_space...  39.5 us
    dot_general x4, matrix products, dense(): return jnp.dot(left, right, preferred_element_type=F32)  28.6 us
    dot_general x4, matrix products, dot_t(): lax.dot_general(left, right, (((1,), (1,)), ((), ())), preferred_element_...  26.8 us
    dot_general x4, matrix products, t_dot(): lax.dot_general(left, right, (((0,), (0,)), ((), ())), preferred_element_...  25.6 us
    pallas_call x1, Pallas kernels, attend_back(): pl.pallas_call(kernel, name='attend_back', grid=(heads,), in_specs=[pl.Bl...  23 us
    pallas_call x1, Pallas kernels, other_weights(): pl.pallas_call(kernel, name='other_weights', grid=(STEPS,), in_specs=[pl....  22.5 us
  transfers between devices with their start and end apart: 131, of which 50 were waited for; matrix products, arithmetic and copies ran while one was open for 7% of the time, Pallas kernels for 4%

profile of v3, /device:TPU:0, one launch (start us, length us, event | category | flops | bytes accessed | tf_op | source)
XLA Modules:
  0.0 834.2 jit_solution(17797532265626032520)
XLA Ops:
  50.4 10.7 %collective-permute-done.16.refs_8_ = bf16[944,128]{1,0:T(8,128)(2,1)S(1)} collective-permute-done((bf16[944,128]{1,0:T(8,128)(2,1)S(1)}, bf16[944,128]{1,0:T(8,128)(2,1)S(1)}, u32[]{:S(2)}, u32[]{:S(2)}) %collective-permute-start.16) | collective-permute-done | bytes 241696 | tf_op jit(solution)/shard_map/ppermute | solution.py:578
  114.4 10.2 %first_weights.1 = bf16[1152,3456]{1,0:T(8,128)(2,1)} custom-call(s32[5]{0:T(128)} %stack.23.place_ref, bf16[944,128]{1,0:T(8,128)(2,1)} %copy-done.11, bf16[944,128]{1,0:T(8,128)(2,1)} %copy-done.24, bf16[944,128]{1,0:T(8,128)(2,1)} %copy-done.25, bf16[944,128]{1,0:T(8,128)(2,1)} %copy-done.29, bf16[944,128]{1,0:T(8,128)(2,1)} %copy-done.23, ...), custom_call_target="tpu_custom_call" | custom-call | tf_op jit(solution)/shard_map/first_weights/pallas_call | solution.py:215
  150.4 16.2 %collective-permute-done.45.refs_1_ = bf16[256,864]{1,0:T(8,128)(2,1)S(1)} collective-permute-done((bf16[256,864]{1,0:T(8,128)(2,1)}, bf16[256,864]{1,0:T(8,128)(2,1)S(1)}, u32[]{:S(2)}, u32[]{:S(2)}) %collective-permute-start.45) | collective-permute-done | bytes 442400 | tf_op jit(solution)/shard_map/ppermute | solution.py:578
  167.5 12.8 %collective-permute-done.46.refs_2_ = bf16[256,864]{1,0:T(8,128)(2,1)S(1)} collective-permute-done((bf16[256,864]{1,0:T(8,128)(2,1)}, bf16[256,864]{1,0:T(8,128)(2,1)S(1)}, u32[]{:S(2)}, u32[]{:S(2)}) %collective-permute-start.46) | collective-permute-done | bytes 442400 | tf_op jit(solution)/shard_map/ppermute | solution.py:578
  190.3 11.7 %collective-permute-done.60.refs_10_ = bf16[2832,128]{1,0:T(8,128)(2,1)S(1)} collective-permute-done((bf16[2832,128]{1,0:T(8,128)(2,1)}, bf16[2832,128]{1,0:T(8,128)(2,1)S(1)}, u32[]{:S(2)}, u32[]{:S(2)}) %collective-permute-start.60) | collective-permute-done | bytes 725024 | tf_op jit(solution)/shard_map/ppermute | solution.py:578
  202.0 18.6 %collective-permute-done.62.refs_12_ = bf16[2832,128]{1,0:T(8,128)(2,1)S(1)} collective-permute-done((bf16[2832,128]{1,0:T(8,128)(2,1)}, bf16[2832,128]{1,0:T(8,128)(2,1)S(1)}, u32[]{:S(2)}, u32[]{:S(2)}) %collective-permute-start.62) | collective-permute-done | bytes 725024 | tf_op jit(solution)/shard_map/ppermute | solution.py:578
  224.7 15.0 %attend.1 = (bf16[256,288]{1,0:T(8,128)(2,1)}, bf16[256,288]{1,0:T(8,128)(2,1)}, bf16[256,288]{1,0:T(8,128)(2,1)}, bf16[256,288]{1,0:T(8,128)(2,1)}, f32[4,1024,1]{2,1,0:T(8,128)}) custom-call(s32[1]{0:T(128)} %copy.33.count, s32[5]{0:T(128)} %stack.23.place_ref, bf16[256,864]{1,0:T(8,128)(2,1)} %bitcast.126, bf16[256,864]{1,0:T(8,128)(2,1)} %copy-done.5, ...), custom_call_target="tpu_custom_call" | custom-call | tf_op jit(solution)/shard_map/attend/pallas_call | solution.py:465
  247.3 9.4 %collective-permute-done.49 = bf16[256,288]{1,0:T(8,128)(2,1)S(1)} collective-permute-done((bf16[256,288]{1,0:T(8,128)(2,1)}, bf16[256,288]{1,0:T(8,128)(2,1)S(1)}, u32[]{:S(2)}, u32[]{:S(2)}) %collective-permute-start.49) | collective-permute-done | bytes 147488 | tf_op jit(solution)/shard_map/ppermute | solution.py:578
  269.5 15.6 %collective-permute-done.61.refs_11_ = bf16[2832,128]{1,0:T(8,128)(2,1)} collective-permute-done((bf16[2832,128]{1,0:T(8,128)(2,1)}, bf16[2832,128]{1,0:T(8,128)(2,1)}, u32[]{:S(2)}, u32[]{:S(2)}) %collective-permute-start.61) | collective-permute-done | bytes 725024 | tf_op jit(solution)/shard_map/ppermute | solution.py:578
  285.6 13.2 %collective-permute-done.64.refs_14_ = bf16[2832,128]{1,0:T(8,128)(2,1)} collective-permute-done((bf16[2832,128]{1,0:T(8,128)(2,1)}, bf16[2832,128]{1,0:T(8,128)(2,1)}, u32[]{:S(2)}, u32[]{:S(2)}) %collective-permute-start.64) | collective-permute-done | bytes 725024 | tf_op jit(solution)/shard_map/ppermute | solution.py:578
  302.8 15.8 %collective-permute-done.65.refs_15_ = bf16[2832,128]{1,0:T(8,128)(2,1)} collective-permute-done((bf16[2832,128]{1,0:T(8,128)(2,1)}, bf16[2832,128]{1,0:T(8,128)(2,1)}, u32[]{:S(2)}, u32[]{:S(2)}) %collective-permute-start.65) | collective-permute-done | bytes 725024 | tf_op jit(solution)/shard_map/ppermute | solution.py:578
  321.2 22.5 %other_weights.1 = (bf16[1152,1152]{1,0:T(8,128)(2,1)}, bf16[1152,4304]{1,0:T(8,128)(2,1)}, bf16[4304,1152]{1,0:T(8,128)(2,1)}) custom-call(s32[5]{0:T(128)} %stack.23.place_ref, bf16[2832,128]{1,0:T(8,128)(2,1)} %copy-done.3, bf16[2832,128]{1,0:T(8,128)(2,1)} %collective-permute-done.51.refs_1_, bf16[2832,128]{1,0:T(8,128)(2,1)} %collective-permute-done.52.refs_2_, ...), custom_call_target="tpu_custom_call" | custom-call | tf_op jit(solution)/shard_map/other_weights/pallas_call | solution.py:258
  346.9 10.6 %convolution_add_fusion = f32[256,4304]{0,1:T(8,128)} fusion(bf16[1152,4304]{1,0:T(8,128)(2,1)} %get-tuple-element.88, f32[4304]{0:T(1024)S(1)} %slice.391, f32[256,1152]{1,0:T(8,128)S(1)} %get-tuple-element.224, f32[1152]{0:T(1024)S(1)} %get-tuple-element.217, f32[1152]{0:T(1024)S(1)} %get-tuple-element.215, f32[256]{0:T(256)S(1)} %add_rsqrt_fusion, ...), kind=kOutput, calls=%fused_computation.4 | convolution fusion | flops 2541178880 | bytes 15531840 | tf_op jit(solution)/shard_map/dot_general | solution.py:409
  357.4 10.1 %convolution_convert_fusion.refs_1_ = bf16[4304,1152]{1,0:T(8,128)(2,1)} fusion(f32[1,256,1152]{2,1,0:T(8,128)S(1)} %copy-done.9, f32[256]{0:T(256)S(1)} %compare_convert_fusion, f32[256,4304]{0,1:T(8,128)} %convolution_add_fusion), kind=kOutput, calls=%fused_computation | convolution fusion | flops 2554066944 | bytes 15504384 | tf_op jit(solution)/shard_map/dot_general | solution.py:405
  383.1 16.5 %shard_map.109 = (bf16[30208,128]{1,0:T(8,128)(2,1)}, bf16[30208,128]{1,0:T(8,128)(2,1)}) custom-call(s32[5]{0:T(128)} %stack.23.place_ref, bf16[1152,4304]{1,0:T(8,128)(2,1)} %convolution_convert_fusion.1.refs_0_.refs_1_, bf16[4304,1152]{1,0:T(8,128)(2,1)} %convolution_convert_fusion.refs_1_), custom_call_target="tpu_custom_call" | custom-call | tf_op jit(solution)/shard_map/pallas_call | solution.py:384
  427.3 10.9 %collective-permute-done.83.refs_6_ = bf16[256,288]{1,0:T(8,128)(2,1)} collective-permute-done((bf16[256,288]{1,0:T(8,128)(2,1)}, bf16[256,288]{1,0:T(8,128)(2,1)}, u32[]{:S(2)}, u32[]{:S(2)}) %collective-permute-start.83) | collective-permute-done | bytes 147488 | tf_op jit(solution)/shard_map/ppermute | solution.py:578
  438.3 23.0 %attend_back.1 = (bf16[256,864]{1,0:T(8,128)(2,1)}, bf16[256,864]{1,0:T(8,128)(2,1)}, bf16[256,864]{1,0:T(8,128)(2,1)}, bf16[256,864]{1,0:T(8,128)(2,1)}, f32[4,2,72]{2,1,0:T(2,128)}) custom-call(s32[1]{0:T(128)} %copy.33.count, s32[5]{0:T(128)} %stack.23.place_ref, f32[4,1024,1]{2,1,0:T(8,128)} %get-tuple-element.93.logs, bf16[256,864]{1,0:T(8,128)(2,1)} %bitcast.127, ...), custom_call_target="tpu_custom_call" | custom-call | tf_op jit(solution)/shard_map/attend_back/pallas_call | solution.py:527
  473.7 10.1 %collective-permute-done.87 = bf16[256,864]{1,0:T(8,128)(2,1)} collective-permute-done((bf16[256,864]{1,0:T(8,128)(2,1)}, bf16[256,864]{1,0:T(8,128)(2,1)}, u32[]{:S(2)}, u32[]{:S(2)}) %collective-permute-start.87) | collective-permute-done | bytes 442400 | tf_op jit(solution)/shard_map/ppermute | solution.py:578
  483.8 16.0 %collective-permute-done.86 = bf16[256,864]{1,0:T(8,128)(2,1)} collective-permute-done((bf16[256,864]{1,0:T(8,128)(2,1)}, bf16[256,864]{1,0:T(8,128)(2,1)}, u32[]{:S(2)}, u32[]{:S(2)}) %collective-permute-start.86) | collective-permute-done | bytes 442400 | tf_op jit(solution)/shard_map/ppermute | solution.py:578
  516.8 11.0 %shard_map.110 = (bf16[15104,128]{1,0:T(8,128)(2,1)}, bf16[15104,128]{1,0:T(8,128)(2,1)}, bf16[1344,128]{1,0:T(8,128)(2,1)}) custom-call(s32[5]{0:T(128)} %stack.23.place_ref, bf16[1152,3456]{1,0:T(8,128)(2,1)} %convolution_convert_fusion.2.refs_0_), custom_call_target="tpu_custom_call" | custom-call | tf_op jit(solution)/shard_map/pallas_call | solution.py:384
  541.8 12.0 %shard_map.111 = (bf16[15104,128]{1,0:T(8,128)(2,1)}, bf16[15104,128]{1,0:T(8,128)(2,1)}) custom-call(s32[5]{0:T(128)} %stack.23.place_ref, bf16[1152,1152]{1,0:T(8,128)(2,1)} %convolution_convert_fusion.3.refs_0_, bf16[1152,4304]{1,0:T(8,128)(2,1)} %convolution_convert_fusion.1.refs_0_.refs_1_), custom_call_target="tpu_custom_call" | custom-call | tf_op jit(solution)/shard_map/pallas_call | solution.py:384
  556.4 9.3 %fusion.9 = bf16[1,256,1152]{2,1,0:T(8,128)(2,1)} fusion(f32[256,1152]{1,0:T(8,128)S(1)} %get-tuple-element.224, bf16[4304,1152]{1,0:T(8,128)(2,1)} %get-tuple-element.89, f32[1152]{0:T(1024)S(1)} %copy-done.62, f32[256,4304]{0,1:T(8,128)} %convolution_add_fusion), kind=kOutput, calls=%fused_computation.20 | convolution fusion | flops 2549403648 | bytes 16097792 | tf_op jit(solution)/shard_map/dot_general | solution.py:409
  593.2 12.5 %collective-permute-start.103 = (bf16[1888,128]{1,0:T(8,128)(2,1)S(1)}, bf16[1888,128]{1,0:T(8,128)(2,1)S(1)}, u32[]{:S(2)}, u32[]{:S(2)}) collective-permute-start(bf16[1888,128]{1,0:T(8,128)(2,1)S(1)} %get-tuple-element.119), channel_id=1, source_target_pairs={{0,8},{4,12},{8,0},{12,4},{16,24},{20,28},{24,16},{28,20},{1,9},{5... | collective-permute-start | bytes 1449992 | tf_op jit(solution)/shard_map/ppermute | solution.py:578
  605.9 13.8 %collective-permute-done.99 = bf16[1888,128]{1,0:T(8,128)(2,1)S(1)} collective-permute-done((bf16[1888,128]{1,0:T(8,128)(2,1)S(1)}, bf16[1888,128]{1,0:T(8,128)(2,1)S(1)}, u32[]{:S(2)}, u32[]{:S(2)}) %collective-permute-start.99) | collective-permute-done | bytes 483360 | tf_op jit(solution)/shard_map/ppermute | solution.py:578
  645.4 8.7 %collective-permute-done.94 = bf16[1888,128]{1,0:T(8,128)(2,1)S(1)} collective-permute-done((bf16[1888,128]{1,0:T(8,128)(2,1)S(1)}, bf16[1888,128]{1,0:T(8,128)(2,1)S(1)}, u32[]{:S(2)}, u32[]{:S(2)}) %collective-permute-start.94) | collective-permute-done | bytes 483360 | tf_op jit(solution)/shard_map/ppermute | solution.py:578
  655.6 10.3 %collective-permute-done.89 = bf16[1888,128]{1,0:T(8,128)(2,1)S(1)} collective-permute-done((bf16[1888,128]{1,0:T(8,128)(2,1)S(1)}, bf16[1888,128]{1,0:T(8,128)(2,1)S(1)}, u32[]{:S(2)}, u32[]{:S(2)}) %collective-permute-start.89) | collective-permute-done | bytes 483360 | tf_op jit(solution)/shard_map/ppermute | solution.py:578
  700.7 13.9 %collective-permute-done.114 = bf16[3776,128]{1,0:T(8,128)(2,1)S(1)} collective-permute-done((bf16[3776,128]{1,0:T(8,128)(2,1)S(1)}, bf16[3776,128]{1,0:T(8,128)(2,1)S(1)}, u32[]{:S(2)}, u32[]{:S(2)}) %collective-permute-start.114) | collective-permute-done | bytes 966688 | tf_op jit(solution)/shard_map/ppermute | solution.py:578
  715.4 21.3 %collective-permute-done.109 = bf16[3776,128]{1,0:T(8,128)(2,1)S(1)} collective-permute-done((bf16[3776,128]{1,0:T(8,128)(2,1)S(1)}, bf16[3776,128]{1,0:T(8,128)(2,1)S(1)}, u32[]{:S(2)}, u32[]{:S(2)}) %collective-permute-start.109) | collective-permute-done | bytes 966688 | tf_op jit(solution)/shard_map/ppermute | solution.py:578
  739.0 20.6 %collective-permute-done.115 = bf16[3776,128]{1,0:T(8,128)(2,1)S(1)} collective-permute-done((bf16[3776,128]{1,0:T(8,128)(2,1)S(1)}, bf16[3776,128]{1,0:T(8,128)(2,1)S(1)}, u32[]{:S(2)}, u32[]{:S(2)}) %collective-permute-start.115) | collective-permute-done | bytes 966688 | tf_op jit(solution)/shard_map/ppermute | solution.py:578
  760.6 9.4 %collective-permute-done.111 = bf16[3776,128]{1,0:T(8,128)(2,1)S(1)} collective-permute-done((bf16[3776,128]{1,0:T(8,128)(2,1)S(1)}, bf16[3776,128]{1,0:T(8,128)(2,1)S(1)}, u32[]{:S(2)}, u32[]{:S(2)}) %collective-permute-start.111) | collective-permute-done | bytes 966688 | tf_op jit(solution)/shard_map/ppermute | solution.py:578
  774.5 19.6 %collective-permute-done.116 = bf16[1888,128]{1,0:T(8,128)(2,1)S(1)} collective-permute-done((bf16[1888,128]{1,0:T(8,128)(2,1)S(1)}, bf16[1888,128]{1,0:T(8,128)(2,1)S(1)}, u32[]{:S(2)}, u32[]{:S(2)}) %collective-permute-start.116) | collective-permute-done | bytes 483360 | tf_op jit(solution)/shard_map/ppermute | solution.py:578
  824.7 9.3 %finish.1 = (f32[1,476288]{1,0:T(1,128)}, f32[1,476288]{1,0:T(1,128)}, f32[1,476288]{1,0:T(1,128)}, f32[1,476288]{1,0:T(1,128)}) custom-call(s32[5]{0:T(128)} %stack.23.place_ref, bf16[944,128]{1,0:T(8,128)(2,1)} %get-tuple-element.190.refs_0_, bf16[944,128]{1,0:T(8,128)(2,1)} %copy-done.48, bf16[944,128]{1,0:T(8,128)(2,1)} %copy-done.49, ...), custom_call_target="tpu_custom_call" | custom-call | tf_op jit(solution)/shard_map/finish/pallas_call | solution.py:819
  (502 shorter events, 390.6 us)
Async XLA Ops:
  107.5 34.4 %collective-permute-start.58 = (bf16[2832,128]{1,0:T(8,128)(2,1)S(1)}, bf16[2832,128]{1,0:T(8,128)(2,1)}, u32[]{:S(2)}, u32[]{:S(2)}) collective-permute-start(bf16[2832,128]{1,0:T(8,128)(2,1)S(1)} %pad_maximum_fusion.2.refs_0_), channel_id=1, source_target_pairs={{0,2},{1,3},{2,0},{3,1},{4,6},{5,7},{6,4},{7,5},{8,10},{9,11},{10,... | collective-permute-start | bytes 2174984 | tf_op jit(solution)/shard_map/ppermute | solution.py:578
  109.7 36.3 %collective-permute-start.51 = (bf16[2832,128]{1,0:T(8,128)(2,1)S(1)}, bf16[2832,128]{1,0:T(8,128)(2,1)}, u32[]{:S(2)}, u32[]{:S(2)}) collective-permute-start(bf16[2832,128]{1,0:T(8,128)(2,1)S(1)} %pad_maximum_fusion.2.refs_0_), channel_id=1, source_target_pairs={{0,8},{4,12},{8,0},{12,4},{16,24},{20,28},{24,16},{28,20},{1,9},{5... | collective-permute-start | bytes 2174984 | tf_op jit(solution)/shard_map/ppermute | solution.py:578
  110.0 36.1 %collective-permute-start.52 = (bf16[2832,128]{1,0:T(8,128)(2,1)S(1)}, bf16[2832,128]{1,0:T(8,128)(2,1)}, u32[]{:S(2)}, u32[]{:S(2)}) collective-permute-start(bf16[2832,128]{1,0:T(8,128)(2,1)S(1)} %pad_maximum_fusion.2.refs_0_), channel_id=1, source_target_pairs={{0,16},{4,20},{8,24},{12,28},{16,0},{20,4},{24,8},{28,12},{1,17},{... | collective-permute-start | bytes 2174984 | tf_op jit(solution)/shard_map/ppermute | solution.py:578
  111.3 36.5 %collective-permute-start.66 = (bf16[2832,128]{1,0:T(8,128)(2,1)S(1)}, bf16[2832,128]{1,0:T(8,128)(2,1)}, u32[]{:S(2)}, u32[]{:S(2)}) collective-permute-start(bf16[2832,128]{1,0:T(8,128)(2,1)S(1)} %pad_maximum_fusion.2.refs_0_), channel_id=1, source_target_pairs={{0,4},{4,0},{8,12},{12,8},{16,20},{20,16},{24,28},{28,24},{1,5},{5... | collective-permute-start | bytes 2174984 | tf_op jit(solution)/shard_map/ppermute | solution.py:578
  112.6 76.8 %collective-permute-start.55 = (bf16[2832,128]{1,0:T(8,128)(2,1)}, bf16[2832,128]{1,0:T(8,128)(2,1)}, u32[]{:S(2)}, u32[]{:S(2)}) collective-permute-start(bf16[2832,128]{1,0:T(8,128)(2,1)} %collective-permute-done.54.refs_4_), channel_id=1, source_target_pairs={{0,8},{4,12},{8,0},{12,4},{16,24},{20,28},{24,16},{28,20},{1,9},{5... | collective-permute-start | bytes 2174984 | tf_op jit(solution)/shard_map/ppermute | solution.py:578
  141.9 47.5 %collective-permute-start.56 = (bf16[2832,128]{1,0:T(8,128)(2,1)}, bf16[2832,128]{1,0:T(8,128)(2,1)S(1)}, u32[]{:S(2)}, u32[]{:S(2)}) collective-permute-start(bf16[2832,128]{1,0:T(8,128)(2,1)} %collective-permute-done.54.refs_4_), channel_id=1, source_target_pairs={{0,16},{4,20},{8,24},{12,28},{16,0},{20,4},{24,8},{28,12},{1,17},{... | collective-permute-start | bytes 2174984 | tf_op jit(solution)/shard_map/ppermute | solution.py:578
  146.1 34.2 %collective-permute-start.46 = (bf16[256,864]{1,0:T(8,128)(2,1)}, bf16[256,864]{1,0:T(8,128)(2,1)S(1)}, u32[]{:S(2)}, u32[]{:S(2)}) collective-permute-start(bf16[256,864]{1,0:T(8,128)(2,1)} %bitcast.134), channel_id=1, source_target_pairs={{0,2},{1,3},{2,0},{3,1},{4,6},{5,7},{6,4},{7,5},{8,10},{9,11},{10,... | collective-permute-start | bytes 1327112 | tf_op jit(solution)/shard_map/ppermute | solution.py:578
  147.7 35.0 %collective-permute-start.47 = (bf16[256,864]{1,0:T(8,128)(2,1)}, bf16[256,864]{1,0:T(8,128)(2,1)S(1)}, u32[]{:S(2)}, u32[]{:S(2)}) collective-permute-start(bf16[256,864]{1,0:T(8,128)(2,1)} %bitcast.132), channel_id=1, source_target_pairs={{0,3},{1,2},{2,1},{3,0},{4,7},{5,6},{6,5},{7,4},{8,11},{9,10},{10,... | collective-permute-start | bytes 1327112 | tf_op jit(solution)/shard_map/ppermute | solution.py:578
  182.8 37.7 %collective-permute-start.62 = (bf16[2832,128]{1,0:T(8,128)(2,1)}, bf16[2832,128]{1,0:T(8,128)(2,1)S(1)}, u32[]{:S(2)}, u32[]{:S(2)}) collective-permute-start(bf16[2832,128]{1,0:T(8,128)(2,1)} %collective-permute-done.54.refs_4_), channel_id=1, source_target_pairs={{0,2},{1,3},{2,0},{3,1},{4,6},{5,7},{6,4},{7,5},{8,10},{9,11},{10,... | collective-permute-start | bytes 2174984 | tf_op jit(solution)/shard_map/ppermute | solution.py:578
  189.4 31.1 %collective-permute-start.70 = (bf16[2832,128]{1,0:T(8,128)(2,1)}, bf16[2832,128]{1,0:T(8,128)(2,1)S(1)}, u32[]{:S(2)}, u32[]{:S(2)}) collective-permute-start(bf16[2832,128]{1,0:T(8,128)(2,1)} %collective-permute-done.54.refs_4_), channel_id=1, source_target_pairs={{0,4},{4,0},{8,12},{12,8},{16,20},{20,16},{24,28},{28,24},{1,5},{5... | collective-permute-start | bytes 2174984 | tf_op jit(solution)/shard_map/ppermute | solution.py:578
  189.5 50.2 %collective-permute-start.74 = (bf16[2832,128]{1,0:T(8,128)(2,1)}, bf16[2832,128]{1,0:T(8,128)(2,1)}, u32[]{:S(2)}, u32[]{:S(2)}) collective-permute-start(bf16[2832,128]{1,0:T(8,128)(2,1)} %collective-permute-done.58.refs_8_), channel_id=1, source_target_pairs={{0,4},{4,0},{8,12},{12,8},{16,20},{20,16},{24,28},{28,24},{1,5},{5... | collective-permute-start | bytes 2174984 | tf_op jit(solution)/shard_map/ppermute | solution.py:578
  190.0 76.3 %collective-permute-start.53 = (bf16[2832,128]{1,0:T(8,128)(2,1)}, bf16[2832,128]{1,0:T(8,128)(2,1)}, u32[]{:S(2)}, u32[]{:S(2)}) collective-permute-start(bf16[2832,128]{1,0:T(8,128)(2,1)} %collective-permute-done.51.refs_1_), channel_id=1, source_target_pairs={{0,16},{4,20},{8,24},{12,28},{16,0},{20,4},{24,8},{28,12},{1,17},{... | collective-permute-start | bytes 2174984 | tf_op jit(solution)/shard_map/ppermute | solution.py:578
  202.0 65.0 %collective-permute-start.67 = (bf16[2832,128]{1,0:T(8,128)(2,1)}, bf16[2832,128]{1,0:T(8,128)(2,1)}, u32[]{:S(2)}, u32[]{:S(2)}) collective-permute-start(bf16[2832,128]{1,0:T(8,128)(2,1)} %collective-permute-done.51.refs_1_), channel_id=1, source_target_pairs={{0,4},{4,0},{8,12},{12,8},{16,20},{20,16},{24,28},{28,24},{1,5},{5... | collective-permute-start | bytes 2174984 | tf_op jit(solution)/shard_map/ppermute | solution.py:578
  220.5 48.5 %collective-permute-start.68 = (bf16[2832,128]{1,0:T(8,128)(2,1)}, bf16[2832,128]{1,0:T(8,128)(2,1)}, u32[]{:S(2)}, u32[]{:S(2)}) collective-permute-start(bf16[2832,128]{1,0:T(8,128)(2,1)} %collective-permute-done.52.refs_2_), channel_id=1, source_target_pairs={{0,4},{4,0},{8,12},{12,8},{16,20},{20,16},{24,28},{28,24},{1,5},{5... | collective-permute-start | bytes 2174984 | tf_op jit(solution)/shard_map/ppermute | solution.py:578
  222.3 46.7 %collective-permute-start.57 = (bf16[2832,128]{1,0:T(8,128)(2,1)S(1)}, bf16[2832,128]{1,0:T(8,128)(2,1)}, u32[]{:S(2)}, u32[]{:S(2)}) collective-permute-start(bf16[2832,128]{1,0:T(8,128)(2,1)S(1)} %collective-permute-done.56.refs_6_), channel_id=1, source_target_pairs={{0,8},{4,12},{8,0},{12,4},{16,24},{20,28},{24,16},{28,20},{1,9},{5... | collective-permute-start | bytes 2174984 | tf_op jit(solution)/shard_map/ppermute | solution.py:578
  266.9 31.8 %collective-permute-start.64 = (bf16[2832,128]{1,0:T(8,128)(2,1)}, bf16[2832,128]{1,0:T(8,128)(2,1)}, u32[]{:S(2)}, u32[]{:S(2)}) collective-permute-start(bf16[2832,128]{1,0:T(8,128)(2,1)} %copy-done.15), channel_id=1, source_target_pairs={{0,16},{4,20},{8,24},{12,28},{16,0},{20,4},{24,8},{28,12},{1,17},{... | collective-permute-start | bytes 2174984 | tf_op jit(solution)/shard_map/ppermute | solution.py:578
  269.0 29.8 %collective-permute-start.71 = (bf16[2832,128]{1,0:T(8,128)(2,1)}, bf16[2832,128]{1,0:T(8,128)(2,1)S(1)}, u32[]{:S(2)}, u32[]{:S(2)}) collective-permute-start(bf16[2832,128]{1,0:T(8,128)(2,1)} %collective-permute-done.55.refs_5_), channel_id=1, source_target_pairs={{0,4},{4,0},{8,12},{12,8},{16,20},{20,16},{24,28},{28,24},{1,5},{5... | collective-permute-start | bytes 2174984 | tf_op jit(solution)/shard_map/ppermute | solution.py:578
  269.0 30.3 %collective-permute-start.72 = (bf16[2832,128]{1,0:T(8,128)(2,1)S(1)}, bf16[2832,128]{1,0:T(8,128)(2,1)S(1)}, u32[]{:S(2)}, u32[]{:S(2)}) collective-permute-start(bf16[2832,128]{1,0:T(8,128)(2,1)S(1)} %collective-permute-done.56.refs_6_), channel_id=1, source_target_pairs={{0,4},{4,0},{8,12},{12,8},{16,20},{20,16},{24,28},{28,24},{1,5},{5... | collective-permute-start | bytes 2174984 | tf_op jit(solution)/shard_map/ppermute | solution.py:578
  465.6 34.3 %collective-permute-start.86 = (bf16[256,864]{1,0:T(8,128)(2,1)}, bf16[256,864]{1,0:T(8,128)(2,1)}, u32[]{:S(2)}, u32[]{:S(2)}) collective-permute-start(bf16[256,864]{1,0:T(8,128)(2,1)} %get-tuple-element.95), channel_id=1, source_target_pairs={{0,2},{1,3},{2,0},{3,1},{4,6},{5,7},{6,4},{7,5},{8,10},{9,11},{10,... | collective-permute-start | bytes 1327112 | tf_op jit(solution)/shard_map/ppermute | solution.py:578
  465.6 34.3 %collective-permute-start.85 = (bf16[256,864]{1,0:T(8,128)(2,1)}, bf16[256,864]{1,0:T(8,128)(2,1)}, u32[]{:S(2)}, u32[]{:S(2)}) collective-permute-start(bf16[256,864]{1,0:T(8,128)(2,1)} %get-tuple-element.94), channel_id=1, source_target_pairs={{0,3},{1,2},{2,1},{3,0},{4,7},{5,6},{6,5},{7,4},{8,11},{9,10},{10,... | collective-permute-start | bytes 1327112 | tf_op jit(solution)/shard_map/ppermute | solution.py:578
  541.8 132.3 %collective-permute-start.108 = (bf16[30208,128]{1,0:T(8,128)(2,1)}, bf16[30208,128]{1,0:T(8,128)(2,1)}, u32[]{:S(2)}, u32[]{:S(2)}) collective-permute-start(bf16[30208,128]{1,0:T(8,128)(2,1)} %get-tuple-element.123), channel_id=1, source_target_pairs={{0,4},{4,0},{8,12},{12,8},{16,20},{20,16},{24,28},{28,24},{1,5},{5... | collective-permute-start | bytes 23199752 | tf_op jit(solution)/shard_map/ppermute | solution.py:578
  553.8 34.4 %collective-permute-start.98 = (bf16[15104,128]{1,0:T(8,128)(2,1)}, bf16[15104,128]{1,0:T(8,128)(2,1)S(1)}, u32[]{:S(2)}, u32[]{:S(2)}) collective-permute-start(bf16[15104,128]{1,0:T(8,128)(2,1)} %get-tuple-element.113), channel_id=1, source_target_pairs={{0,4},{4,0},{8,12},{12,8},{16,20},{20,16},{24,28},{28,24},{1,5},{5... | collective-permute-start | bytes 11599880 | tf_op jit(solution)/shard_map/ppermute | solution.py:578
  567.9 51.9 %collective-permute-start.88 = (bf16[15104,128]{1,0:T(8,128)(2,1)S(1)}, bf16[15104,128]{1,0:T(8,128)(2,1)S(1)}, u32[]{:S(2)}, u32[]{:S(2)}) collective-permute-start(bf16[15104,128]{1,0:T(8,128)(2,1)S(1)} %copy-done.67), channel_id=1, source_target_pairs={{0,4},{4,0},{8,12},{12,8},{16,20},{20,16},{24,28},{28,24},{1,5},{5... | collective-permute-start | bytes 11599880 | tf_op jit(solution)/shard_map/ppermute | solution.py:578
  592.6 225.1 %collective-permute-start.125 = (bf16[1344,128]{1,0:T(8,128)(2,1)S(1)}, bf16[1344,128]{1,0:T(8,128)(2,1)S(1)}, u32[]{:S(2)}, u32[]{:S(2)}) collective-permute-start(bf16[1344,128]{1,0:T(8,128)(2,1)S(1)} %add_convert_fusion.41), channel_id=1, source_target_pairs={{9,8}} | collective-permute-start | bytes 1032200 | tf_op jit(solution)/shard_map/ppermute | solution.py:715
  593.2 29.7 %collective-permute-start.103 = (bf16[1888,128]{1,0:T(8,128)(2,1)S(1)}, bf16[1888,128]{1,0:T(8,128)(2,1)S(1)}, u32[]{:S(2)}, u32[]{:S(2)}) collective-permute-start(bf16[1888,128]{1,0:T(8,128)(2,1)S(1)} %get-tuple-element.119), channel_id=1, source_target_pairs={{0,8},{4,12},{8,0},{12,4},{16,24},{20,28},{24,16},{28,20},{1,9},{5... | collective-permute-start | bytes 1449992 | tf_op jit(solution)/shard_map/ppermute | solution.py:578
  634.9 45.0 %collective-permute-start.93 = (bf16[1888,128]{1,0:T(8,128)(2,1)S(1)}, bf16[1888,128]{1,0:T(8,128)(2,1)S(1)}, u32[]{:S(2)}, u32[]{:S(2)}) collective-permute-start(bf16[1888,128]{1,0:T(8,128)(2,1)S(1)} %get-tuple-element.109), channel_id=1, source_target_pairs={{0,8},{4,12},{8,0},{12,4},{16,24},{20,28},{24,16},{28,20},{1,9},{5... | collective-permute-start | bytes 1449992 | tf_op jit(solution)/shard_map/ppermute | solution.py:578
  643.7 40.5 %collective-permute-start.91 = (bf16[1888,128]{1,0:T(8,128)(2,1)S(1)}, bf16[1888,128]{1,0:T(8,128)(2,1)S(1)}, u32[]{:S(2)}, u32[]{:S(2)}) collective-permute-start(bf16[1888,128]{1,0:T(8,128)(2,1)S(1)} %get-tuple-element.107), channel_id=1, source_target_pairs={{0,16},{4,20},{8,24},{12,28},{16,0},{20,4},{24,8},{28,12},{1,17},{... | collective-permute-start | bytes 1449992 | tf_op jit(solution)/shard_map/ppermute | solution.py:578
  672.6 121.7 %collective-permute-start.102 = (bf16[944,128]{1,0:T(8,128)(2,1)S(1)}, bf16[944,128]{1,0:T(8,128)(2,1)S(1)}, u32[]{:S(2)}, u32[]{:S(2)}) collective-permute-start(bf16[944,128]{1,0:T(8,128)(2,1)S(1)} %slice.426), channel_id=1, source_target_pairs={{0,1},{1,0},{2,3},{3,2},{4,5},{5,4},{6,7},{7,6},{8,9},{9,8},{10,11... | collective-permute-start | bytes 725000 | tf_op jit(solution)/shard_map/ppermute | solution.py:578
  683.4 31.2 %collective-permute-start.114 = (bf16[3776,128]{1,0:T(8,128)(2,1)S(1)}, bf16[3776,128]{1,0:T(8,128)(2,1)S(1)}, u32[]{:S(2)}, u32[]{:S(2)}) collective-permute-start(bf16[3776,128]{1,0:T(8,128)(2,1)S(1)} %get-tuple-element.131), channel_id=1, source_target_pairs={{0,8},{4,12},{8,0},{12,4},{16,24},{20,28},{24,16},{28,20},{1,9},{5... | collective-permute-start | bytes 2899976 | tf_op jit(solution)/shard_map/ppermute | solution.py:578
  684.2 111.6 %collective-permute-start.107 = (bf16[944,128]{1,0:T(8,128)(2,1)S(1)}, bf16[944,128]{1,0:T(8,128)(2,1)S(1)}, u32[]{:S(2)}, u32[]{:S(2)}) collective-permute-start(bf16[944,128]{1,0:T(8,128)(2,1)S(1)} %add_convert_fusion.46), channel_id=1, source_target_pairs={{0,2},{1,3},{2,0},{3,1},{4,6},{5,7},{6,4},{7,5},{8,10},{9,11},{10,... | collective-permute-start | bytes 725000 | tf_op jit(solution)/shard_map/ppermute | solution.py:578
  700.1 37.4 %collective-permute-start.113 = (bf16[3776,128]{1,0:T(8,128)(2,1)S(1)}, bf16[3776,128]{1,0:T(8,128)(2,1)S(1)}, u32[]{:S(2)}, u32[]{:S(2)}) collective-permute-start(bf16[3776,128]{1,0:T(8,128)(2,1)S(1)} %get-tuple-element.129), channel_id=1, source_target_pairs={{0,8},{4,12},{8,0},{12,4},{16,24},{20,28},{24,16},{28,20},{1,9},{5... | collective-permute-start | bytes 2899976 | tf_op jit(solution)/shard_map/ppermute | solution.py:578
  737.5 32.5 %collective-permute-start.111 = (bf16[3776,128]{1,0:T(8,128)(2,1)S(1)}, bf16[3776,128]{1,0:T(8,128)(2,1)S(1)}, u32[]{:S(2)}, u32[]{:S(2)}) collective-permute-start(bf16[3776,128]{1,0:T(8,128)(2,1)S(1)} %get-tuple-element.127), channel_id=1, source_target_pairs={{0,16},{4,20},{8,24},{12,28},{16,0},{20,4},{24,8},{28,12},{1,17},{... | collective-permute-start | bytes 2899976 | tf_op jit(solution)/shard_map/ppermute | solution.py:578
  (173 other events, 2646.5 us)

commit v4 on v3

--- a/solution.py
+++ b/solution.py
@@ -617,10 +617,10 @@
 
 def gather(layout, share, behind=None):
     held = {0: share}
-    bit = 1
-    while bit < layout.ctx:
+    bit = layout.ctx // 2
+    while bit:
         held.update({key ^ bit: exchange(held[key], "ctx", bit) for key in list(held)})
-        bit *= 2
+        bit //= 2
     arrays = []
     for key in range(layout.ctx):
         own = held[key]
@@ -699,22 +699,26 @@
     return found
 
 
-def broadcast(layout, shard, owner, held):
-    have = [owner]
+def everywhere(layout, array, bit):
+    if bit < layout.ctx:
+        return exchange(array, "ctx", bit)
+    return exchange(array, "dp", bit // layout.ctx)
+
+
+def broadcast(layout, shard, sources):
+    held = jnp.concatenate([rows for _, rows in sources])
+    owner = jnp.concatenate(
+        [jnp.full((rows.shape[0], 1), source, jnp.int32) for source, rows in sources]
+    )
     for bit in bits(layout):
-        other = lax.ppermute(held, ("dp", "ctx"), [(index, index ^ bit) for index in have])
-        have += [index ^ bit for index in have]
-        held = jnp.where((shard & bit) != (owner & bit), other, held)
+        other = everywhere(layout, held, bit)
+        held = jnp.where(((owner ^ shard) & bit) == 0, held, other)
     return held
 
 
-def sum_to(layout, owner, held):
-    have = list(range(layout.devices))
+def sum_all(layout, held):
     for bit in reversed(bits(layout)):
-        senders = [index for index in have if (index & bit) != (owner & bit)]
-        other = lax.ppermute(held, ("dp", "ctx"), [(index, index ^ bit) for index in senders])
-        have = [index for index in have if index not in senders]
-        held = (held.astype(F32) + other.astype(F32)).astype(held.dtype)
+        held = add(held, everywhere(layout, held, bit))
     return held
 
 
@@ -766,16 +770,17 @@
     )(place, params, before)
 
 
-def finish(layout, place, pieces, leftover, vectors, params, first, second):
+def finish(layout, place, pieces, small, params, first, second):
     length = layout.columns * layout.piece
     steps = pl.cdiv(layout.rows, SWEEP)
     held = max(length, TILE + steps * SWEEP)
     vector_first = ROW_VEC - layout.start(layout.devices - 1)
     columns = layout.columns
+    extra = sum(rows for _, rows in layout.leftover())
 
     def kernel(place_ref, *refs):
         sums, refs = (refs[:columns], refs[columns:])
-        rest, vector, master, one, two, grads, new, new_one, new_two, wide = refs
+        rest, master, one, two, grads, new, new_one, new_two, wide = refs
         step = pl.program_id(0)
         shard = place_ref[4]
 
@@ -796,7 +801,7 @@
 
             @pl.when(shard == layout.devices - 1)
             def _():
-                wide[pl.ds(vector_first, VEC_ROWS), :] += vector[...]
+                wide[pl.ds(vector_first, VEC_ROWS), :] += rest[pl.ds(extra, VEC_ROWS), :].astype(F32)
 
         grad = wide[pl.ds(place_ref[3] + step * SWEEP, SWEEP), :]
         row = lax.broadcasted_iota(jnp.int32, (SWEEP, LANES), 0)
@@ -822,12 +827,12 @@
         grid=(steps,),
         in_specs=[pl.BlockSpec(memory_space=pltpu.SMEM)]
         + [whole(piece) for piece in pieces]
-        + [whole(leftover), whole(vectors), flat, flat, flat],
+        + [whole(small), flat, flat, flat],
         out_specs=[flat] * 4,
         out_shape=[jax.ShapeDtypeStruct(params.shape, F32)] * 4,
         scratch_shapes=[pltpu.VMEM((held, LANES), F32)],
         compiler_params=pltpu.CompilerParams(vmem_limit_bytes=VMEM_LIMIT),
-    )(place, *pieces, leftover, vectors, params, first, second)
+    )(place, *pieces, small, params, first, second)
 
 
 def shards(layout, inputs, counts, params, first_moment, second_moment, out_cotangent):
@@ -856,10 +861,9 @@
     shared_rest = jnp.concatenate(groups[layout.first :])
     shared_rest = lax.optimization_barrier((shared_rest, along))[0]
     gathered_rest, _, _ = gather(layout, shared_rest, behind)
-    leftover = jnp.concatenate(
-        [broadcast(layout, shard, owner, aligned[-2][:rows]) for owner, rows in layout.leftover()]
-    )
-    spread = broadcast(layout, shard, last, aligned[-1])
+    sources = [(owner, aligned[-2][:rows]) for owner, rows in layout.leftover()]
+    spread = broadcast(layout, shard, sources + [(last, aligned[-1])])
+    leftover, spread = (spread[:-VEC_ROWS], spread[-VEC_ROWS:])
     flat_vectors = spread.reshape(-1).astype(F32)
     vectors = []
     used = 0
@@ -963,14 +967,8 @@
     ]
     padding = jnp.zeros((VEC_ROWS * LANES - sum(VEC_LENGTHS),), F32)
     vector_grads = jnp.concatenate(vector_terms + [padding]).reshape(VEC_ROWS, LANES)
-    vector_grads = sum_to(layout, last, vector_grads)
-    used = 0
-    sums_left = []
-    for owner, rows in layout.leftover():
-        part = leftover_terms[used : used + rows]
-        sums_left.append(sum_to(layout, owner, part))
-        used += rows
-    leftover_sum = jnp.concatenate(sums_left)
+    small_terms = jnp.concatenate([leftover_terms, vector_grads.astype(BF)])
+    small_sum = sum_all(layout, small_terms)
 
     summed = jnp.concatenate([sum_first, sum_middle, sum_last])
     summed = summed.reshape(layout.columns, layout.piece, LANES)
@@ -980,7 +978,7 @@
     ]
     pieces = pieces[:1] + [exchange(pieces[key], "dp", 2 * key) for key in range(1, layout.columns)]
     param_grads, new_params, new_first, new_second = finish(
-        layout, place, pieces, leftover_sum, vector_grads, params, first_moment, second_moment
+        layout, place, pieces, small_sum, params, first_moment, second_moment
     )
     return (output[None], input_grad[None], param_grads, new_params, new_first, new_second)
 

time: 844 us -> 785 us (0.930)
  starting transfers between devices: 162 us -> 119 us
  waiting for transfers between devices: 397 us -> 383 us
    ppermute x20 -> x0, starting transfers between devices: 22.8 us -> none  [the longest x10 11.6 us: broadcast(): lax.ppermute(held, ('dp', 'ctx'), [(index, index ^ bit) for index in have])]
    ppermute x110 -> x120, starting transfers between devices: 134 us -> 114 us  [exchange(): lax.ppermute(array, axis, [(index, index ^ bit) for index in range(size)])]
    ppermute x20 -> x0, waiting for transfers between devices: 17.2 us -> none  [the longest x10 10.4 us: sum_to(): lax.ppermute(held, ('dp', 'ctx'), [(index, index ^ bit) for index in send...]
    ppermute x110 -> x120, waiting for transfers between devices: 380 us -> 383 us  [exchange(): lax.ppermute(array, axis, [(index, index ^ bit) for index in range(size)])]
  transfers between devices with their start and end apart: 131 -> 121, of which waited for: 50 -> 51; matrix products, arithmetic and copies ran while one was open for 7% -> 10% of each run, Pallas kernels for 4% -> 9%
where the time goes in v4:
time: 785 us; the launch traced here: 775 us
  waiting for transfers between devices  383 us (49%)
  Pallas kernels  126 us (16%)
  starting transfers between devices  119 us (15%)
  matrix products  80.3 us (10%)
  local copies, waits for them, and re-layouts  41.1 us (5%)
  other arithmetic  22.5 us (3%)
    ppermute x120, waiting for transfers between devices, exchange(): lax.ppermute(array, axis, [(index, index ^ bit) for index in range(size)])  383 us
    ppermute x120, starting transfers between devices, exchange(): lax.ppermute(array, axis, [(index, index ^ bit) for index in range(size)])  114 us
    pallas_call x3, Pallas kernels, gradient_pieces(): pl.pallas_call(kernel, grid=(steps,), in_specs=[pl.BlockSpec(memory_space...  39.8 us
    dot_general x4, matrix products, dense(): return jnp.dot(left, right, preferred_element_type=F32)  28.7 us
    dot_general x4, matrix products, dot_t(): lax.dot_general(left, right, (((1,), (1,)), ((), ())), preferred_element_...  26.2 us
    dot_general x4, matrix products, t_dot(): lax.dot_general(left, right, (((0,), (0,)), ((), ())), preferred_element_...  25.5 us
    pallas_call x1, Pallas kernels, other_weights(): pl.pallas_call(kernel, name='other_weights', grid=(STEPS,), in_specs=[pl....  22.9 us
    pallas_call x1, Pallas kernels, attend_back(): pl.pallas_call(kernel, name='attend_back', grid=(heads,), in_specs=[pl.Bl...  22.8 us
  transfers between devices with their start and end apart: 121, of which 51 were waited for; matrix products, arithmetic and copies ran while one was open for 10% of the time, Pallas kernels for 9%

profile of v4, /device:TPU:0, one launch (start us, length us, event | category | flops | bytes accessed | tf_op | source)
XLA Modules:
  0.0 775.0 jit_solution(2046885695147889557)
XLA Ops:
  31.8 15.2 %collective-permute-done.2 = bf16[1472,128]{1,0:T(8,128)(2,1)S(1)} collective-permute-done((bf16[1472,128]{1,0:T(8,128)(2,1)S(1)}, bf16[1472,128]{1,0:T(8,128)(2,1)S(1)}, u32[]{:S(2)}, u32[]{:S(2)}) %collective-permute-start.2) | collective-permute-done | bytes 376864 | tf_op jit(solution)/shard_map/ppermute | solution.py:578
  51.5 11.7 %collective-permute-done.9.refs_1_ = bf16[944,128]{1,0:T(8,128)(2,1)S(1)} collective-permute-done((bf16[944,128]{1,0:T(8,128)(2,1)S(1)}, bf16[944,128]{1,0:T(8,128)(2,1)S(1)}, u32[]{:S(2)}, u32[]{:S(2)}) %collective-permute-start.9) | collective-permute-done | bytes 241696 | tf_op jit(solution)/shard_map/ppermute | solution.py:578
  100.0 13.2 %collective-permute-done.49.refs_4_ = bf16[2832,128]{1,0:T(8,128)(2,1)S(1)} collective-permute-done((bf16[2832,128]{1,0:T(8,128)(2,1)S(1)}, bf16[2832,128]{1,0:T(8,128)(2,1)S(1)}, u32[]{:S(2)}, u32[]{:S(2)}) %collective-permute-start.49) | collective-permute-done | bytes 725024 | tf_op jit(solution)/shard_map/ppermute | solution.py:578
  133.4 10.3 %first_weights.1 = bf16[1152,3456]{1,0:T(8,128)(2,1)} custom-call(s32[5]{0:T(128)} %stack.23.place_ref, bf16[944,128]{1,0:T(8,128)(2,1)} %copy-done.12, bf16[944,128]{1,0:T(8,128)(2,1)} %copy-done.24, bf16[944,128]{1,0:T(8,128)(2,1)} %copy-done.27, bf16[944,128]{1,0:T(8,128)(2,1)} %collective-permute-done.11.refs_3_, bf16[944,128]{1,0:T(8,128)(2,1)} %copy-done.25, ...), custom_call_target="tpu_custom_call" | custom-call | tf_op jit(solution)/shard_map/first_weights/pallas_call | solution.py:215
  152.6 10.6 %collective-permute-done.50.refs_5_ = bf16[2832,128]{1,0:T(8,128)(2,1)} collective-permute-done((bf16[2832,128]{1,0:T(8,128)(2,1)S(1)}, bf16[2832,128]{1,0:T(8,128)(2,1)}, u32[]{:S(2)}, u32[]{:S(2)}) %collective-permute-start.50) | collective-permute-done | bytes 725024 | tf_op jit(solution)/shard_map/ppermute | solution.py:578
  180.5 9.6 %collective-permute-done.57.refs_12_ = bf16[2832,128]{1,0:T(8,128)(2,1)} collective-permute-done((bf16[2832,128]{1,0:T(8,128)(2,1)}, bf16[2832,128]{1,0:T(8,128)(2,1)}, u32[]{:S(2)}, u32[]{:S(2)}) %collective-permute-start.57) | collective-permute-done | bytes 725024 | tf_op jit(solution)/shard_map/ppermute | solution.py:578
  199.8 12.5 %collective-permute-done.41.refs_2_ = bf16[256,864]{1,0:T(8,128)(2,1)S(1)} collective-permute-done((bf16[256,864]{1,0:T(8,128)(2,1)}, bf16[256,864]{1,0:T(8,128)(2,1)S(1)}, u32[]{:S(2)}, u32[]{:S(2)}) %collective-permute-start.41) | collective-permute-done | bytes 442400 | tf_op jit(solution)/shard_map/ppermute | solution.py:578
  215.1 15.3 %attend.1 = (bf16[256,288]{1,0:T(8,128)(2,1)}, bf16[256,288]{1,0:T(8,128)(2,1)}, bf16[256,288]{1,0:T(8,128)(2,1)}, bf16[256,288]{1,0:T(8,128)(2,1)}, f32[4,1024,1]{2,1,0:T(8,128)}) custom-call(s32[1]{0:T(128)} %copy.34.count, s32[5]{0:T(128)} %stack.23.place_ref, bf16[256,864]{1,0:T(8,128)(2,1)} %bitcast.124, bf16[256,864]{1,0:T(8,128)(2,1)} %copy-done.5, ...), custom_call_target="tpu_custom_call" | custom-call | tf_op jit(solution)/shard_map/attend/pallas_call | solution.py:465
  230.4 9.0 %collective-permute-start.45 = (bf16[256,288]{1,0:T(8,128)(2,1)}, bf16[256,288]{1,0:T(8,128)(2,1)S(1)}, u32[]{:S(2)}, u32[]{:S(2)}) collective-permute-start(bf16[256,288]{1,0:T(8,128)(2,1)} %get-tuple-element.80), channel_id=1, source_target_pairs={{0,1},{1,0},{2,3},{3,2},{4,5},{5,4},{6,7},{7,6},{8,9},{9,8},{10,11... | collective-permute-start | bytes 442376 | tf_op jit(solution)/shard_map/ppermute | solution.py:578
  246.6 8.9 %collective-permute-done.44 = bf16[256,288]{1,0:T(8,128)(2,1)S(1)} collective-permute-done((bf16[256,288]{1,0:T(8,128)(2,1)}, bf16[256,288]{1,0:T(8,128)(2,1)S(1)}, u32[]{:S(2)}, u32[]{:S(2)}) %collective-permute-start.44) | collective-permute-done | bytes 147488 | tf_op jit(solution)/shard_map/ppermute | solution.py:578
  261.7 12.1 %collective-permute-done.59.refs_14_ = bf16[2832,128]{1,0:T(8,128)(2,1)} collective-permute-done((bf16[2832,128]{1,0:T(8,128)(2,1)}, bf16[2832,128]{1,0:T(8,128)(2,1)}, u32[]{:S(2)}, u32[]{:S(2)}) %collective-permute-start.59) | collective-permute-done | bytes 725024 | tf_op jit(solution)/shard_map/ppermute | solution.py:578
  277.4 15.5 %collective-permute-done.60.refs_15_ = bf16[2832,128]{1,0:T(8,128)(2,1)} collective-permute-done((bf16[2832,128]{1,0:T(8,128)(2,1)}, bf16[2832,128]{1,0:T(8,128)(2,1)}, u32[]{:S(2)}, u32[]{:S(2)}) %collective-permute-start.60) | collective-permute-done | bytes 725024 | tf_op jit(solution)/shard_map/ppermute | solution.py:578
  296.5 22.9 %other_weights.1 = (bf16[1152,1152]{1,0:T(8,128)(2,1)}, bf16[1152,4304]{1,0:T(8,128)(2,1)}, bf16[4304,1152]{1,0:T(8,128)(2,1)}) custom-call(s32[5]{0:T(128)} %stack.23.place_ref, bf16[2832,128]{1,0:T(8,128)(2,1)} %copy-done.3, bf16[2832,128]{1,0:T(8,128)(2,1)} %copy-done.14, bf16[2832,128]{1,0:T(8,128)(2,1)} %collective-permute-done.47.refs_2_, ...), custom_call_target="tpu_custom_call" | custom-call | tf_op jit(solution)/shard_map/other_weights/pallas_call | solution.py:258
  322.6 10.6 %convolution_add_fusion = f32[256,4304]{0,1:T(8,128)} fusion(bf16[1152,4304]{1,0:T(8,128)(2,1)} %get-tuple-element.88, f32[4304]{0:T(1024)S(1)} %copy-done.56, f32[256,1152]{1,0:T(8,128)S(1)} %get-tuple-element.231, f32[1152]{0:T(1024)S(1)} %copy-done.53, f32[1152]{0:T(1024)S(1)} %get-tuple-element.217, f32[256]{0:T(256)S(1)} %add_rsqrt_fusion, ...), kind=kOutput, calls=%fused_computation.4 | convolution fusion | flops 2541178880 | bytes 15531840 | tf_op jit(solution)/shard_map/dot_general | solution.py:409
  333.2 10.0 %convolution_convert_fusion.refs_1_ = bf16[4304,1152]{1,0:T(8,128)(2,1)} fusion(f32[1,256,1152]{2,1,0:T(8,128)S(1)} %copy-done.10, f32[256]{0:T(256)S(1)} %copy-done.68, f32[256,4304]{0,1:T(8,128)} %convolution_add_fusion), kind=kOutput, calls=%fused_computation | convolution fusion | flops 2554066944 | bytes 15504384 | tf_op jit(solution)/shard_map/dot_general | solution.py:405
  358.8 16.5 %shard_map.109 = (bf16[30208,128]{1,0:T(8,128)(2,1)}, bf16[30208,128]{1,0:T(8,128)(2,1)}) custom-call(s32[5]{0:T(128)} %stack.23.place_ref, bf16[1152,4304]{1,0:T(8,128)(2,1)} %convolution_convert_fusion.1.refs_0_.refs_1_, bf16[4304,1152]{1,0:T(8,128)(2,1)} %convolution_convert_fusion.refs_1_), custom_call_target="tpu_custom_call" | custom-call | tf_op jit(solution)/shard_map/pallas_call | solution.py:384
  402.9 10.3 %collective-permute-done.78.refs_6_ = bf16[256,288]{1,0:T(8,128)(2,1)} collective-permute-done((bf16[256,288]{1,0:T(8,128)(2,1)}, bf16[256,288]{1,0:T(8,128)(2,1)}, u32[]{:S(2)}, u32[]{:S(2)}) %collective-permute-start.78) | collective-permute-done | bytes 147488 | tf_op jit(solution)/shard_map/ppermute | solution.py:578
  413.2 22.8 %attend_back.1 = (bf16[256,864]{1,0:T(8,128)(2,1)}, bf16[256,864]{1,0:T(8,128)(2,1)}, bf16[256,864]{1,0:T(8,128)(2,1)}, bf16[256,864]{1,0:T(8,128)(2,1)}, f32[4,2,72]{2,1,0:T(2,128)}) custom-call(s32[1]{0:T(128)} %copy.34.count, s32[5]{0:T(128)} %stack.23.place_ref, f32[4,1024,1]{2,1,0:T(8,128)} %get-tuple-element.93.logs, bf16[256,864]{1,0:T(8,128)(2,1)} %bitcast.125, ...), custom_call_target="tpu_custom_call" | custom-call | tf_op jit(solution)/shard_map/attend_back/pallas_call | solution.py:527
  445.0 12.1 %shard_map.111 = (bf16[15104,128]{1,0:T(8,128)(2,1)}, bf16[15104,128]{1,0:T(8,128)(2,1)}) custom-call(s32[5]{0:T(128)} %stack.23.place_ref, bf16[1152,1152]{1,0:T(8,128)(2,1)} %convolution_convert_fusion.3.refs_0_, bf16[1152,4304]{1,0:T(8,128)(2,1)} %convolution_convert_fusion.1.refs_0_.refs_1_), custom_call_target="tpu_custom_call" | custom-call | tf_op jit(solution)/shard_map/pallas_call | solution.py:384
  459.6 14.8 %collective-permute-done.81 = bf16[256,864]{1,0:T(8,128)(2,1)} collective-permute-done((bf16[256,864]{1,0:T(8,128)(2,1)}, bf16[256,864]{1,0:T(8,128)(2,1)}, u32[]{:S(2)}, u32[]{:S(2)}) %collective-permute-start.81) | collective-permute-done | bytes 442400 | tf_op jit(solution)/shard_map/ppermute | solution.py:578
  490.3 11.2 %shard_map.110 = (bf16[15104,128]{1,0:T(8,128)(2,1)}, bf16[15104,128]{1,0:T(8,128)(2,1)}, bf16[1344,128]{1,0:T(8,128)(2,1)}) custom-call(s32[5]{0:T(128)} %stack.23.place_ref, bf16[1152,3456]{1,0:T(8,128)(2,1)} %convolution_convert_fusion.2.refs_0_), custom_call_target="tpu_custom_call" | custom-call | tf_op jit(solution)/shard_map/pallas_call | solution.py:384
  510.0 9.3 %fusion.9 = bf16[1,256,1152]{2,1,0:T(8,128)(2,1)} fusion(f32[256,1152]{1,0:T(8,128)S(1)} %get-tuple-element.231, bf16[4304,1152]{1,0:T(8,128)(2,1)} %get-tuple-element.89, f32[1152]{0:T(1024)S(1)} %copy-done.65, f32[256,4304]{0,1:T(8,128)} %convolution_add_fusion), kind=kOutput, calls=%fused_computation.20 | convolution fusion | flops 2549403648 | bytes 16097792 | tf_op jit(solution)/shard_map/dot_general | solution.py:409
  521.4 9.2 %collective-permute-done.117 = bf16[1472,128]{1,0:T(8,128)(2,1)S(1)} collective-permute-done((bf16[1472,128]{1,0:T(8,128)(2,1)S(1)}, bf16[1472,128]{1,0:T(8,128)(2,1)S(1)}, u32[]{:S(2)}, u32[]{:S(2)}) %collective-permute-start.117) | collective-permute-done | bytes 376864 | tf_op jit(solution)/shard_map/ppermute | solution.py:578
  553.8 10.8 %collective-permute-done.119 = bf16[1472,128]{1,0:T(8,128)(2,1)S(1)} collective-permute-done((bf16[1472,128]{1,0:T(8,128)(2,1)S(1)}, bf16[1472,128]{1,0:T(8,128)(2,1)S(1)}, u32[]{:S(2)}, u32[]{:S(2)}) %collective-permute-start.119) | collective-permute-done | bytes 376864 | tf_op jit(solution)/shard_map/ppermute | solution.py:578
  566.9 10.2 %collective-permute-done.94 = bf16[1888,128]{1,0:T(8,128)(2,1)S(1)} collective-permute-done((bf16[1888,128]{1,0:T(8,128)(2,1)S(1)}, bf16[1888,128]{1,0:T(8,128)(2,1)S(1)}, u32[]{:S(2)}, u32[]{:S(2)}) %collective-permute-start.94) | collective-permute-done | bytes 483360 | tf_op jit(solution)/shard_map/ppermute | solution.py:578
  581.4 15.9 %collective-permute-done.100 = bf16[1888,128]{1,0:T(8,128)(2,1)S(1)} collective-permute-done((bf16[1888,128]{1,0:T(8,128)(2,1)S(1)}, bf16[1888,128]{1,0:T(8,128)(2,1)S(1)}, u32[]{:S(2)}, u32[]{:S(2)}) %collective-permute-start.100) | collective-permute-done | bytes 483360 | tf_op jit(solution)/shard_map/ppermute | solution.py:578
  600.7 10.6 %collective-permute-done.89 = bf16[1888,128]{1,0:T(8,128)(2,1)S(1)} collective-permute-done((bf16[1888,128]{1,0:T(8,128)(2,1)S(1)}, bf16[1888,128]{1,0:T(8,128)(2,1)S(1)}, u32[]{:S(2)}, u32[]{:S(2)}) %collective-permute-start.89) | collective-permute-done | bytes 483360 | tf_op jit(solution)/shard_map/ppermute | solution.py:578
  655.7 12.7 %collective-permute-done.109 = bf16[3776,128]{1,0:T(8,128)(2,1)S(1)} collective-permute-done((bf16[3776,128]{1,0:T(8,128)(2,1)S(1)}, bf16[3776,128]{1,0:T(8,128)(2,1)S(1)}, u32[]{:S(2)}, u32[]{:S(2)}) %collective-permute-start.109) | collective-permute-done | bytes 966688 | tf_op jit(solution)/shard_map/ppermute | solution.py:578
  669.6 23.1 %collective-permute-done.104 = bf16[3776,128]{1,0:T(8,128)(2,1)S(1)} collective-permute-done((bf16[3776,128]{1,0:T(8,128)(2,1)S(1)}, bf16[3776,128]{1,0:T(8,128)(2,1)S(1)}, u32[]{:S(2)}, u32[]{:S(2)}) %collective-permute-start.104) | collective-permute-done | bytes 966688 | tf_op jit(solution)/shard_map/ppermute | solution.py:578
  695.0 12.0 %collective-permute-done.110 = bf16[3776,128]{1,0:T(8,128)(2,1)S(1)} collective-permute-done((bf16[3776,128]{1,0:T(8,128)(2,1)S(1)}, bf16[3776,128]{1,0:T(8,128)(2,1)S(1)}, u32[]{:S(2)}, u32[]{:S(2)}) %collective-permute-start.110) | collective-permute-done | bytes 966688 | tf_op jit(solution)/shard_map/ppermute | solution.py:578
  721.9 11.5 %collective-permute-done.111 = bf16[1888,128]{1,0:T(8,128)(2,1)S(1)} collective-permute-done((bf16[1888,128]{1,0:T(8,128)(2,1)S(1)}, bf16[1888,128]{1,0:T(8,128)(2,1)S(1)}, u32[]{:S(2)}, u32[]{:S(2)}) %collective-permute-start.111) | collective-permute-done | bytes 483360 | tf_op jit(solution)/shard_map/ppermute | solution.py:578
  765.5 9.3 %finish.1 = (f32[1,476288]{1,0:T(1,128)}, f32[1,476288]{1,0:T(1,128)}, f32[1,476288]{1,0:T(1,128)}, f32[1,476288]{1,0:T(1,128)}) custom-call(s32[5]{0:T(128)} %stack.23.place_ref, bf16[944,128]{1,0:T(8,128)(2,1)} %get-tuple-element.190.refs_0_, bf16[944,128]{1,0:T(8,128)(2,1)} %copy-done.48, bf16[944,128]{1,0:T(8,128)(2,1)} %copy-done.49, ...), custom_call_target="tpu_custom_call" | custom-call | tf_op jit(solution)/shard_map/finish/pallas_call | solution.py:824
  (488 shorter events, 362.6 us)
Async XLA Ops:
  82.5 30.8 %collective-permute-start.49 = (bf16[2832,128]{1,0:T(8,128)(2,1)S(1)}, bf16[2832,128]{1,0:T(8,128)(2,1)S(1)}, u32[]{:S(2)}, u32[]{:S(2)}) collective-permute-start(bf16[2832,128]{1,0:T(8,128)(2,1)S(1)} %pad_maximum_fusion.2.refs_0_), channel_id=1, source_target_pairs={{0,1},{1,0},{2,3},{3,2},{4,5},{5,4},{6,7},{7,6},{8,9},{9,8},{10,11... | collective-permute-start | bytes 2174984 | tf_op jit(solution)/shard_map/ppermute | solution.py:578
  82.5 33.8 %collective-permute-start.53 = (bf16[2832,128]{1,0:T(8,128)(2,1)S(1)}, bf16[2832,128]{1,0:T(8,128)(2,1)}, u32[]{:S(2)}, u32[]{:S(2)}) collective-permute-start(bf16[2832,128]{1,0:T(8,128)(2,1)S(1)} %pad_maximum_fusion.2.refs_0_), channel_id=1, source_target_pairs={{0,2},{1,3},{2,0},{3,1},{4,6},{5,7},{6,4},{7,5},{8,10},{9,11},{10,... | collective-permute-start | bytes 2174984 | tf_op jit(solution)/shard_map/ppermute | solution.py:578
  91.8 25.5 %collective-permute-start.21 = (bf16[944,128]{1,0:T(8,128)(2,1)}, bf16[944,128]{1,0:T(8,128)(2,1)S(1)}, u32[]{:S(2)}, u32[]{:S(2)}) collective-permute-start(bf16[944,128]{1,0:T(8,128)(2,1)} %collective-permute-done.20.refs_12_), channel_id=1, source_target_pairs={{0,8},{4,12},{8,0},{12,4},{16,24},{20,28},{24,16},{28,20},{1,9},{5... | collective-permute-start | bytes 725000 | tf_op jit(solution)/shard_map/ppermute | solution.py:578
  131.0 32.1 %collective-permute-start.50 = (bf16[2832,128]{1,0:T(8,128)(2,1)S(1)}, bf16[2832,128]{1,0:T(8,128)(2,1)}, u32[]{:S(2)}, u32[]{:S(2)}) collective-permute-start(bf16[2832,128]{1,0:T(8,128)(2,1)S(1)} %collective-permute-done.49.refs_4_), channel_id=1, source_target_pairs={{0,8},{4,12},{8,0},{12,4},{16,24},{20,28},{24,16},{28,20},{1,9},{5... | collective-permute-start | bytes 2174984 | tf_op jit(solution)/shard_map/ppermute | solution.py:578
  132.4 35.8 %collective-permute-start.51 = (bf16[2832,128]{1,0:T(8,128)(2,1)S(1)}, bf16[2832,128]{1,0:T(8,128)(2,1)}, u32[]{:S(2)}, u32[]{:S(2)}) collective-permute-start(bf16[2832,128]{1,0:T(8,128)(2,1)S(1)} %collective-permute-done.49.refs_4_), channel_id=1, source_target_pairs={{0,16},{4,20},{8,24},{12,28},{16,0},{20,4},{24,8},{28,12},{1,17},{... | collective-permute-start | bytes 2174984 | tf_op jit(solution)/shard_map/ppermute | solution.py:578
  149.9 28.2 %collective-permute-start.54 = (bf16[2832,128]{1,0:T(8,128)(2,1)}, bf16[2832,128]{1,0:T(8,128)(2,1)}, u32[]{:S(2)}, u32[]{:S(2)}) collective-permute-start(bf16[2832,128]{1,0:T(8,128)(2,1)} %collective-permute-done.53.refs_8_), channel_id=1, source_target_pairs={{0,8},{4,12},{8,0},{12,4},{16,24},{20,28},{24,16},{28,20},{1,9},{5... | collective-permute-start | bytes 2174984 | tf_op jit(solution)/shard_map/ppermute | solution.py:578
  151.0 28.4 %collective-permute-start.55 = (bf16[2832,128]{1,0:T(8,128)(2,1)}, bf16[2832,128]{1,0:T(8,128)(2,1)}, u32[]{:S(2)}, u32[]{:S(2)}) collective-permute-start(bf16[2832,128]{1,0:T(8,128)(2,1)} %collective-permute-done.53.refs_8_), channel_id=1, source_target_pairs={{0,16},{4,20},{8,24},{12,28},{16,0},{20,4},{24,8},{28,12},{1,17},{... | collective-permute-start | bytes 2174984 | tf_op jit(solution)/shard_map/ppermute | solution.py:578
  152.5 37.6 %collective-permute-start.65 = (bf16[2832,128]{1,0:T(8,128)(2,1)S(1)}, bf16[2832,128]{1,0:T(8,128)(2,1)}, u32[]{:S(2)}, u32[]{:S(2)}) collective-permute-start(bf16[2832,128]{1,0:T(8,128)(2,1)S(1)} %collective-permute-done.49.refs_4_), channel_id=1, source_target_pairs={{0,4},{4,0},{8,12},{12,8},{16,20},{20,16},{24,28},{28,24},{1,5},{5... | collective-permute-start | bytes 2174984 | tf_op jit(solution)/shard_map/ppermute | solution.py:578
  163.1 27.1 %collective-permute-start.57 = (bf16[2832,128]{1,0:T(8,128)(2,1)}, bf16[2832,128]{1,0:T(8,128)(2,1)}, u32[]{:S(2)}, u32[]{:S(2)}) collective-permute-start(bf16[2832,128]{1,0:T(8,128)(2,1)} %collective-permute-done.53.refs_8_), channel_id=1, source_target_pairs={{0,1},{1,0},{2,3},{3,2},{4,5},{5,4},{6,7},{7,6},{8,9},{9,8},{10,11... | collective-permute-start | bytes 2174984 | tf_op jit(solution)/shard_map/ppermute | solution.py:578
  168.2 31.6 %collective-permute-start.40 = (bf16[256,864]{1,0:T(8,128)(2,1)}, bf16[256,864]{1,0:T(8,128)(2,1)S(1)}, u32[]{:S(2)}, u32[]{:S(2)}) collective-permute-start(bf16[256,864]{1,0:T(8,128)(2,1)} %bitcast.129), channel_id=1, source_target_pairs={{0,1},{1,0},{2,3},{3,2},{4,5},{5,4},{6,7},{7,6},{8,9},{9,8},{10,11... | collective-permute-start | bytes 1327112 | tf_op jit(solution)/shard_map/ppermute | solution.py:578
  178.1 34.2 %collective-permute-start.41 = (bf16[256,864]{1,0:T(8,128)(2,1)}, bf16[256,864]{1,0:T(8,128)(2,1)S(1)}, u32[]{:S(2)}, u32[]{:S(2)}) collective-permute-start(bf16[256,864]{1,0:T(8,128)(2,1)} %bitcast.130), channel_id=1, source_target_pairs={{0,2},{1,3},{2,0},{3,1},{4,6},{5,7},{6,4},{7,5},{8,10},{9,11},{10,... | collective-permute-start | bytes 1327112 | tf_op jit(solution)/shard_map/ppermute | solution.py:578
  179.4 32.9 %collective-permute-start.42 = (bf16[256,864]{1,0:T(8,128)(2,1)}, bf16[256,864]{1,0:T(8,128)(2,1)S(1)}, u32[]{:S(2)}, u32[]{:S(2)}) collective-permute-start(bf16[256,864]{1,0:T(8,128)(2,1)} %bitcast.131), channel_id=1, source_target_pairs={{0,3},{1,2},{2,1},{3,0},{4,7},{5,6},{6,5},{7,4},{8,11},{9,10},{10,... | collective-permute-start | bytes 1327112 | tf_op jit(solution)/shard_map/ppermute | solution.py:578
  190.2 40.2 %collective-permute-start.69 = (bf16[2832,128]{1,0:T(8,128)(2,1)}, bf16[2832,128]{1,0:T(8,128)(2,1)}, u32[]{:S(2)}, u32[]{:S(2)}) collective-permute-start(bf16[2832,128]{1,0:T(8,128)(2,1)} %collective-permute-done.53.refs_8_), channel_id=1, source_target_pairs={{0,4},{4,0},{8,12},{12,8},{16,20},{20,16},{24,28},{28,24},{1,5},{5... | collective-permute-start | bytes 2174984 | tf_op jit(solution)/shard_map/ppermute | solution.py:578
  190.2 49.2 %collective-permute-start.48 = (bf16[2832,128]{1,0:T(8,128)(2,1)}, bf16[2832,128]{1,0:T(8,128)(2,1)S(1)}, u32[]{:S(2)}, u32[]{:S(2)}) collective-permute-start(bf16[2832,128]{1,0:T(8,128)(2,1)} %copy-done.14), channel_id=1, source_target_pairs={{0,16},{4,20},{8,24},{12,28},{16,0},{20,4},{24,8},{28,12},{1,17},{... | collective-permute-start | bytes 2174984 | tf_op jit(solution)/shard_map/ppermute | solution.py:578
  199.8 39.6 %collective-permute-start.62 = (bf16[2832,128]{1,0:T(8,128)(2,1)}, bf16[2832,128]{1,0:T(8,128)(2,1)}, u32[]{:S(2)}, u32[]{:S(2)}) collective-permute-start(bf16[2832,128]{1,0:T(8,128)(2,1)} %copy-done.14), channel_id=1, source_target_pairs={{0,4},{4,0},{8,12},{12,8},{16,20},{20,16},{24,28},{28,24},{1,5},{5... | collective-permute-start | bytes 2174984 | tf_op jit(solution)/shard_map/ppermute | solution.py:578
  212.3 29.5 %collective-permute-start.63 = (bf16[2832,128]{1,0:T(8,128)(2,1)}, bf16[2832,128]{1,0:T(8,128)(2,1)}, u32[]{:S(2)}, u32[]{:S(2)}) collective-permute-start(bf16[2832,128]{1,0:T(8,128)(2,1)} %collective-permute-done.47.refs_2_), channel_id=1, source_target_pairs={{0,4},{4,0},{8,12},{12,8},{16,20},{20,16},{24,28},{28,24},{1,5},{5... | collective-permute-start | bytes 2174984 | tf_op jit(solution)/shard_map/ppermute | solution.py:578
  212.3 44.8 %collective-permute-start.52 = (bf16[2832,128]{1,0:T(8,128)(2,1)}, bf16[2832,128]{1,0:T(8,128)(2,1)}, u32[]{:S(2)}, u32[]{:S(2)}) collective-permute-start(bf16[2832,128]{1,0:T(8,128)(2,1)} %collective-permute-done.51.refs_6_), channel_id=1, source_target_pairs={{0,8},{4,12},{8,0},{12,4},{16,24},{20,28},{24,16},{28,20},{1,9},{5... | collective-permute-start | bytes 2174984 | tf_op jit(solution)/shard_map/ppermute | solution.py:578
  402.9 225.2 %collective-permute-start.103 = (bf16[30208,128]{1,0:T(8,128)(2,1)}, bf16[30208,128]{1,0:T(8,128)(2,1)}, u32[]{:S(2)}, u32[]{:S(2)}) collective-permute-start(bf16[30208,128]{1,0:T(8,128)(2,1)} %get-tuple-element.123), channel_id=1, source_target_pairs={{0,4},{4,0},{8,12},{12,8},{16,20},{20,16},{24,28},{28,24},{1,5},{5... | collective-permute-start | bytes 23199752 | tf_op jit(solution)/shard_map/ppermute | solution.py:578
  436.0 23.6 %collective-permute-start.82 = (bf16[256,864]{1,0:T(8,128)(2,1)}, bf16[256,864]{1,0:T(8,128)(2,1)}, u32[]{:S(2)}, u32[]{:S(2)}) collective-permute-start(bf16[256,864]{1,0:T(8,128)(2,1)} %get-tuple-element.96), channel_id=1, source_target_pairs={{0,1},{1,0},{2,3},{3,2},{4,5},{5,4},{6,7},{7,6},{8,9},{9,8},{10,11... | collective-permute-start | bytes 1327112 | tf_op jit(solution)/shard_map/ppermute | solution.py:578
  440.1 34.3 %collective-permute-start.81 = (bf16[256,864]{1,0:T(8,128)(2,1)}, bf16[256,864]{1,0:T(8,128)(2,1)}, u32[]{:S(2)}, u32[]{:S(2)}) collective-permute-start(bf16[256,864]{1,0:T(8,128)(2,1)} %get-tuple-element.95), channel_id=1, source_target_pairs={{0,2},{1,3},{2,0},{3,1},{4,6},{5,7},{6,4},{7,5},{8,10},{9,11},{10,... | collective-permute-start | bytes 1327112 | tf_op jit(solution)/shard_map/ppermute | solution.py:578
  440.2 34.2 %collective-permute-start.80 = (bf16[256,864]{1,0:T(8,128)(2,1)}, bf16[256,864]{1,0:T(8,128)(2,1)}, u32[]{:S(2)}, u32[]{:S(2)}) collective-permute-start(bf16[256,864]{1,0:T(8,128)(2,1)} %get-tuple-element.94), channel_id=1, source_target_pairs={{0,3},{1,2},{2,1},{3,0},{4,7},{5,6},{6,5},{7,4},{8,11},{9,10},{10,... | collective-permute-start | bytes 1327112 | tf_op jit(solution)/shard_map/ppermute | solution.py:578
  457.1 92.1 %collective-permute-start.93 = (bf16[15104,128]{1,0:T(8,128)(2,1)}, bf16[15104,128]{1,0:T(8,128)(2,1)}, u32[]{:S(2)}, u32[]{:S(2)}) collective-permute-start(bf16[15104,128]{1,0:T(8,128)(2,1)} %get-tuple-element.113), channel_id=1, source_target_pairs={{0,4},{4,0},{8,12},{12,8},{16,20},{20,16},{24,28},{28,24},{1,5},{5... | collective-permute-start | bytes 11599880 | tf_op jit(solution)/shard_map/ppermute | solution.py:578
  519.2 58.9 %collective-permute-start.83 = (bf16[15104,128]{1,0:T(8,128)(2,1)S(1)}, bf16[15104,128]{1,0:T(8,128)(2,1)S(1)}, u32[]{:S(2)}, u32[]{:S(2)}) collective-permute-start(bf16[15104,128]{1,0:T(8,128)(2,1)S(1)} %copy-done.72), channel_id=1, source_target_pairs={{0,4},{4,0},{8,12},{12,8},{16,20},{20,16},{24,28},{28,24},{1,5},{5... | collective-permute-start | bytes 11599880 | tf_op jit(solution)/shard_map/ppermute | solution.py:578
  540.7 23.9 %collective-permute-start.119 = (bf16[1472,128]{1,0:T(8,128)(2,1)S(1)}, bf16[1472,128]{1,0:T(8,128)(2,1)S(1)}, u32[]{:S(2)}, u32[]{:S(2)}) collective-permute-start(bf16[1472,128]{1,0:T(8,128)(2,1)S(1)} %add_convert_fusion.42), channel_id=1, source_target_pairs={{0,2},{1,3},{2,0},{3,1},{4,6},{5,7},{6,4},{7,5},{8,10},{9,11},{10,... | collective-permute-start | bytes 1130504 | tf_op jit(solution)/shard_map/ppermute | solution.py:578
  564.7 193.2 %collective-permute-start.120 = (bf16[1472,128]{1,0:T(8,128)(2,1)S(1)}, bf16[1472,128]{1,0:T(8,128)(2,1)S(1)}, u32[]{:S(2)}, u32[]{:S(2)}) collective-permute-start(bf16[1472,128]{1,0:T(8,128)(2,1)S(1)} %add_convert_fusion.41), channel_id=1, source_target_pairs={{0,1},{1,0},{2,3},{3,2},{4,5},{5,4},{6,7},{7,6},{8,9},{9,8},{10,11... | collective-permute-start | bytes 1130504 | tf_op jit(solution)/shard_map/ppermute | solution.py:578
  598.6 35.1 %collective-permute-start.88 = (bf16[1888,128]{1,0:T(8,128)(2,1)S(1)}, bf16[1888,128]{1,0:T(8,128)(2,1)S(1)}, u32[]{:S(2)}, u32[]{:S(2)}) collective-permute-start(bf16[1888,128]{1,0:T(8,128)(2,1)S(1)} %get-tuple-element.109), channel_id=1, source_target_pairs={{0,8},{4,12},{8,0},{12,4},{16,24},{20,28},{24,16},{28,20},{1,9},{5... | collective-permute-start | bytes 1449992 | tf_op jit(solution)/shard_map/ppermute | solution.py:578
  599.7 38.6 %collective-permute-start.86 = (bf16[1888,128]{1,0:T(8,128)(2,1)S(1)}, bf16[1888,128]{1,0:T(8,128)(2,1)S(1)}, u32[]{:S(2)}, u32[]{:S(2)}) collective-permute-start(bf16[1888,128]{1,0:T(8,128)(2,1)S(1)} %get-tuple-element.107), channel_id=1, source_target_pairs={{0,16},{4,20},{8,24},{12,28},{16,0},{20,4},{24,8},{28,12},{1,17},{... | collective-permute-start | bytes 1449992 | tf_op jit(solution)/shard_map/ppermute | solution.py:578
  626.8 106.8 %collective-permute-start.97 = (bf16[944,128]{1,0:T(8,128)(2,1)S(1)}, bf16[944,128]{1,0:T(8,128)(2,1)S(1)}, u32[]{:S(2)}, u32[]{:S(2)}) collective-permute-start(bf16[944,128]{1,0:T(8,128)(2,1)S(1)} %slice.436), channel_id=1, source_target_pairs={{0,1},{1,0},{2,3},{3,2},{4,5},{5,4},{6,7},{7,6},{8,9},{9,8},{10,11... | collective-permute-start | bytes 725000 | tf_op jit(solution)/shard_map/ppermute | solution.py:578
  636.9 31.5 %collective-permute-start.109 = (bf16[3776,128]{1,0:T(8,128)(2,1)S(1)}, bf16[3776,128]{1,0:T(8,128)(2,1)S(1)}, u32[]{:S(2)}, u32[]{:S(2)}) collective-permute-start(bf16[3776,128]{1,0:T(8,128)(2,1)S(1)} %get-tuple-element.131), channel_id=1, source_target_pairs={{0,8},{4,12},{8,0},{12,4},{16,24},{20,28},{24,16},{28,20},{1,9},{5... | collective-permute-start | bytes 2899976 | tf_op jit(solution)/shard_map/ppermute | solution.py:578
  638.3 97.2 %collective-permute-start.102 = (bf16[944,128]{1,0:T(8,128)(2,1)S(1)}, bf16[944,128]{1,0:T(8,128)(2,1)S(1)}, u32[]{:S(2)}, u32[]{:S(2)}) collective-permute-start(bf16[944,128]{1,0:T(8,128)(2,1)S(1)} %add_convert_fusion.46), channel_id=1, source_target_pairs={{0,2},{1,3},{2,0},{3,1},{4,6},{5,7},{6,4},{7,5},{8,10},{9,11},{10,... | collective-permute-start | bytes 725000 | tf_op jit(solution)/shard_map/ppermute | solution.py:578
  653.9 39.9 %collective-permute-start.108 = (bf16[3776,128]{1,0:T(8,128)(2,1)S(1)}, bf16[3776,128]{1,0:T(8,128)(2,1)S(1)}, u32[]{:S(2)}, u32[]{:S(2)}) collective-permute-start(bf16[3776,128]{1,0:T(8,128)(2,1)S(1)} %get-tuple-element.129), channel_id=1, source_target_pairs={{0,8},{4,12},{8,0},{12,4},{16,24},{20,28},{24,16},{28,20},{1,9},{5... | collective-permute-start | bytes 2899976 | tf_op jit(solution)/shard_map/ppermute | solution.py:578
  668.4 24.3 %collective-permute-start.104 = (bf16[3776,128]{1,0:T(8,128)(2,1)S(1)}, bf16[3776,128]{1,0:T(8,128)(2,1)S(1)}, u32[]{:S(2)}, u32[]{:S(2)}) collective-permute-start(bf16[3776,128]{1,0:T(8,128)(2,1)S(1)} %get-tuple-element.126), channel_id=1, source_target_pairs={{0,16},{4,20},{8,24},{12,28},{16,0},{20,4},{24,8},{28,12},{1,17},{... | collective-permute-start | bytes 2899976 | tf_op jit(solution)/shard_map/ppermute | solution.py:578
  (168 other events, 2507.9 us)

commit v5 on v4

--- a/solution.py
+++ b/solution.py
@@ -658,6 +658,7 @@
             for index in range(2 * layout.columns)
         ]
     )
+    first_parts = parts
     if layout.columns == 4:
         low = add(parts[2], exchange(parts[6], "dp", 4))
         high = add(parts[5], exchange(parts[7], "dp", 2))
@@ -686,7 +687,7 @@
             moved = exchange(held.pop(key), "ctx", bit)
             held[key ^ bit] = add(held[key ^ bit], moved)
         bit *= 2
-    return held[0]
+    return held[0], first_parts
 
 
 def bits(layout):
@@ -710,7 +711,7 @@
     owner = jnp.concatenate(
         [jnp.full((rows.shape[0], 1), source, jnp.int32) for source, rows in sources]
     )
-    for bit in bits(layout):
+    for bit in reversed(bits(layout)):
         other = everywhere(layout, held, bit)
         held = jnp.where(((owner ^ shard) & bit) == 0, held, other)
     return held
@@ -899,7 +900,6 @@
     normed_two_round = (unit_two * gain_two + shift_two).astype(BF)
     pre_gelu = dense(normed_two_round, up_weight) + bias_up
     activated = jax.nn.gelu(pre_gelu, approximate=True).astype(BF)
-    output = (middle + dense(activated, down_weight) + bias_down).astype(BF)
 
     positions = lax.axis_index("ctx") * local_rows + jnp.arange(local_rows, dtype=jnp.int32)
     row_valid = (positions < counts[0])[:, None].astype(F32)
@@ -918,7 +918,7 @@
         layout, place, (middle_group, layout.columns), {"up": grad_up, "down": grad_down}
     )
     grad_pre_round, terms = lax.optimization_barrier((grad_pre_round, terms))
-    sum_last = scatter(layout, *terms)
+    sum_last, _ = scatter(layout, *terms)
     grad_normed_two = dot_t(grad_pre_round, up_weight)
     grad_gain_two = jnp.sum(grad_normed_two * unit_two, 0)
     grad_shift_two = jnp.sum(grad_normed_two, 0)
@@ -931,7 +931,7 @@
     terms = gradient_pieces(
         layout, place, (layout.first, middle_group), {"out": grad_out, "up": grad_up}
     )
-    sum_middle = scatter(layout, *terms)
+    sum_middle, _ = scatter(layout, *terms)
     grad_packed, sums = attend_back(
         counts, place, packed, log_total, grad_mixed_heads, chunk
     )
@@ -943,7 +943,11 @@
     grad_projected, leftover_terms, *terms = lax.optimization_barrier(
         (grad_projected, leftover_terms, *terms)
     )
-    sum_first = scatter(layout, *terms)
+    sum_first, kept_first = scatter(layout, *terms)
+    grad_projected, activated, _ = lax.optimization_barrier(
+        (grad_projected, activated, kept_first)
+    )
+    output = (middle + dense(activated, down_weight) + bias_down).astype(BF)
     grad_normed_one = dot_t(grad_projected, qkv_weight)
     grad_gain_one = jnp.sum(grad_normed_one * unit_one, 0)
     grad_shift_one = jnp.sum(grad_normed_one, 0)

time: 785 us -> 744 us (0.948)
  waiting for transfers between devices: 383 us -> 333 us
  other arithmetic: 22.5 us -> 35.6 us
  starting transfers between devices: 119 us -> 128 us
  matrix products: 80.3 us -> 71.9 us
    ppermute x120, waiting for transfers between devices: 383 us -> 332 us  [exchange(): lax.ppermute(array, axis, [(index, index ^ bit) for index in range(size)])]
    convert_element_type x26, other arithmetic: 13.4 us -> 26.7 us  [add(): functools.reduce(jnp.add, [array.astype(F32) for array in arrays])]
    ppermute x120, starting transfers between devices: 114 us -> 123 us  [exchange(): lax.ppermute(array, axis, [(index, index ^ bit) for index in range(size)])]
  transfers between devices with their start and end apart: 121 -> 121, of which waited for: 51 -> 50; matrix products, arithmetic and copies ran while one was open for 10% -> 13% of each run, Pallas kernels for 9% -> 7%
where the time goes in v5:
time: 744 us; the launch traced here: 734 us
  waiting for transfers between devices  333 us (45%)
  starting transfers between devices  128 us (17%)
  Pallas kernels  125 us (17%)
  matrix products  71.9 us (10%)
  local copies, waits for them, and re-layouts  37.9 us (5%)
  other arithmetic  35.6 us (5%)
    ppermute x120, waiting for transfers between devices, exchange(): lax.ppermute(array, axis, [(index, index ^ bit) for index in range(size)])  332 us
    ppermute x120, starting transfers between devices, exchange(): lax.ppermute(array, axis, [(index, index ^ bit) for index in range(size)])  123 us
    pallas_call x3, Pallas kernels, gradient_pieces(): pl.pallas_call(kernel, grid=(steps,), in_specs=[pl.BlockSpec(memory_space...  39.6 us
    convert_element_type x26, other arithmetic, add(): functools.reduce(jnp.add, [array.astype(F32) for array in arrays])  26.7 us
    dot_general x4, matrix products, dense(): return jnp.dot(left, right, preferred_element_type=F32)  24.8 us
    dot_general x4, matrix products, dot_t(): lax.dot_general(left, right, (((1,), (1,)), ((), ())), preferred_element_...  24.3 us
    pallas_call x1, Pallas kernels, attend_back(): pl.pallas_call(kernel, name='attend_back', grid=(heads,), in_specs=[pl.Bl...  22.8 us
    dot_general x4, matrix products, t_dot(): lax.dot_general(left, right, (((0,), (0,)), ((), ())), preferred_element_...  22.7 us
  transfers between devices with their start and end apart: 121, of which 50 were waited for; matrix products, arithmetic and copies ran while one was open for 13% of the time, Pallas kernels for 7%

profile of v5, /device:TPU:0, one launch (start us, length us, event | category | flops | bytes accessed | tf_op | source)
XLA Modules:
  0.0 733.9 jit_solution(5320325461218677686)
XLA Ops:
  26.1 11.3 %collective-permute-done.2 = bf16[1472,128]{1,0:T(8,128)(2,1)S(1)} collective-permute-done((bf16[1472,128]{1,0:T(8,128)(2,1)S(1)}, bf16[1472,128]{1,0:T(8,128)(2,1)S(1)}, u32[]{:S(2)}, u32[]{:S(2)}) %collective-permute-start.2) | collective-permute-done | bytes 376864 | tf_op jit(solution)/shard_map/ppermute | solution.py:578
  75.7 8.5 %collective-permute-done.4 = bf16[1472,128]{1,0:T(8,128)(2,1)S(1)} collective-permute-done((bf16[1472,128]{1,0:T(8,128)(2,1)S(1)}, bf16[1472,128]{1,0:T(8,128)(2,1)S(1)}, u32[]{:S(2)}, u32[]{:S(2)}) %collective-permute-start.4) | collective-permute-done | bytes 376864 | tf_op jit(solution)/shard_map/ppermute | solution.py:578
  93.8 9.6 %collective-permute-done.49.refs_4_ = bf16[2832,128]{1,0:T(8,128)(2,1)} collective-permute-done((bf16[2832,128]{1,0:T(8,128)(2,1)S(1)}, bf16[2832,128]{1,0:T(8,128)(2,1)}, u32[]{:S(2)}, u32[]{:S(2)}) %collective-permute-start.49) | collective-permute-done | bytes 725024 | tf_op jit(solution)/shard_map/ppermute | solution.py:578
  103.4 11.8 %collective-permute-done.53.refs_8_ = bf16[2832,128]{1,0:T(8,128)(2,1)} collective-permute-done((bf16[2832,128]{1,0:T(8,128)(2,1)S(1)}, bf16[2832,128]{1,0:T(8,128)(2,1)}, u32[]{:S(2)}, u32[]{:S(2)}) %collective-permute-start.53) | collective-permute-done | bytes 725024 | tf_op jit(solution)/shard_map/ppermute | solution.py:578
  116.7 9.2 %collective-permute-done.5 = bf16[1472,128]{1,0:T(8,128)(2,1)S(1)} collective-permute-done((bf16[1472,128]{1,0:T(8,128)(2,1)S(1)}, bf16[1472,128]{1,0:T(8,128)(2,1)S(1)}, u32[]{:S(2)}, u32[]{:S(2)}) %collective-permute-start.5) | collective-permute-done | bytes 376864 | tf_op jit(solution)/shard_map/ppermute | solution.py:578
  140.3 10.3 %first_weights.1 = bf16[1152,3456]{1,0:T(8,128)(2,1)} custom-call(s32[5]{0:T(128)} %stack.23.place_ref, bf16[944,128]{1,0:T(8,128)(2,1)} %copy-done.22, bf16[944,128]{1,0:T(8,128)(2,1)} %copy-done.38, bf16[944,128]{1,0:T(8,128)(2,1)} %copy-done.41, bf16[944,128]{1,0:T(8,128)(2,1)} %copy-done.43, bf16[944,128]{1,0:T(8,128)(2,1)} %copy-done.39, ...), custom_call_target="tpu_custom_call" | custom-call | tf_op jit(solution)/shard_map/first_weights/pallas_call | solution.py:215
  158.5 11.5 %collective-permute-done.50.refs_5_ = bf16[2832,128]{1,0:T(8,128)(2,1)} collective-permute-done((bf16[2832,128]{1,0:T(8,128)(2,1)}, bf16[2832,128]{1,0:T(8,128)(2,1)}, u32[]{:S(2)}, u32[]{:S(2)}) %collective-permute-start.50) | collective-permute-done | bytes 725024 | tf_op jit(solution)/shard_map/ppermute | solution.py:578
  189.0 9.0 %collective-permute-done.57.refs_12_ = bf16[2832,128]{1,0:T(8,128)(2,1)} collective-permute-done((bf16[2832,128]{1,0:T(8,128)(2,1)}, bf16[2832,128]{1,0:T(8,128)(2,1)}, u32[]{:S(2)}, u32[]{:S(2)}) %collective-permute-start.57) | collective-permute-done | bytes 725024 | tf_op jit(solution)/shard_map/ppermute | solution.py:578
  206.7 12.5 %collective-permute-done.41.refs_2_ = bf16[256,864]{1,0:T(8,128)(2,1)S(1)} collective-permute-done((bf16[256,864]{1,0:T(8,128)(2,1)}, bf16[256,864]{1,0:T(8,128)(2,1)S(1)}, u32[]{:S(2)}, u32[]{:S(2)}) %collective-permute-start.41) | collective-permute-done | bytes 442400 | tf_op jit(solution)/shard_map/ppermute | solution.py:578
  221.6 15.2 %attend.1 = (bf16[256,288]{1,0:T(8,128)(2,1)}, bf16[256,288]{1,0:T(8,128)(2,1)}, bf16[256,288]{1,0:T(8,128)(2,1)}, bf16[256,288]{1,0:T(8,128)(2,1)}, f32[4,1024,1]{2,1,0:T(8,128)}) custom-call(s32[1]{0:T(128)} %copy.34.count, s32[5]{0:T(128)} %stack.23.place_ref, bf16[256,864]{1,0:T(8,128)(2,1)} %bitcast.128, bf16[256,864]{1,0:T(8,128)(2,1)} %copy-done.17, ...), custom_call_target="tpu_custom_call" | custom-call | tf_op jit(solution)/shard_map/attend/pallas_call | solution.py:465
  236.8 9.0 %collective-permute-start.45 = (bf16[256,288]{1,0:T(8,128)(2,1)}, bf16[256,288]{1,0:T(8,128)(2,1)S(1)}, u32[]{:S(2)}, u32[]{:S(2)}) collective-permute-start(bf16[256,288]{1,0:T(8,128)(2,1)} %get-tuple-element.82), channel_id=1, source_target_pairs={{0,1},{1,0},{2,3},{3,2},{4,5},{5,4},{6,7},{7,6},{8,9},{9,8},{10,11... | collective-permute-start | bytes 442376 | tf_op jit(solution)/shard_map/ppermute | solution.py:578
  253.6 8.6 %collective-permute-done.44 = bf16[256,288]{1,0:T(8,128)(2,1)S(1)} collective-permute-done((bf16[256,288]{1,0:T(8,128)(2,1)}, bf16[256,288]{1,0:T(8,128)(2,1)S(1)}, u32[]{:S(2)}, u32[]{:S(2)}) %collective-permute-start.44) | collective-permute-done | bytes 147488 | tf_op jit(solution)/shard_map/ppermute | solution.py:578
  268.1 12.1 %collective-permute-done.59.refs_14_ = bf16[2832,128]{1,0:T(8,128)(2,1)} collective-permute-done((bf16[2832,128]{1,0:T(8,128)(2,1)}, bf16[2832,128]{1,0:T(8,128)(2,1)}, u32[]{:S(2)}, u32[]{:S(2)}) %collective-permute-start.59) | collective-permute-done | bytes 725024 | tf_op jit(solution)/shard_map/ppermute | solution.py:578
  283.8 15.5 %collective-permute-done.60.refs_15_ = bf16[2832,128]{1,0:T(8,128)(2,1)} collective-permute-done((bf16[2832,128]{1,0:T(8,128)(2,1)}, bf16[2832,128]{1,0:T(8,128)(2,1)}, u32[]{:S(2)}, u32[]{:S(2)}) %collective-permute-start.60) | collective-permute-done | bytes 725024 | tf_op jit(solution)/shard_map/ppermute | solution.py:578
  301.8 22.3 %other_weights.1 = (bf16[1152,1152]{1,0:T(8,128)(2,1)}, bf16[1152,4304]{1,0:T(8,128)(2,1)}, bf16[4304,1152]{1,0:T(8,128)(2,1)}) custom-call(s32[5]{0:T(128)} %stack.23.place_ref, bf16[2832,128]{1,0:T(8,128)(2,1)} %copy-done.8, bf16[2832,128]{1,0:T(8,128)(2,1)} %copy-done.23, bf16[2832,128]{1,0:T(8,128)(2,1)} %copy-done.25, ...), custom_call_target="tpu_custom_call" | custom-call | tf_op jit(solution)/shard_map/other_weights/pallas_call | solution.py:258
  327.4 8.2 %multiply_convert_fusion = (bf16[256,4304]{0,1:T(8,128)(2,1)S(1)}, f32[256,4304]{0,1:T(8,128)S(1)}) fusion(f32[4304]{0:T(1024)S(1)} %slice.401, bf16[1152,4304]{1,0:T(8,128)(2,1)} %get-tuple-element.92, f32[256,1152]{1,0:T(8,128)S(1)} %get-tuple-element.235, f32[1152]{0:T(1024)S(1)} %copy-done.68, f32[1152]{0:T(1024)S(1)} %get-tuple-element.223, ...), kind=kOutput, calls=%fused_computation.13 | convolution fusion | flops 2551095296 | bytes 17735488 | tf_op jit(solution)/shard_map/dot_general | solution.py:409
  354.0 16.6 %shard_map.109 = (bf16[30208,128]{1,0:T(8,128)(2,1)}, bf16[30208,128]{1,0:T(8,128)(2,1)}) custom-call(s32[5]{0:T(128)} %stack.23.place_ref, bf16[1152,4304]{1,0:T(8,128)(2,1)} %convolution_convert_fusion.1.refs_0_.refs_1_, bf16[4304,1152]{1,0:T(8,128)(2,1)} %convolution_convert_fusion.refs_1_), custom_call_target="tpu_custom_call" | custom-call | tf_op jit(solution)/shard_map/pallas_call | solution.py:384
  370.6 8.6 %multiply_reduce_fusion = (bf16[1152]{0:T(1024)(128)(2,1)}, f32[256]{0:T(256)S(1)}, f32[256]{0:T(256)S(1)}, bf16[1152]{0:T(1024)(128)(2,1)}, f32[256,1152]{1,0:T(8,128)S(1)}) fusion(f32[256,1152]{1,0:T(8,128)S(1)} %get-tuple-element.235, f32[256]{0:T(256)S(1)} %add_rsqrt_fusion, f32[256]{0:T(256)S(1)} %broadcast_multiply_fusion.4, ...), kind=kOutput, calls=%fused_computation.59 | convolution fusion | flops 2541254144 | bytes 14492672 | tf_op jit(solution)/shard_map/dot_general | solution.py:401
  398.4 10.6 %collective-permute-done.78.refs_6_ = bf16[256,288]{1,0:T(8,128)(2,1)} collective-permute-done((bf16[256,288]{1,0:T(8,128)(2,1)}, bf16[256,288]{1,0:T(8,128)(2,1)}, u32[]{:S(2)}, u32[]{:S(2)}) %collective-permute-start.78) | collective-permute-done | bytes 147488 | tf_op jit(solution)/shard_map/ppermute | solution.py:578
  409.0 22.8 %attend_back.1 = (bf16[256,864]{1,0:T(8,128)(2,1)}, bf16[256,864]{1,0:T(8,128)(2,1)}, bf16[256,864]{1,0:T(8,128)(2,1)}, bf16[256,864]{1,0:T(8,128)(2,1)}, f32[4,2,72]{2,1,0:T(2,128)}) custom-call(s32[1]{0:T(128)} %copy.34.count, s32[5]{0:T(128)} %stack.23.place_ref, f32[4,1024,1]{2,1,0:T(8,128)} %get-tuple-element.90.logs, bf16[256,864]{1,0:T(8,128)(2,1)} %bitcast.129, ...), custom_call_target="tpu_custom_call" | custom-call | tf_op jit(solution)/shard_map/attend_back/pallas_call | solution.py:527
  442.3 12.2 %shard_map.111 = (bf16[15104,128]{1,0:T(8,128)(2,1)}, bf16[15104,128]{1,0:T(8,128)(2,1)}) custom-call(s32[5]{0:T(128)} %stack.23.place_ref, bf16[1152,1152]{1,0:T(8,128)(2,1)} %convolution_convert_fusion.3.refs_0_, bf16[1152,4304]{1,0:T(8,128)(2,1)} %convolution_convert_fusion.1.refs_0_.refs_1_), custom_call_target="tpu_custom_call" | custom-call | tf_op jit(solution)/shard_map/pallas_call | solution.py:384
  454.8 15.4 %collective-permute-done.81 = bf16[256,864]{1,0:T(8,128)(2,1)} collective-permute-done((bf16[256,864]{1,0:T(8,128)(2,1)}, bf16[256,864]{1,0:T(8,128)(2,1)}, u32[]{:S(2)}, u32[]{:S(2)}) %collective-permute-start.81) | collective-permute-done | bytes 442400 | tf_op jit(solution)/shard_map/ppermute | solution.py:578
  487.2 10.8 %shard_map.110 = (bf16[15104,128]{1,0:T(8,128)(2,1)}, bf16[15104,128]{1,0:T(8,128)(2,1)}, bf16[1344,128]{1,0:T(8,128)(2,1)}) custom-call(s32[5]{0:T(128)} %stack.23.place_ref, bf16[1152,3456]{1,0:T(8,128)(2,1)} %convolution_convert_fusion.2.refs_0_), custom_call_target="tpu_custom_call" | custom-call | tf_op jit(solution)/shard_map/pallas_call | solution.py:384
  507.9 10.1 %collective-permute-done.99 = bf16[1888,128]{1,0:T(8,128)(2,1)} collective-permute-done((bf16[1888,128]{1,0:T(8,128)(2,1)}, bf16[1888,128]{1,0:T(8,128)(2,1)}, u32[]{:S(2)}, u32[]{:S(2)}) %collective-permute-start.99) | collective-permute-done | bytes 483360 | tf_op jit(solution)/shard_map/ppermute | solution.py:578
  521.0 9.5 %collective-permute-done.94 = bf16[1888,128]{1,0:T(8,128)(2,1)S(1)} collective-permute-done((bf16[1888,128]{1,0:T(8,128)(2,1)}, bf16[1888,128]{1,0:T(8,128)(2,1)S(1)}, u32[]{:S(2)}, u32[]{:S(2)}) %collective-permute-start.94) | collective-permute-done | bytes 483360 | tf_op jit(solution)/shard_map/ppermute | solution.py:578
  564.4 8.6 %collective-permute-start.101 = (bf16[944,128]{1,0:T(8,128)(2,1)S(1)}, bf16[944,128]{1,0:T(8,128)(2,1)S(1)}, u32[]{:S(2)}, u32[]{:S(2)}) collective-permute-start(bf16[944,128]{1,0:T(8,128)(2,1)S(1)} %slice.438), channel_id=1, source_target_pairs={{0,1},{1,0},{2,3},{3,2},{4,5},{5,4},{6,7},{7,6},{8,9},{9,8},{10,11... | collective-permute-start | bytes 725000 | tf_op jit(solution)/shard_map/ppermute | solution.py:578
  583.0 9.3 %collective-permute-done.117 = bf16[1472,128]{1,0:T(8,128)(2,1)S(1)} collective-permute-done((bf16[1472,128]{1,0:T(8,128)(2,1)S(1)}, bf16[1472,128]{1,0:T(8,128)(2,1)S(1)}, u32[]{:S(2)}, u32[]{:S(2)}) %collective-permute-start.117) | collective-permute-done | bytes 376864 | tf_op jit(solution)/shard_map/ppermute | solution.py:578
  619.9 15.0 %collective-permute-done.92 = bf16[944,128]{1,0:T(8,128)(2,1)S(1)} collective-permute-done((bf16[944,128]{1,0:T(8,128)(2,1)S(1)}, bf16[944,128]{1,0:T(8,128)(2,1)S(1)}, u32[]{:S(2)}, u32[]{:S(2)}) %collective-permute-start.92) | collective-permute-done | bytes 241696 | tf_op jit(solution)/shard_map/ppermute | solution.py:578
  641.6 33.1 %collective-permute-done.104 = bf16[3776,128]{1,0:T(8,128)(2,1)S(1)} collective-permute-done((bf16[3776,128]{1,0:T(8,128)(2,1)S(1)}, bf16[3776,128]{1,0:T(8,128)(2,1)S(1)}, u32[]{:S(2)}, u32[]{:S(2)}) %collective-permute-start.104) | collective-permute-done | bytes 966688 | tf_op jit(solution)/shard_map/ppermute | solution.py:578
  676.7 8.4 %collective-permute-done.110 = bf16[3776,128]{1,0:T(8,128)(2,1)S(1)} collective-permute-done((bf16[3776,128]{1,0:T(8,128)(2,1)S(1)}, bf16[3776,128]{1,0:T(8,128)(2,1)S(1)}, u32[]{:S(2)}, u32[]{:S(2)}) %collective-permute-start.110) | collective-permute-done | bytes 966688 | tf_op jit(solution)/shard_map/ppermute | solution.py:578
  702.4 8.9 %collective-permute-done.112 = bf16[1888,128]{1,0:T(8,128)(2,1)S(1)} collective-permute-done((bf16[1888,128]{1,0:T(8,128)(2,1)S(1)}, bf16[1888,128]{1,0:T(8,128)(2,1)S(1)}, u32[]{:S(2)}, u32[]{:S(2)}) %collective-permute-start.112) | collective-permute-done | bytes 483360 | tf_op jit(solution)/shard_map/ppermute | solution.py:578
  724.1 9.3 %finish.1 = (f32[1,476288]{1,0:T(1,128)}, f32[1,476288]{1,0:T(1,128)}, f32[1,476288]{1,0:T(1,128)}, f32[1,476288]{1,0:T(1,128)}) custom-call(s32[5]{0:T(128)} %stack.23.place_ref, bf16[944,128]{1,0:T(8,128)(2,1)} %get-tuple-element.194.refs_0_, bf16[944,128]{1,0:T(8,128)(2,1)} %copy-done.63, bf16[944,128]{1,0:T(8,128)(2,1)} %copy-done.64, ...), custom_call_target="tpu_custom_call" | custom-call | tf_op jit(solution)/shard_map/finish/pallas_call | solution.py:825
  (504 shorter events, 336.8 us)
Async XLA Ops:
  71.4 32.0 %collective-permute-start.49 = (bf16[2832,128]{1,0:T(8,128)(2,1)S(1)}, bf16[2832,128]{1,0:T(8,128)(2,1)}, u32[]{:S(2)}, u32[]{:S(2)}) collective-permute-start(bf16[2832,128]{1,0:T(8,128)(2,1)S(1)} %pad_maximum_fusion.2.refs_0_), channel_id=1, source_target_pairs={{0,1},{1,0},{2,3},{3,2},{4,5},{5,4},{6,7},{7,6},{8,9},{9,8},{10,11... | collective-permute-start | bytes 2174984 | tf_op jit(solution)/shard_map/ppermute | solution.py:578
  71.4 43.9 %collective-permute-start.53 = (bf16[2832,128]{1,0:T(8,128)(2,1)S(1)}, bf16[2832,128]{1,0:T(8,128)(2,1)}, u32[]{:S(2)}, u32[]{:S(2)}) collective-permute-start(bf16[2832,128]{1,0:T(8,128)(2,1)S(1)} %pad_maximum_fusion.2.refs_0_), channel_id=1, source_target_pairs={{0,2},{1,3},{2,0},{3,1},{4,6},{5,7},{6,4},{7,5},{8,10},{9,11},{10,... | collective-permute-start | bytes 2174984 | tf_op jit(solution)/shard_map/ppermute | solution.py:578
  85.1 30.7 %collective-permute-start.21 = (bf16[944,128]{1,0:T(8,128)(2,1)}, bf16[944,128]{1,0:T(8,128)(2,1)S(1)}, u32[]{:S(2)}, u32[]{:S(2)}) collective-permute-start(bf16[944,128]{1,0:T(8,128)(2,1)} %collective-permute-done.20.refs_12_), channel_id=1, source_target_pairs={{0,8},{4,12},{8,0},{12,4},{16,24},{20,28},{24,16},{28,20},{1,9},{5... | collective-permute-start | bytes 725000 | tf_op jit(solution)/shard_map/ppermute | solution.py:578
  137.0 33.0 %collective-permute-start.50 = (bf16[2832,128]{1,0:T(8,128)(2,1)}, bf16[2832,128]{1,0:T(8,128)(2,1)}, u32[]{:S(2)}, u32[]{:S(2)}) collective-permute-start(bf16[2832,128]{1,0:T(8,128)(2,1)} %collective-permute-done.49.refs_4_), channel_id=1, source_target_pairs={{0,8},{4,12},{8,0},{12,4},{16,24},{20,28},{24,16},{28,20},{1,9},{5... | collective-permute-start | bytes 2174984 | tf_op jit(solution)/shard_map/ppermute | solution.py:578
  139.1 36.6 %collective-permute-start.51 = (bf16[2832,128]{1,0:T(8,128)(2,1)}, bf16[2832,128]{1,0:T(8,128)(2,1)}, u32[]{:S(2)}, u32[]{:S(2)}) collective-permute-start(bf16[2832,128]{1,0:T(8,128)(2,1)} %collective-permute-done.49.refs_4_), channel_id=1, source_target_pairs={{0,16},{4,20},{8,24},{12,28},{16,0},{20,4},{24,8},{28,12},{1,17},{... | collective-permute-start | bytes 2174984 | tf_op jit(solution)/shard_map/ppermute | solution.py:578
  156.9 28.2 %collective-permute-start.54 = (bf16[2832,128]{1,0:T(8,128)(2,1)}, bf16[2832,128]{1,0:T(8,128)(2,1)}, u32[]{:S(2)}, u32[]{:S(2)}) collective-permute-start(bf16[2832,128]{1,0:T(8,128)(2,1)} %collective-permute-done.53.refs_8_), channel_id=1, source_target_pairs={{0,8},{4,12},{8,0},{12,4},{16,24},{20,28},{24,16},{28,20},{1,9},{5... | collective-permute-start | bytes 2174984 | tf_op jit(solution)/shard_map/ppermute | solution.py:578
  157.6 29.7 %collective-permute-start.55 = (bf16[2832,128]{1,0:T(8,128)(2,1)}, bf16[2832,128]{1,0:T(8,128)(2,1)}, u32[]{:S(2)}, u32[]{:S(2)}) collective-permute-start(bf16[2832,128]{1,0:T(8,128)(2,1)} %collective-permute-done.53.refs_8_), channel_id=1, source_target_pairs={{0,16},{4,20},{8,24},{12,28},{16,0},{20,4},{24,8},{28,12},{1,17},{... | collective-permute-start | bytes 2174984 | tf_op jit(solution)/shard_map/ppermute | solution.py:578
  158.5 39.5 %collective-permute-start.65 = (bf16[2832,128]{1,0:T(8,128)(2,1)}, bf16[2832,128]{1,0:T(8,128)(2,1)}, u32[]{:S(2)}, u32[]{:S(2)}) collective-permute-start(bf16[2832,128]{1,0:T(8,128)(2,1)} %collective-permute-done.49.refs_4_), channel_id=1, source_target_pairs={{0,4},{4,0},{8,12},{12,8},{16,20},{20,16},{24,28},{28,24},{1,5},{5... | collective-permute-start | bytes 2174984 | tf_op jit(solution)/shard_map/ppermute | solution.py:578
  170.0 27.9 %collective-permute-start.57 = (bf16[2832,128]{1,0:T(8,128)(2,1)}, bf16[2832,128]{1,0:T(8,128)(2,1)}, u32[]{:S(2)}, u32[]{:S(2)}) collective-permute-start(bf16[2832,128]{1,0:T(8,128)(2,1)} %collective-permute-done.53.refs_8_), channel_id=1, source_target_pairs={{0,1},{1,0},{2,3},{3,2},{4,5},{5,4},{6,7},{7,6},{8,9},{9,8},{10,11... | collective-permute-start | bytes 2174984 | tf_op jit(solution)/shard_map/ppermute | solution.py:578
  175.7 31.1 %collective-permute-start.40 = (bf16[256,864]{1,0:T(8,128)(2,1)}, bf16[256,864]{1,0:T(8,128)(2,1)S(1)}, u32[]{:S(2)}, u32[]{:S(2)}) collective-permute-start(bf16[256,864]{1,0:T(8,128)(2,1)} %bitcast.133), channel_id=1, source_target_pairs={{0,1},{1,0},{2,3},{3,2},{4,5},{5,4},{6,7},{7,6},{8,9},{9,8},{10,11... | collective-permute-start | bytes 1327112 | tf_op jit(solution)/shard_map/ppermute | solution.py:578
  185.1 34.2 %collective-permute-start.41 = (bf16[256,864]{1,0:T(8,128)(2,1)}, bf16[256,864]{1,0:T(8,128)(2,1)S(1)}, u32[]{:S(2)}, u32[]{:S(2)}) collective-permute-start(bf16[256,864]{1,0:T(8,128)(2,1)} %bitcast.134), channel_id=1, source_target_pairs={{0,2},{1,3},{2,0},{3,1},{4,6},{5,7},{6,4},{7,5},{8,10},{9,11},{10,... | collective-permute-start | bytes 1327112 | tf_op jit(solution)/shard_map/ppermute | solution.py:578
  187.2 32.0 %collective-permute-start.42 = (bf16[256,864]{1,0:T(8,128)(2,1)}, bf16[256,864]{1,0:T(8,128)(2,1)S(1)}, u32[]{:S(2)}, u32[]{:S(2)}) collective-permute-start(bf16[256,864]{1,0:T(8,128)(2,1)} %bitcast.135), channel_id=1, source_target_pairs={{0,3},{1,2},{2,1},{3,0},{4,7},{5,6},{6,5},{7,4},{8,11},{9,10},{10,... | collective-permute-start | bytes 1327112 | tf_op jit(solution)/shard_map/ppermute | solution.py:578
  198.0 38.8 %collective-permute-start.69 = (bf16[2832,128]{1,0:T(8,128)(2,1)}, bf16[2832,128]{1,0:T(8,128)(2,1)}, u32[]{:S(2)}, u32[]{:S(2)}) collective-permute-start(bf16[2832,128]{1,0:T(8,128)(2,1)} %collective-permute-done.53.refs_8_), channel_id=1, source_target_pairs={{0,4},{4,0},{8,12},{12,8},{16,20},{20,16},{24,28},{28,24},{1,5},{5... | collective-permute-start | bytes 2174984 | tf_op jit(solution)/shard_map/ppermute | solution.py:578
  198.0 47.8 %collective-permute-start.48 = (bf16[2832,128]{1,0:T(8,128)(2,1)S(1)}, bf16[2832,128]{1,0:T(8,128)(2,1)}, u32[]{:S(2)}, u32[]{:S(2)}) collective-permute-start(bf16[2832,128]{1,0:T(8,128)(2,1)S(1)} %copy-done.24), channel_id=1, source_target_pairs={{0,16},{4,20},{8,24},{12,28},{16,0},{20,4},{24,8},{28,12},{1,17},{... | collective-permute-start | bytes 2174984 | tf_op jit(solution)/shard_map/ppermute | solution.py:578
  206.7 39.5 %collective-permute-start.62 = (bf16[2832,128]{1,0:T(8,128)(2,1)S(1)}, bf16[2832,128]{1,0:T(8,128)(2,1)}, u32[]{:S(2)}, u32[]{:S(2)}) collective-permute-start(bf16[2832,128]{1,0:T(8,128)(2,1)S(1)} %copy-done.24), channel_id=1, source_target_pairs={{0,4},{4,0},{8,12},{12,8},{16,20},{20,16},{24,28},{28,24},{1,5},{5... | collective-permute-start | bytes 2174984 | tf_op jit(solution)/shard_map/ppermute | solution.py:578
  219.2 29.0 %collective-permute-start.63 = (bf16[2832,128]{1,0:T(8,128)(2,1)}, bf16[2832,128]{1,0:T(8,128)(2,1)}, u32[]{:S(2)}, u32[]{:S(2)}) collective-permute-start(bf16[2832,128]{1,0:T(8,128)(2,1)} %copy-done.25), channel_id=1, source_target_pairs={{0,4},{4,0},{8,12},{12,8},{16,20},{20,16},{24,28},{28,24},{1,5},{5... | collective-permute-start | bytes 2174984 | tf_op jit(solution)/shard_map/ppermute | solution.py:578
  219.2 44.0 %collective-permute-start.52 = (bf16[2832,128]{1,0:T(8,128)(2,1)}, bf16[2832,128]{1,0:T(8,128)(2,1)}, u32[]{:S(2)}, u32[]{:S(2)}) collective-permute-start(bf16[2832,128]{1,0:T(8,128)(2,1)} %collective-permute-done.51.refs_6_), channel_id=1, source_target_pairs={{0,8},{4,12},{8,0},{12,4},{16,24},{20,28},{24,16},{28,20},{1,9},{5... | collective-permute-start | bytes 2174984 | tf_op jit(solution)/shard_map/ppermute | solution.py:578
  435.9 34.3 %collective-permute-start.81 = (bf16[256,864]{1,0:T(8,128)(2,1)}, bf16[256,864]{1,0:T(8,128)(2,1)}, u32[]{:S(2)}, u32[]{:S(2)}) collective-permute-start(bf16[256,864]{1,0:T(8,128)(2,1)} %get-tuple-element.97), channel_id=1, source_target_pairs={{0,2},{1,3},{2,0},{3,1},{4,6},{5,7},{6,4},{7,5},{8,10},{9,11},{10,... | collective-permute-start | bytes 1327112 | tf_op jit(solution)/shard_map/ppermute | solution.py:578
  436.3 33.8 %collective-permute-start.80 = (bf16[256,864]{1,0:T(8,128)(2,1)}, bf16[256,864]{1,0:T(8,128)(2,1)}, u32[]{:S(2)}, u32[]{:S(2)}) collective-permute-start(bf16[256,864]{1,0:T(8,128)(2,1)} %get-tuple-element.96), channel_id=1, source_target_pairs={{0,3},{1,2},{2,1},{3,0},{4,7},{5,6},{6,5},{7,4},{8,11},{9,10},{10,... | collective-permute-start | bytes 1327112 | tf_op jit(solution)/shard_map/ppermute | solution.py:578
  454.5 43.6 %collective-permute-start.93 = (bf16[15104,128]{1,0:T(8,128)(2,1)}, bf16[15104,128]{1,0:T(8,128)(2,1)}, u32[]{:S(2)}, u32[]{:S(2)}) collective-permute-start(bf16[15104,128]{1,0:T(8,128)(2,1)} %get-tuple-element.117), channel_id=1, source_target_pairs={{0,4},{4,0},{8,12},{12,8},{16,20},{20,16},{24,28},{28,24},{1,5},{5... | collective-permute-start | bytes 11599880 | tf_op jit(solution)/shard_map/ppermute | solution.py:578
  498.0 35.4 %collective-permute-start.83 = (bf16[15104,128]{1,0:T(8,128)(2,1)}, bf16[15104,128]{1,0:T(8,128)(2,1)}, u32[]{:S(2)}, u32[]{:S(2)}) collective-permute-start(bf16[15104,128]{1,0:T(8,128)(2,1)} %get-tuple-element.105), channel_id=1, source_target_pairs={{0,4},{4,0},{8,12},{12,8},{16,20},{20,16},{24,28},{28,24},{1,5},{5... | collective-permute-start | bytes 11599880 | tf_op jit(solution)/shard_map/ppermute | solution.py:578
  505.2 105.9 %collective-permute-start.103 = (bf16[30208,128]{1,0:T(8,128)(2,1)}, bf16[30208,128]{1,0:T(8,128)(2,1)}, u32[]{:S(2)}, u32[]{:S(2)}) collective-permute-start(bf16[30208,128]{1,0:T(8,128)(2,1)} %get-tuple-element.127), channel_id=1, source_target_pairs={{0,4},{4,0},{8,12},{12,8},{16,20},{20,16},{24,28},{28,24},{1,5},{5... | collective-permute-start | bytes 23199752 | tf_op jit(solution)/shard_map/ppermute | solution.py:578
  506.3 51.7 %collective-permute-start.98 = (bf16[1888,128]{1,0:T(8,128)(2,1)}, bf16[1888,128]{1,0:T(8,128)(2,1)}, u32[]{:S(2)}, u32[]{:S(2)}) collective-permute-start(bf16[1888,128]{1,0:T(8,128)(2,1)} %get-tuple-element.123), channel_id=1, source_target_pairs={{0,8},{4,12},{8,0},{12,4},{16,24},{20,28},{24,16},{28,20},{1,9},{5... | collective-permute-start | bytes 1449992 | tf_op jit(solution)/shard_map/ppermute | solution.py:578
  506.9 54.5 %collective-permute-start.96 = (bf16[1888,128]{1,0:T(8,128)(2,1)}, bf16[1888,128]{1,0:T(8,128)(2,1)}, u32[]{:S(2)}, u32[]{:S(2)}) collective-permute-start(bf16[1888,128]{1,0:T(8,128)(2,1)} %get-tuple-element.121), channel_id=1, source_target_pairs={{0,16},{4,20},{8,24},{12,28},{16,0},{20,4},{24,8},{28,12},{1,17},{... | collective-permute-start | bytes 1449992 | tf_op jit(solution)/shard_map/ppermute | solution.py:578
  530.5 28.2 %collective-permute-start.100 = (bf16[1888,128]{1,0:T(8,128)(2,1)}, bf16[1888,128]{1,0:T(8,128)(2,1)}, u32[]{:S(2)}, u32[]{:S(2)}) collective-permute-start(bf16[1888,128]{1,0:T(8,128)(2,1)} %add_convert_fusion.17), channel_id=1, source_target_pairs={{0,16},{4,20},{8,24},{12,28},{16,0},{20,4},{24,8},{28,12},{1,17},{... | collective-permute-start | bytes 1449992 | tf_op jit(solution)/shard_map/ppermute | solution.py:578
  533.4 29.3 %collective-permute-start.95 = (bf16[1888,128]{1,0:T(8,128)(2,1)}, bf16[1888,128]{1,0:T(8,128)(2,1)}, u32[]{:S(2)}, u32[]{:S(2)}) collective-permute-start(bf16[1888,128]{1,0:T(8,128)(2,1)} %add_convert_fusion.19), channel_id=1, source_target_pairs={{0,8},{4,12},{8,0},{12,4},{16,24},{20,28},{24,16},{28,20},{1,9},{5... | collective-permute-start | bytes 1449992 | tf_op jit(solution)/shard_map/ppermute | solution.py:578
  558.7 44.1 %collective-permute-start.88 = (bf16[1888,128]{1,0:T(8,128)(2,1)S(1)}, bf16[1888,128]{1,0:T(8,128)(2,1)S(1)}, u32[]{:S(2)}, u32[]{:S(2)}) collective-permute-start(bf16[1888,128]{1,0:T(8,128)(2,1)S(1)} %copy-done.34), channel_id=1, source_target_pairs={{0,8},{4,12},{8,0},{12,4},{16,24},{20,28},{24,16},{28,20},{1,9},{5... | collective-permute-start | bytes 1449992 | tf_op jit(solution)/shard_map/ppermute | solution.py:578
  619.3 78.1 %collective-permute-start.119 = (bf16[1472,128]{1,0:T(8,128)(2,1)S(1)}, bf16[1472,128]{1,0:T(8,128)(2,1)S(1)}, u32[]{:S(2)}, u32[]{:S(2)}) collective-permute-start(bf16[1472,128]{1,0:T(8,128)(2,1)S(1)} %add_convert_fusion.42), channel_id=1, source_target_pairs={{0,2},{1,3},{2,0},{3,1},{4,6},{5,7},{6,4},{7,5},{8,10},{9,11},{10,... | collective-permute-start | bytes 1130504 | tf_op jit(solution)/shard_map/ppermute | solution.py:578
  635.0 41.7 %collective-permute-start.108 = (bf16[3776,128]{1,0:T(8,128)(2,1)S(1)}, bf16[3776,128]{1,0:T(8,128)(2,1)S(1)}, u32[]{:S(2)}, u32[]{:S(2)}) collective-permute-start(bf16[3776,128]{1,0:T(8,128)(2,1)S(1)} %get-tuple-element.133), channel_id=1, source_target_pairs={{0,8},{4,12},{8,0},{12,4},{16,24},{20,28},{24,16},{28,20},{1,9},{5... | collective-permute-start | bytes 2899976 | tf_op jit(solution)/shard_map/ppermute | solution.py:578
  635.9 49.6 %collective-permute-start.106 = (bf16[3776,128]{1,0:T(8,128)(2,1)S(1)}, bf16[3776,128]{1,0:T(8,128)(2,1)S(1)}, u32[]{:S(2)}, u32[]{:S(2)}) collective-permute-start(bf16[3776,128]{1,0:T(8,128)(2,1)S(1)} %get-tuple-element.131), channel_id=1, source_target_pairs={{0,16},{4,20},{8,24},{12,28},{16,0},{20,4},{24,8},{28,12},{1,17},{... | collective-permute-start | bytes 2899976 | tf_op jit(solution)/shard_map/ppermute | solution.py:578
  637.1 37.6 %collective-permute-start.104 = (bf16[3776,128]{1,0:T(8,128)(2,1)S(1)}, bf16[3776,128]{1,0:T(8,128)(2,1)S(1)}, u32[]{:S(2)}, u32[]{:S(2)}) collective-permute-start(bf16[3776,128]{1,0:T(8,128)(2,1)S(1)} %get-tuple-element.130), channel_id=1, source_target_pairs={{0,16},{4,20},{8,24},{12,28},{16,0},{20,4},{24,8},{28,12},{1,17},{... | collective-permute-start | bytes 2899976 | tf_op jit(solution)/shard_map/ppermute | solution.py:578
  640.3 44.7 %collective-permute-start.110 = (bf16[3776,128]{1,0:T(8,128)(2,1)S(1)}, bf16[3776,128]{1,0:T(8,128)(2,1)S(1)}, u32[]{:S(2)}, u32[]{:S(2)}) collective-permute-start(bf16[3776,128]{1,0:T(8,128)(2,1)S(1)} %add_convert_fusion.1), channel_id=1, source_target_pairs={{0,16},{4,20},{8,24},{12,28},{16,0},{20,4},{24,8},{28,12},{1,17},{... | collective-permute-start | bytes 2899976 | tf_op jit(solution)/shard_map/ppermute | solution.py:578
  (176 other events, 2702.8 us)
